TPU v7x, 32 devices: a whole 2x2x4 slice. The times are simulated.
32 devices in a mesh: groups: 2 (over y), ctx: 16 (over z, x, core).
Axes of the slice: x: 2, y: 2, z: 4, core: 2. Of those that a mesh axis runs over, the one named last changes fastest.
Arguments:
- tokens_in: bfloat16 [4096, 1024], P(('groups', 'ctx')), parts along dimension 0, may hold values from -6 to 6
- grad_out: bfloat16 [4096, 1024], P(('groups', 'ctx')), parts along dimension 0, may hold values from -6 to 6
- decay_rate: float32 [1024], replicated, as said below
- w_in: float32 [64], replicated, may hold values from -16 to 16
- b_in: float32 [64], replicated, may hold values from -6 to 6
- w_mid: float32 [64, 64], replicated, may hold values from -0.75 to 0.75
- w_out: float32 [64, 1024], replicated, may hold values from -0.75 to 0.75
Outputs:
- grad_tokens: bfloat16 [4096, 1024], P(('groups', 'ctx')), parts along dimension 0
- grad_w_in: float32 [128], P('groups'), parts along dimension 0
- grad_b_in: float32 [128], P('groups'), parts along dimension 0
- grad_w_mid: float32 [128, 64], P('groups'), parts along dimension 0
- grad_w_out: float32 [128, 1024], P('groups'), parts along dimension 0
There are 2 independent parts, one for each index of `groups`. A program takes and returns all parts, laid end to end along the dimension named above; an argument that names none is the same for every part. Nothing has to cross between parts.
Inputs may be any that keep to these rules, and one draw needn't show every extreme that they name: `decay_rate`: every channel's rate is positive.
All inputs are finite; a program needn't handle non-finite values.
Results may differ from a plain program's by a relative error of at most 0.0051.
Values may be sent and summed in bfloat16 or wider, within the bound.
No kernel may reach another device: no remote copies, remote signals or barrier semaphores. Data moves between devices by JAX's collectives and lax.ppermute only.
A program may use at most 64 MiB of HBM per device.

v0:
```python
import math

import jax
import jax.numpy as jnp
from jax import lax
from jax.sharding import PartitionSpec as P

HIGHEST = lax.Precision.HIGHEST
TWO_PI = 2.0 * math.pi


def phase_angle(product, period):
    return TWO_PI / period * (product % period).astype(jnp.float32)


def frequency_rows(devices):
    row_index = jnp.arange(2 * devices, dtype=jnp.int32)
    row_block = row_index // 2
    second = row_index % 2
    paired = jnp.where(row_block == 0, devices, 2 * devices - row_block)
    return jnp.where(second == 0, row_block, paired)


def source_rows(devices):
    row_index = jnp.arange(2 * devices, dtype=jnp.int32)
    return row_index // 2 + row_index % 2 * devices


def envelope(lag_values, decay_rate, length):
    double = 2.0 * decay_rate
    geometric = 1.0 + 2.0 * jnp.exp(-double) * jnp.expm1(-double * (length - 1)) / jnp.expm1(
        -double
    )
    distance = jnp.abs(lag_values).astype(jnp.float32)[..., None]
    live_mask = (lag_values != -length).astype(jnp.float32)[..., None]
    return live_mask * lax.rsqrt(geometric) * jnp.exp(-distance * decay_rate)


def position_mlp(scaled, w_first, w_bias, w_middle, w_last):
    hidden_one = jax.nn.silu(scaled[..., None] * w_first + w_bias)
    hidden_two = jax.nn.silu(jnp.dot(hidden_one, w_middle, precision=HIGHEST))
    return jnp.dot(hidden_two, w_last, precision=HIGHEST)


def rotate(real_a, imag_a, real_b, imag_b):
    return (real_a * real_b - imag_a * imag_b, real_a * imag_b + imag_a * real_b)


def first_section(signal, columns, freq_order, local_slab, padded):
    freq_count = freq_order.shape[0]
    angles = phase_angle(freq_order[:, None] * columns[None, :], freq_count)
    real_part = jnp.einsum("fp,prc->frc", jnp.cos(angles), signal, precision=HIGHEST)
    imag_part = jnp.einsum("fp,prc->frc", -jnp.sin(angles), signal, precision=HIGHEST)
    twiddle = phase_angle(freq_order[:, None] * local_slab[None, :], padded)[:, :, None]
    return rotate(real_part, imag_part, jnp.cos(twiddle), -jnp.sin(twiddle))


def along_rows(stacked, direction):
    row_count = stacked.shape[1]
    half_width = stacked.shape[2] // 2
    positions = jnp.arange(row_count, dtype=jnp.int32)
    angles = phase_angle(positions[:, None] * positions[None, :], row_count)
    with_cos = jnp.einsum("gm,imc->igc", jnp.cos(angles), stacked, precision=HIGHEST)
    with_sin = jnp.einsum("gm,imc->igc", direction * jnp.sin(angles), stacked, precision=HIGHEST)
    real_part = with_cos[..., :half_width] - with_sin[..., half_width:]
    imag_part = with_cos[..., half_width:] + with_sin[..., :half_width]
    return (real_part, imag_part)


def last_section(stacked, out_rows, freq_order, padded):
    freq_count = freq_order.shape[0]
    half_width = stacked.shape[2] // 2
    angles = phase_angle(out_rows[:, None] * freq_order[None, :], freq_count)
    cos_table = jnp.cos(angles) / padded
    sin_table = jnp.sin(angles) / padded
    real_in = stacked[..., :half_width]
    imag_in = stacked[..., half_width:]
    leading, trailing, factor = (real_in, imag_in, -1.0)
    return jnp.einsum("pf,frc->prc", cos_table, leading, precision=HIGHEST) + factor * jnp.einsum(
        "pf,frc->prc", sin_table, trailing, precision=HIGHEST
    )


def on_device(tokens_in, grad_out, decay_rate, w_in, b_in, w_mid, w_out):
    devices = lax.axis_size("ctx")
    own_index = lax.axis_index("ctx")
    tok_rows = tokens_in.shape[0]
    slab_rows = tok_rows // devices
    length = tok_rows * devices
    padded = 2 * length
    freq_order = frequency_rows(devices)
    lag_rows = source_rows(devices)
    token_cols = jnp.arange(devices, dtype=jnp.int32)
    local_slab = own_index * slab_rows + jnp.arange(slab_rows, dtype=jnp.int32)
    pair_index = jnp.arange(2, dtype=jnp.int32)
    local_freq = jnp.where(
        pair_index == 0, own_index, jnp.where(own_index == 0, devices, 2 * devices - own_index)
    )
    circular = (own_index + pair_index * devices)[:, None] * tok_rows + jnp.arange(
        tok_rows, dtype=jnp.int32
    )[None, :]
    lag_values = jnp.where(circular < length, circular, circular - padded)
    scaled = lag_values.astype(jnp.float32) / length
    weights_env = envelope(lag_values, decay_rate, length)

    def position_net(w_first, w_bias, w_middle, w_last):
        return position_mlp(scaled, w_first, w_bias, w_middle, w_last)

    position, pull_back = jax.vjp(position_net, w_in, b_in, w_mid, w_out)
    kernel = (position * weights_env).astype(jnp.bfloat16)
    tokens_mid, grads_mid, kernel_mid = (
        lax.all_to_all(tokens_in[None], "ctx", split_axis=1, concat_axis=0, tiled=True),
        lax.all_to_all(grad_out[None], "ctx", split_axis=1, concat_axis=0, tiled=True),
        lax.all_to_all(kernel, "ctx", split_axis=1, concat_axis=0, tiled=True),
    )
    token_real, token_imag = first_section(
        tokens_mid.astype(jnp.float32), token_cols, freq_order, local_slab, padded
    )
    cotan_real, cotan_imag = first_section(
        grads_mid.astype(jnp.float32), token_cols, freq_order, local_slab, padded
    )
    kern_real, kern_imag = first_section(
        kernel_mid.astype(jnp.float32), lag_rows, freq_order, local_slab, padded
    )
    kernel_stack = jnp.concatenate([kern_real, kern_imag], axis=2)
    token_stack = jnp.concatenate([token_real, token_imag], axis=2)
    cotan_stack = jnp.concatenate([cotan_real, cotan_imag], axis=2)
    token_spec, cotan_spec, kernel_spec = (
        lax.all_to_all(token_stack, "ctx", split_axis=0, concat_axis=1, tiled=True),
        lax.all_to_all(cotan_stack, "ctx", split_axis=0, concat_axis=1, tiled=True),
        lax.all_to_all(kernel_stack, "ctx", split_axis=0, concat_axis=1, tiled=True),
    )
    spec_token_real, spec_token_imag = along_rows(token_spec, -1.0)
    spec_cotan_real, spec_cotan_imag = along_rows(cotan_spec, -1.0)
    spec_kern_real, spec_kern_imag = along_rows(kernel_spec, -1.0)
    input_real = spec_kern_real * spec_cotan_real + spec_kern_imag * spec_cotan_imag
    input_imag = spec_kern_real * spec_cotan_imag - spec_kern_imag * spec_cotan_real
    lagged_real = spec_cotan_real * spec_token_real + spec_cotan_imag * spec_token_imag
    lagged_imag = spec_cotan_imag * spec_token_real - spec_cotan_real * spec_token_imag
    positions = jnp.arange(tok_rows, dtype=jnp.int32)
    back_angle = phase_angle(local_freq[:, None] * positions[None, :], padded)[:, :, None]
    back_cos = jnp.cos(back_angle)
    back_sin = jnp.sin(back_angle)

    def inverse_rows(real_part, imag_part):
        stacked = jnp.concatenate([real_part, imag_part], axis=2)
        out_real, out_imag = along_rows(stacked, 1.0)
        turned_real, turned_imag = rotate(out_real, out_imag, back_cos, back_sin)
        return jnp.concatenate([turned_real, turned_imag], axis=2)

    spread_input, spread_lagged = (
        lax.all_to_all(
            inverse_rows(input_real, input_imag), "ctx", split_axis=1, concat_axis=0, tiled=True
        ),
        lax.all_to_all(
            inverse_rows(lagged_real, lagged_imag), "ctx", split_axis=1, concat_axis=0, tiled=True
        ),
    )
    input_rows = last_section(spread_input, token_cols, freq_order, padded)
    lagged_rows = last_section(spread_lagged, lag_rows, freq_order, padded)
    input_back, lag_back = (
        lax.all_to_all(input_rows, "ctx", split_axis=0, concat_axis=1, tiled=True),
        lax.all_to_all(lagged_rows, "ctx", split_axis=0, concat_axis=1, tiled=True),
    )
    input_grad = input_back[0]
    gradients = pull_back(lag_back * weights_env)
    summed = lax.psum((gradients[0], gradients[1], gradients[2], gradients[3]), "ctx")
    loss_scale = 1.0 / math.sqrt(length)
    return (
        input_grad.astype(jnp.bfloat16),
        summed[0] * loss_scale,
        summed[1] * loss_scale,
        summed[2] * loss_scale,
        summed[3] * loss_scale,
    )


def solution(mesh):
    in_specs = (P(("groups", "ctx"), None), P(("groups", "ctx"), None), P(), P(), P(), P(), P())
    out_specs = (
        P(("groups", "ctx"), None),
        P("groups"),
        P("groups"),
        P("groups", None),
        P("groups", None),
    )
    return jax.shard_map(
        on_device, mesh=mesh, in_specs=in_specs, out_specs=out_specs, check_vma=False
    )
```

profile of v0, /device:TPU:0, one launch (start us, length us, event | category | flops | bytes accessed | tf_op | source)
XLA Modules:
  0.0 568.0 jit_solution(4367355569631194448)
XLA Ops:
  12.2 7.4 %all-to-all-start.2 = ((bf16[16,2,4096]{2,1,0:T(2,128)(2,1)}), bf16[16,2,4096]{2,1,0:T(2,128)(2,1)S(1)}, u32[]{:S(2)}, u32[]{:S(2)}) async-start(bf16[16,2,4096]{2,1,0:T(2,128)(2,1)} %reshape.315), calls=%async_computation.2 | async-start | bytes 524288 | tf_op jit(solution)/shard_map/all_to_all | solution.py:113
  23.5 6.1 %all-to-all-done.2 = bf16[16,2,4096]{2,1,0:T(2,128)(2,1)S(1)} async-done(((bf16[16,2,4096]{2,1,0:T(2,128)(2,1)}), bf16[16,2,4096]{2,1,0:T(2,128)(2,1)S(1)}, u32[]{:S(2)}, u32[]{:S(2)}) %all-to-all-start.2) | async-done | bytes 262176 | tf_op jit(solution)/shard_map/all_to_all | solution.py:113
  36.2 6.9 %all-to-all-done.6 = bf16[16,2,4096]{2,1,0:T(2,128)(2,1)S(1)} async-done(((bf16[16,2,4096]{2,1,0:T(2,128)(2,1)}), bf16[16,2,4096]{2,1,0:T(2,128)(2,1)S(1)}, u32[]{:S(2)}, u32[]{:S(2)}) %all-to-all-start.6) | async-done | bytes 262176 | tf_op jit(solution)/shard_map/all_to_all | solution.py:112
  52.0 9.3 %all-to-all-done = bf16[2,128,1024]{2,0,1:T(2,128)(2,1)S(1)} async-done(((bf16[2,128,1024]{2,0,1:T(2,128)(2,1)}), bf16[2,128,1024]{2,0,1:T(2,128)(2,1)S(1)}, u32[]{:S(2)}, u32[]{:S(2)}) %all-to-all-start) | async-done | bytes 524320 | tf_op jit(solution)/shard_map/all_to_all | solution.py:114
  80.5 37.2 %all-to-all-done.7 = f32[32,8,2048]{2,1,0:T(8,128)S(1)} async-done(((f32[32,8,2048]{2,1,0:T(8,128)}), f32[32,8,2048]{2,1,0:T(8,128)S(1)}, u32[]{:S(2)}, u32[]{:S(2)}) %all-to-all-start.7) | async-done | bytes 2097184 | tf_op jit(solution)/shard_map/all_to_all | solution.py:129
  117.7 11.3 %all-to-all-start.3 = ((f32[32,8,2048]{2,1,0:T(8,128)}), f32[32,8,2048]{2,1,0:T(8,128)}, u32[]{:S(2)}, u32[]{:S(2)}) async-start(f32[32,8,2048]{2,1,0:T(8,128)} %copy.76), calls=%async_computation.3 | async-start | bytes 4194304 | tf_op jit(solution)/shard_map/all_to_all | solution.py:130
  133.0 37.2 %all-to-all-done.3 = f32[32,8,2048]{2,1,0:T(8,128)} async-done(((f32[32,8,2048]{2,1,0:T(8,128)}), f32[32,8,2048]{2,1,0:T(8,128)}, u32[]{:S(2)}, u32[]{:S(2)}) %all-to-all-start.3) | async-done | bytes 2097184 | tf_op jit(solution)/shard_map/all_to_all | solution.py:130
  170.1 11.5 %all-to-all-start.1 = ((f32[32,8,2048]{2,1,0:T(8,128)}), f32[32,8,2048]{2,1,0:T(8,128)}, u32[]{:S(2)}, u32[]{:S(2)}) async-start(f32[32,8,2048]{2,1,0:T(8,128)} %copy.69), calls=%async_computation.1 | async-start | bytes 4194304 | tf_op jit(solution)/shard_map/all_to_all | solution.py:131
  181.7 4.9 convolution_bitcast_fusion.2
  186.6 4.9 convolution_bitcast_fusion.3
  191.5 5.1 convolution_bitcast_fusion.6
  196.6 6.9 %convolution_bitcast_fusion.7 = f32[2,128,2048]{1,2,0:T(8,128)} fusion(f32[2,16,8,2048]{3,2,0,1:T(8,128)} %bitcast.18), kind=kOutput, calls=%fused_computation.7 | convolution fusion | flops 805535744 | bytes 4194304 | tf_op jit(solution)/shard_map/gm,imc->igc/dot_general | solution.py:63
  203.6 19.0 %all-to-all-done.1 = f32[32,8,2048]{2,1,0:T(8,128)} async-done(((f32[32,8,2048]{2,1,0:T(8,128)}), f32[32,8,2048]{2,1,0:T(8,128)}, u32[]{:S(2)}, u32[]{:S(2)}) %all-to-all-start.1) | async-done | bytes 2097184 | tf_op jit(solution)/shard_map/all_to_all | solution.py:131
  222.5 5.4 convolution_bitcast_fusion.8
  228.0 5.4 convolution_bitcast_fusion.9
  247.3 11.2 %all-to-all-start.4 = ((f32[2,128,2048]{2,0,1:T(2,128)}), f32[2,128,2048]{2,0,1:T(2,128)S(1)}, u32[]{:S(2)}, u32[]{:S(2)}) async-start(f32[2,128,2048]{2,0,1:T(2,128)} %copy.80), calls=%async_computation.4 | async-start | bytes 4194304 | tf_op jit(solution)/shard_map/all_to_all | solution.py:152
  265.5 34.1 %all-to-all-done.4 = f32[2,128,2048]{2,0,1:T(2,128)S(1)} async-done(((f32[2,128,2048]{2,0,1:T(2,128)}), f32[2,128,2048]{2,0,1:T(2,128)S(1)}, u32[]{:S(2)}, u32[]{:S(2)}) %all-to-all-start.4) | async-done | bytes 2097184 | tf_op jit(solution)/shard_map/all_to_all | solution.py:152
  300.9 11.2 %all-to-all-start.8 = ((f32[2,128,2048]{2,0,1:T(2,128)}), f32[2,128,2048]{2,0,1:T(2,128)S(1)}, u32[]{:S(2)}, u32[]{:S(2)}) async-start(f32[2,128,2048]{2,0,1:T(2,128)} %copy.91), calls=%async_computation.8 | async-start | bytes 4194304 | tf_op jit(solution)/shard_map/all_to_all | solution.py:155
  326.2 27.1 %all-to-all-done.8 = f32[2,128,2048]{2,0,1:T(2,128)S(1)} async-done(((f32[2,128,2048]{2,0,1:T(2,128)}), f32[2,128,2048]{2,0,1:T(2,128)S(1)}, u32[]{:S(2)}, u32[]{:S(2)}) %all-to-all-start.8) | async-done | bytes 2097184 | tf_op jit(solution)/shard_map/all_to_all | solution.py:155
  353.3 11.4 %all-to-all-start.5 = ((bf16[16,8,1024]{2,1,0:T(8,128)(2,1)}), bf16[16,8,1024]{2,1,0:T(8,128)(2,1)S(1)}, u32[]{:S(2)}, u32[]{:S(2)}) async-start(bf16[16,8,1024]{2,1,0:T(8,128)(2,1)} %copy.83), calls=%async_computation.5 | async-start | bytes 524288 | tf_op jit(solution)/shard_map/all_to_all | solution.py:162
  375.5 6.1 %all-to-all-start.9 = ((f32[32,8,1024]{2,1,0:T(8,128)}), f32[32,8,1024]{2,1,0:T(8,128)S(1)}, u32[]{:S(2)}, u32[]{:S(2)}) async-start(f32[32,8,1024]{2,1,0:T(8,128)} %copy.94), calls=%async_computation.9 | async-start | bytes 2097152 | tf_op jit(solution)/shard_map/all_to_all | solution.py:163
  381.7 22.9 %all-to-all-done.9 = f32[32,8,1024]{2,1,0:T(8,128)S(1)} async-done(((f32[32,8,1024]{2,1,0:T(8,128)}), f32[32,8,1024]{2,1,0:T(8,128)S(1)}, u32[]{:S(2)}, u32[]{:S(2)}) %all-to-all-start.9) | async-done | bytes 1048608 | tf_op jit(solution)/shard_map/all_to_all | solution.py:163
  408.2 62.9 %all-reduce = (f32[64]{0:T(128)S(1)}, f32[64]{0:T(128)S(1)}, f32[64,64]{1,0:T(8,128)S(1)}) all-reduce(f32[64]{0:T(128)S(1)} %get-tuple-element.6, f32[64]{0:T(128)S(1)} %get-tuple-element.5, f32[64,64]{1,0:T(8,128)S(1)} %convolution_bitcast_fusion.11), channel_id=1, replica_groups=mesh['groups'=2,'ctx'=16] {'ctx'}, use_global_device_ids=true, to_apply=%region_1.2 | all-reduce | flops 4224 | bytes 33792 | tf_op jit(solution)/shard_map/psum | solution.py:167
  472.8 85.7 %all-reduce.3.cloned.1.call-done = f32[64,1024]{1,0:T(8,128)} async-done(((f32[64,1024]{1,0:T(8,128)}), f32[64,1024]{1,0:T(8,128)}) %all-reduce.3.cloned.1.call-update) | async-done | bytes 262160 | tf_op jit(solution)/shard_map/psum | solution.py:167
  (100 shorter events, 102.2 us)
Async XLA Ops:
  7.2 26.0 %copy-start = (f32[64,1024]{1,0:T(8,128)S(1)}, f32[64,1024]{1,0:T(8,128)}, u32[]{:S(2)}) copy-start(f32[64,1024]{1,0:T(8,128)} %param.13) | copy-start | bytes 786436
  7.2 12.6 %copy-start.8 = (bf16[128,1024]{1,0:T(8,128)(2,1)S(1)}, bf16[128,1024]{1,0:T(8,128)(2,1)}, u32[]{:S(2)}) copy-start(bf16[128,1024]{1,0:T(8,128)(2,1)} %param.7) | copy-start | bytes 786436
  8.6 14.6 %copy-start.9 = (f32[1024]{0:T(1024)S(1)}, f32[1024]{0:T(1024)}, u32[]{:S(2)}) copy-start(f32[1024]{0:T(1024)} %param.9) | copy-start | bytes 12292
  8.6 14.6 %copy-start.10 = (f32[64,64]{1,0:T(8,128)S(1)}, f32[64,64]{1,0:T(8,128)}, u32[]{:S(2)}) copy-start(f32[64,64]{1,0:T(8,128)} %param.12) | copy-start | bytes 49156
  8.6 14.6 %copy-start.11 = (f32[64]{0:T(128)S(1)}, f32[64]{0:T(128)}, u32[]{:S(2)}) copy-start(f32[64]{0:T(128)} %param.11) | copy-start | bytes 772
  8.6 14.6 %copy-start.12 = (f32[64]{0:T(128)S(1)}, f32[64]{0:T(128)}, u32[]{:S(2)}) copy-start(f32[64]{0:T(128)} %param.10) | copy-start | bytes 772
  12.2 17.4 %all-to-all-start.2 = ((bf16[16,2,4096]{2,1,0:T(2,128)(2,1)}), bf16[16,2,4096]{2,1,0:T(2,128)(2,1)S(1)}, u32[]{:S(2)}, u32[]{:S(2)}) async-start(bf16[16,2,4096]{2,1,0:T(2,128)(2,1)} %reshape.315), calls=%async_computation.2 | async-start | bytes 524288 | tf_op jit(solution)/shard_map/all_to_all | solution.py:113
  29.6 13.5 %all-to-all-start.6 = ((bf16[16,2,4096]{2,1,0:T(2,128)(2,1)}), bf16[16,2,4096]{2,1,0:T(2,128)(2,1)S(1)}, u32[]{:S(2)}, u32[]{:S(2)}) async-start(bf16[16,2,4096]{2,1,0:T(2,128)(2,1)} %reshape.317), calls=%async_computation.6 | async-start | bytes 524288 | tf_op jit(solution)/shard_map/all_to_all | solution.py:112
  43.2 18.2 %all-to-all-start = ((bf16[2,128,1024]{2,0,1:T(2,128)(2,1)}), bf16[2,128,1024]{2,0,1:T(2,128)(2,1)S(1)}, u32[]{:S(2)}, u32[]{:S(2)}) async-start(bf16[2,128,1024]{2,0,1:T(2,128)(2,1)} %copy.67), calls=%async_computation | async-start | bytes 1048576 | tf_op jit(solution)/shard_map/all_to_all | solution.py:114
  63.8 1.2 copy-start.5
  72.4 4.2 copy-start.7
  72.4 45.3 %all-to-all-start.7 = ((f32[32,8,2048]{2,1,0:T(8,128)}), f32[32,8,2048]{2,1,0:T(8,128)S(1)}, u32[]{:S(2)}, u32[]{:S(2)}) async-start(f32[32,8,2048]{2,1,0:T(8,128)} %copy.87), calls=%async_computation.7 | async-start | bytes 4194304 | tf_op jit(solution)/shard_map/all_to_all | solution.py:129
  80.5 48.5 %copy-start.6 = (f32[32,8,1024]{2,0,1:T(8,128)S(1)}, f32[32,8,1024]{2,0,1:T(8,128)}, u32[]{:S(2)}) copy-start(f32[32,8,1024]{2,0,1:T(8,128)} %get-tuple-element.19) | copy-start | bytes 3145732
  117.7 52.4 %all-to-all-start.3 = ((f32[32,8,2048]{2,1,0:T(8,128)}), f32[32,8,2048]{2,1,0:T(8,128)}, u32[]{:S(2)}, u32[]{:S(2)}) async-start(f32[32,8,2048]{2,1,0:T(8,128)} %copy.76), calls=%async_computation.3 | async-start | bytes 4194304 | tf_op jit(solution)/shard_map/all_to_all | solution.py:130
  170.1 52.4 %all-to-all-start.1 = ((f32[32,8,2048]{2,1,0:T(8,128)}), f32[32,8,2048]{2,1,0:T(8,128)}, u32[]{:S(2)}, u32[]{:S(2)}) async-start(f32[32,8,2048]{2,1,0:T(8,128)} %copy.69), calls=%async_computation.1 | async-start | bytes 4194304 | tf_op jit(solution)/shard_map/all_to_all | solution.py:131
  222.5 10.8 %copy-start.4 = (f32[2,128,2048]{1,2,0:T(8,128)S(1)}, f32[2,128,2048]{1,2,0:T(8,128)}, u32[]{:S(2)}) copy-start(f32[2,128,2048]{1,2,0:T(8,128)} %convolution_bitcast_fusion.7) | copy-start | bytes 6291460
  227.9 5.4 copy-start.1
  227.9 5.4 copy-start.2
  247.3 52.3 %all-to-all-start.4 = ((f32[2,128,2048]{2,0,1:T(2,128)}), f32[2,128,2048]{2,0,1:T(2,128)S(1)}, u32[]{:S(2)}, u32[]{:S(2)}) async-start(f32[2,128,2048]{2,0,1:T(2,128)} %copy.80), calls=%async_computation.4 | async-start | bytes 4194304 | tf_op jit(solution)/shard_map/all_to_all | solution.py:152
  299.6 1.3 copy-start.3
  300.9 52.3 %all-to-all-start.8 = ((f32[2,128,2048]{2,0,1:T(2,128)}), f32[2,128,2048]{2,0,1:T(2,128)S(1)}, u32[]{:S(2)}, u32[]{:S(2)}) async-start(f32[2,128,2048]{2,0,1:T(2,128)} %copy.91), calls=%async_computation.8 | async-start | bytes 4194304 | tf_op jit(solution)/shard_map/all_to_all | solution.py:155
  353.3 22.3 %all-to-all-start.5 = ((bf16[16,8,1024]{2,1,0:T(8,128)(2,1)}), bf16[16,8,1024]{2,1,0:T(8,128)(2,1)S(1)}, u32[]{:S(2)}, u32[]{:S(2)}) async-start(bf16[16,8,1024]{2,1,0:T(8,128)(2,1)} %copy.83), calls=%async_computation.5 | async-start | bytes 524288 | tf_op jit(solution)/shard_map/all_to_all | solution.py:162
  375.5 29.1 %all-to-all-start.9 = ((f32[32,8,1024]{2,1,0:T(8,128)}), f32[32,8,1024]{2,1,0:T(8,128)S(1)}, u32[]{:S(2)}, u32[]{:S(2)}) async-start(f32[32,8,1024]{2,1,0:T(8,128)} %copy.94), calls=%async_computation.9 | async-start | bytes 2097152 | tf_op jit(solution)/shard_map/all_to_all | solution.py:163
  381.7 176.9 %all-reduce.3.cloned.1.call-start = ((), (), s32[]{:S(2)}) async-start(), calls=%async_computation.10 | async-start | bytes 524288 | tf_op jit(solution)/shard_map/psum | solution.py:167
Sparse Core Ops, SparseCore 0:
  472.4 86.0 all-reduce.2
where the time goes:
time: 575 us; the launch traced here: 568 us
  waiting for transfers between devices  286 us (50%)
  starting transfers between devices  81.5 us (14%)
  blocking collectives  62.9 us (11%)
  matrix products  62.6 us (11%)
  local copies, waits for them, and re-layouts  44.2 us (8%)
  other arithmetic  16.5 us (3%)
  between operations  14.8 us (3%)
    psum x1, waiting for transfers between devices, on_device(): lax.psum((gradients[0], gradients[1], gradients[2], gradients[3]), 'ctx')  85.7 us
    psum x1, blocking collectives, on_device(): lax.psum((gradients[0], gradients[1], gradients[2], gradients[3]), 'ctx')  62.9 us
    all_to_all x1, waiting for transfers between devices, on_device(): lax.all_to_all(token_stack, 'ctx', split_axis=0, concat_axis=1, tiled=True)  37.2 us
    all_to_all x1, waiting for transfers between devices, on_device(): lax.all_to_all(cotan_stack, 'ctx', split_axis=0, concat_axis=1, tiled=True)  37.2 us
    all_to_all x1, waiting for transfers between devices, on_device(): lax.all_to_all(inverse_rows(input_real, input_imag), 'ctx', split_axis=1,...  34.1 us
    all_to_all x1, waiting for transfers between devices, on_device(): lax.all_to_all(inverse_rows(lagged_real, lagged_imag), 'ctx', split_axis=...  27.1 us
    all_to_all x1, waiting for transfers between devices, on_device(): lax.all_to_all(lagged_rows, 'ctx', split_axis=0, concat_axis=1, tiled=True)  22.9 us
    dot_general x5, matrix products, along_rows(): jnp.einsum('gm,imc->igc', jnp.cos(angles), stacked, precision=HIGHEST)  21.5 us
  transfers between devices with their start and end apart: 11, of which 10 were waited for; matrix products, arithmetic and copies ran while one was open for 12% of the time, Pallas kernels for 0%

commit v1 on v0

--- a/solution.py
+++ b/solution.py
@@ -1,9 +1,439 @@
+import functools
 import math
 
 import jax
 import jax.numpy as jnp
+import numpy as np
 from jax import lax
+from jax.experimental import pallas as pl
+from jax.experimental.pallas import tpu as pltpu
 from jax.sharding import PartitionSpec as P
+
+RADIX = 16
+HALF = RADIX // 2
+CHUNK = 32
+F32 = jnp.float32
+BF16 = jnp.bfloat16
+
+
+def split_pair(value):
+    high = value.astype(BF16)
+    return high, (value - high.astype(F32)).astype(BF16)
+
+
+def dot(left, right):
+    return jnp.dot(left, right, preferred_element_type=F32)
+
+
+def dot_three(left, right):
+    left_high, left_low = left
+    right_high, right_low = right
+    return dot(left_high, right_high) + (dot(left_low, right_high) + dot(left_high, right_low))
+
+
+def dft_tables(padded):
+    inner = padded // RADIX
+    grid = np.outer(np.arange(inner), np.arange(inner)) % inner
+    angles = 2.0 * np.pi * grid / inner
+    matrix = np.concatenate([np.cos(angles), np.sin(angles)], axis=0)
+    high = matrix.astype(jnp.bfloat16)
+    low = (matrix - high.astype(np.float64)).astype(jnp.bfloat16)
+    turn = 2.0 * np.pi * np.outer(np.arange(inner), np.arange(RADIX)) / padded
+    twiddle = np.zeros((inner, 128), np.float32)
+    twiddle[:, :RADIX] = np.cos(turn)
+    twiddle[:, RADIX : 2 * RADIX] = np.sin(turn)
+    return jnp.asarray(high), jnp.asarray(low), jnp.asarray(twiddle)
+
+
+def cos_of(index):
+    return math.cos(2.0 * math.pi * index / RADIX)
+
+
+def sin_of(index):
+    return math.sin(2.0 * math.pi * index / RADIX)
+
+
+def spread(x):
+    plus = [x[q] + x[q + 4] for q in range(4)]
+    minus = [x[q] - x[q + 4] for q in range(4)]
+    root = math.sqrt(0.5)
+    out = [None] * 9
+    even, odd = plus[0] + plus[2], plus[1] + plus[3]
+    out[0] = (even + odd, None)
+    out[8] = (even - odd, None)
+    out[4] = (plus[0] - plus[2], plus[3] - plus[1])
+    across, along = root * (minus[1] - minus[3]), root * (minus[1] + minus[3])
+    out[2] = (minus[0] + across, -minus[2] - along)
+    out[6] = (minus[0] - across, minus[2] - along)
+    differ = {q: x[q] - x[8 - q] for q in (1, 2, 3)}
+    same = {q: x[q] + x[8 - q] for q in (1, 2, 3)}
+    for j in (1, 3):
+        real_even = x[0] + cos_of(2 * j) * differ[2]
+        real_odd = cos_of(j) * differ[1] + cos_of(3 * j) * differ[3]
+        imag_even = sin_of(4 * j) * x[4] + sin_of(2 * j) * same[2]
+        imag_odd = sin_of(j) * same[1] + sin_of(3 * j) * same[3]
+        out[j] = (real_even + real_odd, -(imag_odd + imag_even))
+        out[8 - j] = (real_even - real_odd, imag_even - imag_odd)
+    return out
+
+
+def gather_back(real, imag):
+    even, odd = [None] * 8, [None] * 8
+    total, differ = real[0] + real[8], real[0] - real[8]
+    real_sum, real_dif = real[2] + real[6], real[2] - real[6]
+    imag_sum, imag_dif = imag[2] + imag[6], imag[2] - imag[6]
+    root = math.sqrt(0.5)
+    even[0] = total + real_sum + real[4]
+    even[4] = total - real_sum + real[4]
+    even[2] = total - imag_dif - real[4]
+    even[6] = total + imag_dif - real[4]
+    first, second = root * (real_dif - imag_sum), root * (real_dif + imag_sum)
+    even[1] = differ + first - imag[4]
+    even[5] = differ - first - imag[4]
+    even[3] = differ - second + imag[4]
+    even[7] = differ + second + imag[4]
+    one_sum, one_dif = real[1] + real[7], real[1] - real[7]
+    three_sum, three_dif = real[3] + real[5], real[3] - real[5]
+    ione_sum, ione_dif = imag[1] + imag[7], imag[1] - imag[7]
+    ithree_sum, ithree_dif = imag[3] + imag[5], imag[3] - imag[5]
+    odd[0] = one_sum + three_sum
+    odd[4] = ithree_dif - ione_dif
+    for q in (1, 2, 3):
+        if q % 2 == 0:
+            cosines = cos_of(q) * one_sum + cos_of(3 * q) * three_sum
+            sines = sin_of(q) * ione_dif + sin_of(3 * q) * ithree_dif
+        else:
+            cosines = cos_of(q) * one_dif + cos_of(3 * q) * three_dif
+            sines = sin_of(q) * ione_sum + sin_of(3 * q) * ithree_sum
+        odd[q] = cosines - sines
+        odd[8 - q] = -cosines - sines
+    return even, odd
+
+
+def residues_to_scratch(load, twiddle, high_ref, low_ref, inner):
+    def chunk(step, carry):
+        start = pl.multiple_of(step * CHUNK, CHUNK)
+        rows = pl.ds(start, CHUNK)
+        turn = twiddle[rows, :]
+        for j, (real, imag) in enumerate(spread([load(q * inner + start) for q in range(HALF)])):
+            if j > 0:
+                cosine, sine = turn[:, j : j + 1], turn[:, RADIX + j : RADIX + j + 1]
+                if imag is None:
+                    real, imag = real * cosine, -real * sine
+                else:
+                    real, imag = real * cosine + imag * sine, imag * cosine - real * sine
+            else:
+                imag = jnp.zeros_like(real)
+            for part, value in enumerate((real, imag)):
+                high, low = split_pair(value)
+                high_ref[j, rows, 128 * part : 128 * part + 128] = high
+                low_ref[j, rows, 128 * part : 128 * part + 128] = low
+        return carry
+
+    lax.fori_loop(0, inner // CHUNK, chunk, 0)
+
+
+def inner_dft(pair, matrix_high, matrix_low, inner, direction):
+    high, low = pair
+    product = dot_three((matrix_high[...], matrix_low[...]), (high, low))
+    cos_real, cos_imag = product[:inner, :128], product[:inner, 128:]
+    sin_real, sin_imag = product[inner:, :128], product[inner:, 128:]
+    if direction > 0:
+        return cos_real + sin_imag, cos_imag - sin_real
+    return cos_real - sin_imag, cos_imag + sin_real
+
+
+def low_lanes(rows):
+    return lax.broadcasted_iota(jnp.int32, (rows, 128), 1) < 64
+
+
+def swap(value):
+    return pltpu.roll(value, 64, 1)
+
+
+def pack_kernel(tokens, cotan, out):
+    for block in range(out.shape[0]):
+        lanes = slice(64 * block, 64 * block + 64)
+        out[block] = jnp.concatenate([tokens[:, lanes], cotan[:, lanes]], axis=1)
+
+
+def kernel_spectrum_kernel(
+    length, rate, scale, w_first, w_bias, w_mid, w_last, matrix_high, matrix_low, twiddle,
+    spectrum, env_out, slope_one, slope_two, one_high, one_low, two_high, two_low,
+    taps, high_ref, low_ref,
+):
+    padded = 2 * length
+    inner = padded // RADIX
+    low_half = low_lanes(inner)
+    mid_pair = split_pair(w_mid[...])
+    last_pair = split_pair(w_last[...])
+
+    def block(step, carry):
+        start = pl.multiple_of(step * inner, inner)
+        rows = pl.ds(start, inner)
+        place = start + lax.broadcasted_iota(jnp.int32, (inner, 128), 0)
+        lag = jnp.where(low_half, place, place - length)
+        scaled = lag.astype(F32) / length
+        pre_one = scaled * w_first[...] + w_bias[...]
+        gate_one = 1.0 / (1.0 + jnp.exp(-pre_one))
+        hidden_one = pre_one * gate_one
+        slope_one[rows, :] = gate_one * (1.0 + pre_one * (1.0 - gate_one))
+        pre_two = dot_three(split_pair(hidden_one), mid_pair)
+        gate_two = 1.0 / (1.0 + jnp.exp(-pre_two))
+        hidden_two = pre_two * gate_two
+        slope_two[rows, :] = gate_two * (1.0 + pre_two * (1.0 - gate_two))
+        position = dot_three(split_pair(hidden_two), last_pair)
+        live = jnp.where(lag == -length, 0.0, 1.0)
+        env = live * scale[...] * jnp.exp(-jnp.abs(lag).astype(F32) * rate[...])
+        taps[rows, :] = (position * env).astype(BF16).astype(F32)
+        env_out[rows, 0:128] = jnp.where(low_half, 0.0, swap(env))
+        env_out[rows, 128:256] = jnp.where(low_half, 0.0, env)
+        one_high[:, rows], one_low[:, rows] = split_pair(hidden_one.T)
+        two_high[:, rows], two_low[:, rows] = split_pair(hidden_two.T)
+        return carry
+
+    lax.fori_loop(0, HALF, block, 0)
+    residues_to_scratch(
+        lambda start: taps[pl.ds(start, CHUNK), :], twiddle, high_ref, low_ref, inner
+    )
+
+    def transform(j, carry):
+        real, imag = inner_dft((high_ref[j], low_ref[j]), matrix_high, matrix_low, inner, 1)
+        sign = (1 - 2 * (j % 2)).astype(F32)
+        spectrum[j, :, 0:128] = real + sign * swap(real)
+        spectrum[j, :, 128:256] = imag + sign * swap(imag)
+        return carry
+
+    lax.fori_loop(0, HALF + 1, transform, 0)
+
+
+def gradient_kernel(
+    length, signal, spectrum, env, slope_one, slope_two, one_high, one_low, two_high, two_low,
+    mid_back, last_back, matrix_high, matrix_low, twiddle, out, high_ref, low_ref, back_ref,
+    last_sum, mid_sum, first_sum,
+):
+    padded = 2 * length
+    inner = padded // RADIX
+    low_half = low_lanes(inner)
+    residues_to_scratch(
+        lambda start: signal[pl.ds(start, CHUNK), :].astype(F32), twiddle, high_ref, low_ref, inner
+    )
+
+    def transform(j, carry):
+        real, imag = inner_dft((high_ref[j], low_ref[j]), matrix_high, matrix_low, inner, 1)
+        real_swap, imag_swap = swap(real), swap(imag)
+        cotan_real = jnp.where(low_half, real_swap, real)
+        cotan_imag = jnp.where(low_half, imag_swap, imag)
+        other_real = jnp.where(low_half, spectrum[j, :, 0:128], real_swap)
+        other_imag = jnp.where(low_half, spectrum[j, :, 128:256], imag_swap)
+        product = jnp.concatenate(
+            [
+                cotan_real * other_real + cotan_imag * other_imag,
+                cotan_imag * other_real - cotan_real * other_imag,
+            ],
+            axis=1,
+        )
+        real, imag = inner_dft(split_pair(product), matrix_high, matrix_low, inner, -1)
+        back_ref[j, :, 0:128] = real
+        back_ref[j, :, 128:256] = imag
+        return carry
+
+    lax.fori_loop(0, HALF + 1, transform, 0)
+
+    def unspread(step, carry):
+        start = pl.multiple_of(step * CHUNK, CHUNK)
+        rows = pl.ds(start, CHUNK)
+        turn = twiddle[rows, :]
+        real_list, imag_list = [], []
+        for j in range(HALF + 1):
+            weight = (1.0 if j in (0, HALF) else 2.0) / padded
+            real, imag = back_ref[j, rows, 0:128], back_ref[j, rows, 128:256]
+            if j == 0:
+                real_list.append(real * weight)
+                imag_list.append(None)
+                continue
+            cosine = turn[:, j : j + 1] * weight
+            sine = turn[:, RADIX + j : RADIX + j + 1] * weight
+            real_list.append(real * cosine - imag * sine)
+            imag_list.append(real * sine + imag * cosine)
+        even, odd = gather_back(real_list, imag_list)
+        for q in range(HALF):
+            back_ref[q, rows, 0:128] = even[q] + odd[q]
+            back_ref[q, rows, 128:256] = even[q] - odd[q]
+        return carry
+
+    lax.fori_loop(0, inner // CHUNK, unspread, 0)
+    last_sum[...] = jnp.zeros_like(last_sum)
+    mid_sum[...] = jnp.zeros_like(mid_sum)
+    first_sum[...] = jnp.zeros_like(first_sum)
+    mid_pair = split_pair(mid_back[...])
+    last_pair = split_pair(last_back[...])
+    local_rows = 128
+    half_rows = local_rows // 2
+
+    def block(q, carry):
+        start = pl.multiple_of(q * inner, inner)
+        rows = pl.ds(start, inner)
+        for part in range(inner // local_rows):
+            base = part * local_rows
+            upper = back_ref[q, base : base + half_rows, 0:128]
+            lower = back_ref[q, base + half_rows : base + local_rows, 0:128]
+            out[q * (inner // local_rows) + part, 0:half_rows, :] = jnp.where(
+                low_half[:half_rows], upper, swap(lower)
+            ).astype(BF16)
+        slope = split_pair(back_ref[q] * env[rows, :])
+        last_sum[...] += dot_three((two_high[:, rows], two_low[:, rows]), slope)
+        pre_two = split_pair(dot_three(slope, last_pair) * slope_two[rows, :])
+        mid_sum[...] += dot_three((one_high[:, rows], one_low[:, rows]), pre_two)
+        pre_one = dot_three(pre_two, mid_pair) * slope_one[rows, :]
+        place = start + lax.broadcasted_iota(jnp.int32, (inner, 128), 0)
+        scaled = jnp.where(low_half, place, place - length).astype(F32) / length
+        first_sum[0:8] += jnp.sum((pre_one * scaled).reshape(inner // 8, 8, 128), axis=0)
+        first_sum[8:16] += jnp.sum(pre_one.reshape(inner // 8, 8, 128), axis=0)
+        return carry
+
+    lax.fori_loop(0, HALF, block, 0)
+    low_64 = low_lanes(64)
+    low_32 = low_lanes(32)
+    grad_last = swap(last_sum[0:64, 0:128]) + swap(last_sum[64:128, 128:256])
+    pair = jnp.where(low_32, grad_last[0:32], swap(grad_last[32:64]))
+    mid_total = mid_sum[0:64] + swap(mid_sum[64:128])
+    mid_high = mid_total.astype(BF16).astype(F32)
+    mid_rows = jnp.where(low_64, mid_high, swap(mid_total - mid_high))
+    first = jnp.sum(first_sum[0:8], axis=0, keepdims=True)
+    bias = jnp.sum(first_sum[8:16], axis=0, keepdims=True)
+    first = first + swap(first)
+    bias = bias + swap(bias)
+    joined = jnp.where(low_lanes(1), first, bias)
+    joined_high = joined.astype(BF16).astype(F32)
+    row_index = lax.broadcasted_iota(jnp.int32, (16, 128), 0)
+    joined_rows = jnp.where(
+        row_index == 0, joined_high, jnp.where(row_index == 1, joined - joined_high, 0.0)
+    )
+    tail = jnp.concatenate([pair, mid_rows, joined_rows], axis=0).astype(BF16)
+    for device in range(out.shape[0]):
+        out[device, half_rows:, :] = tail
+
+
+def unpack_kernel(loss_scale, received, grad_tokens, grad_first, grad_bias, grad_mid, grad_last):
+    devices = received.shape[0]
+    half_rows = grad_tokens.shape[0] // 2
+    mid = jnp.zeros((64, 128), F32)
+    joined = jnp.zeros((16, 128), F32)
+    for source in range(devices):
+        lanes = slice(64 * source, 64 * source + 64)
+        tile = received[source, 0:half_rows, :]
+        grad_tokens[0:half_rows, lanes] = tile[:, 0:64]
+        grad_tokens[half_rows:, lanes] = tile[:, 64:128]
+        last = received[source, half_rows : half_rows + 32, :].astype(F32) * loss_scale
+        grad_last[0:32, lanes] = last[:, 0:64]
+        grad_last[32:64, lanes] = last[:, 64:128]
+        mid = mid + received[source, half_rows + 32 : half_rows + 96, :].astype(F32)
+        joined = joined + received[source, half_rows + 96 : half_rows + 112, :].astype(F32)
+    grad_mid[...] = ((mid + swap(mid)) * loss_scale)[:, 0:64]
+    first = (joined[0:1] + joined[1:2]) * loss_scale
+    grad_first[...] = first[:, 0:64]
+    grad_bias[...] = first[:, 64:128]
+
+
+def call(kernel, out_shape, scratch=(), flops=0, limit=24):
+    return pl.pallas_call(
+        kernel,
+        out_shape=out_shape,
+        scratch_shapes=list(scratch),
+        compiler_params=pltpu.CompilerParams(vmem_limit_bytes=limit << 20),
+        cost_estimate=pl.CostEstimate(flops=flops, bytes_accessed=1 << 20, transcendentals=0),
+    )
+
+
+def shape(dims, dtype):
+    return jax.ShapeDtypeStruct(dims, dtype)
+
+
+def twice(value):
+    return jnp.concatenate([value, value]).reshape(1, -1)
+
+
+def diagonal(matrix):
+    empty = jnp.zeros_like(matrix)
+    return jnp.block([[matrix, empty], [empty, matrix]])
+
+
+def by_channels(tokens_in, grad_out, decay_rate, w_in, b_in, w_mid, w_out):
+    devices = lax.axis_size("ctx")
+    own_index = lax.axis_index("ctx")
+    local_rows = tokens_in.shape[0]
+    length = local_rows * devices
+    padded = 2 * length
+    inner = padded // RADIX
+    bins = HALF + 1
+    matrix_high, matrix_low, twiddle = dft_tables(padded)
+    packed = call(pack_kernel, shape((devices, local_rows, 128), BF16))(tokens_in, grad_out)
+    signal = lax.all_to_all(packed, "ctx", split_axis=0, concat_axis=0, tiled=True)
+    signal = signal.reshape(length, 128)
+
+    own_last = lax.dynamic_slice_in_dim(w_out, own_index * 64, 64, axis=1)
+    own_rate = lax.dynamic_slice_in_dim(decay_rate, own_index * 64, 64, axis=0)
+    double = 2.0 * own_rate
+    geometric = 1.0 + 2.0 * jnp.exp(-double) * jnp.expm1(-double * (length - 1)) / jnp.expm1(
+        -double
+    )
+    stage = [pltpu.VMEM((bins, inner, 256), BF16)] * 2
+    (spectrum, env, slope_one, slope_two, one_high, one_low, two_high, two_low) = call(
+        functools.partial(kernel_spectrum_kernel, length),
+        [
+            shape((bins, inner, 256), F32),
+            shape((length, 256), F32),
+            shape((length, 128), F32),
+            shape((length, 128), F32),
+        ]
+        + [shape((128, length), BF16)] * 4,
+        scratch=[pltpu.VMEM((length, 128), F32)] + stage,
+        flops=4 << 30,
+    )(
+        twice(own_rate),
+        twice(lax.rsqrt(geometric)),
+        twice(w_in),
+        twice(b_in),
+        diagonal(w_mid),
+        diagonal(own_last),
+        matrix_high,
+        matrix_low,
+        twiddle,
+    )
+    empty = jnp.zeros((64, 64), F32)
+    last_back = jnp.block(
+        [[empty, empty], [own_last.T, empty], [empty, empty], [empty, own_last.T]]
+    )
+    sent_rows = local_rows // 2 + 32 + 64 + 16
+    sent = call(
+        functools.partial(gradient_kernel, length),
+        shape((devices, sent_rows, 128), BF16),
+        scratch=stage
+        + [
+            pltpu.VMEM((bins, inner, 256), F32),
+            pltpu.VMEM((128, 256), F32),
+            pltpu.VMEM((128, 128), F32),
+            pltpu.VMEM((16, 128), F32),
+        ],
+        flops=8 << 30,
+    )(
+        signal, spectrum, env, slope_one, slope_two, one_high, one_low, two_high, two_low,
+        diagonal(w_mid.T), last_back, matrix_high, matrix_low, twiddle,
+    )
+    received = lax.all_to_all(sent, "ctx", split_axis=0, concat_axis=0, tiled=True)
+    input_grad, grad_first, grad_bias, grad_mid, grad_last = call(
+        functools.partial(unpack_kernel, 1.0 / math.sqrt(length)),
+        [
+            shape(tokens_in.shape, BF16),
+            shape((1, 64), F32),
+            shape((1, 64), F32),
+            shape((64, 64), F32),
+            shape(w_out.shape, F32),
+        ],
+    )(received)
+    return input_grad, grad_first.reshape(64), grad_bias.reshape(64), grad_mid, grad_last
+
 
 HIGHEST = lax.Precision.HIGHEST
 TWO_PI = 2.0 * math.pi
@@ -81,7 +511,7 @@
     )
 
 
-def on_device(tokens_in, grad_out, decay_rate, w_in, b_in, w_mid, w_out):
+def by_frequencies(tokens_in, grad_out, decay_rate, w_in, b_in, w_mid, w_out):
     devices = lax.axis_size("ctx")
     own_index = lax.axis_index("ctx")
     tok_rows = tokens_in.shape[0]
@@ -175,6 +605,17 @@
     )
 
 
+def on_device(tokens_in, grad_out, decay_rate, w_in, b_in, w_mid, w_out):
+    devices = lax.axis_size("ctx")
+    fits = (
+        tokens_in.shape == (128, 64 * devices)
+        and devices * 128 % (128 * HALF) == 0
+        and w_mid.shape == (64, 64)
+    )
+    form = by_channels if fits else by_frequencies
+    return form(tokens_in, grad_out, decay_rate, w_in, b_in, w_mid, w_out)
+
+
 def solution(mesh):
     in_specs = (P(("groups", "ctx"), None), P(("groups", "ctx"), None), P(), P(), P(), P(), P())
     out_specs = (

time: 575 us -> 81.5 us (0.14); the launches traced: 568 us -> 80.7 us
  waiting for transfers between devices: 286 us -> 0.01 us
  starting transfers between devices: 81.5 us -> 7.36 us
  matrix products: 62.6 us -> 0 us
  blocking collectives: 62.9 us -> 24.9 us
  Pallas kernels: 0 us -> 30.3 us
  local copies, waits for them, and re-layouts: 44.2 us -> 16.1 us
  other arithmetic: 16.5 us -> 1.26 us
  between operations: 14.8 us -> 0.78 us
    all_to_all x10 -> x1, waiting for transfers between devices: 200 us -> 0.01 us  [by_channels(): lax.all_to_all(packed, 'ctx', split_axis=0, concat_axis=0, tiled=True)]
    psum x1 -> x0, waiting for transfers between devices: 85.7 us -> none  [on_device(): lax.psum((gradients[0], gradients[1], gradients[2], gradients[3]), 'ctx')]
    all_to_all x10 -> x1, starting transfers between devices: 81.5 us -> 7.36 us  [by_channels(): lax.all_to_all(packed, 'ctx', split_axis=0, concat_axis=0, tiled=True)]
    psum x1 -> x0, blocking collectives: 62.9 us -> none  [on_device(): lax.psum((gradients[0], gradients[1], gradients[2], gradients[3]), 'ctx')]
    dot_general x26 -> x0, matrix products: 62.6 us -> none  [the longest x5 21.5 us: along_rows(): jnp.einsum('gm,imc->igc', jnp.cos(angles), stacked, precision=HIGHEST)]
    pallas_call x0 -> x4, Pallas kernels: none -> 30.3 us  [the longest x1 18.9 us: by_channels(): call(functools.partial(gradient_kernel, length), shape((devices, sent_row...]
    all_to_all x0 -> x1, blocking collectives: none -> 24.9 us  [by_channels(): lax.all_to_all(sent, 'ctx', split_axis=0, concat_axis=0, tiled=True)]
    all_to_all x8 -> x0, local copies, waits for them, and re-layouts: 18.7 us -> none  [the longest x3 9.39 us: on_device(): lax.all_to_all(inverse_rows(input_real, input_imag), 'ctx', split_axis=1,...]
  transfers between devices with their start and end apart: 11 -> 1, of which waited for: 10 -> 0; matrix products, arithmetic and copies ran while one was open for 12% -> 2% of each run, Pallas kernels for 0% -> 12%
where the time goes in v1:
time: 81.5 us; the launch traced here: 80.7 us
  Pallas kernels  30.3 us (37%)
  blocking collectives  24.9 us (31%)
  local copies, waits for them, and re-layouts  16.1 us (20%)
  starting transfers between devices  7.36 us (9%)
  other arithmetic  1.26 us (2%)
    all_to_all x1, blocking collectives, by_channels(): lax.all_to_all(sent, 'ctx', split_axis=0, concat_axis=0, tiled=True)  24.9 us
    pallas_call x1, Pallas kernels, by_channels(): call(functools.partial(gradient_kernel, length), shape((devices, sent_row...  18.9 us
    unnamed x44, local copies, waits for them, and re-layouts  15.9 us
    pallas_call x1, Pallas kernels, by_channels(): call(functools.partial(kernel_spectrum_kernel, length), [shape((bins, inn...  9.29 us
    all_to_all x1, starting transfers between devices, by_channels(): lax.all_to_all(packed, 'ctx', split_axis=0, concat_axis=0, tiled=True)  7.36 us
  transfers between devices with their start and end apart: 1, of which 0 were waited for; matrix products, arithmetic and copies ran while one was open for 2% of the time, Pallas kernels for 12%

profile of v1, /device:TPU:0, one launch (start us, length us, event | category | flops | bytes accessed | tf_op | source)
XLA Modules:
  0.0 80.7 jit_solution(16001813752690139623)
XLA Ops:
  0.7 1.0 %copy-done.1 = bf16[128,1024]{1,0:T(8,128)(2,1)S(1)} copy-done((bf16[128,1024]{1,0:T(8,128)(2,1)S(1)}, bf16[128,1024]{1,0:T(8,128)(2,1)}, u32[]{:S(2)}) %copy-start.1) | copy-done | bytes 262168
  1.6 0.9 %copy-done.2 = bf16[128,1024]{1,0:T(8,128)(2,1)S(1)} copy-done((bf16[128,1024]{1,0:T(8,128)(2,1)S(1)}, bf16[128,1024]{1,0:T(8,128)(2,1)}, u32[]{:S(2)}) %copy-start.2) | copy-done | bytes 262168
  2.6 1.0 %shard_map.137 = bf16[16,128,128]{2,1,0:T(8,128)(2,1)} custom-call(bf16[128,1024]{1,0:T(8,128)(2,1)S(1)} %copy-done.1, bf16[128,1024]{1,0:T(8,128)(2,1)S(1)} %copy-done.2), custom_call_target="tpu_custom_call" | custom-call | bytes 1048576 | tf_op jit(solution)/shard_map/pallas_call | solution.py:371
  3.6 7.4 %all-to-all-start = ((bf16[16,128,128]{2,1,0:T(8,128)(2,1)}), bf16[16,128,128]{2,1,0:T(8,128)(2,1)S(1)}, u32[]{:S(2)}, u32[]{:S(2)}) async-start(bf16[16,128,128]{2,1,0:T(8,128)(2,1)} %shard_map.137), calls=%async_computation | async-start | bytes 1048576 | tf_op jit(solution)/shard_map/all_to_all | solution.py:372
  11.0 0.1 constant_dynamic-slice_fusion
  11.2 0.1 select_maximum_fusion.3
  11.2 0.8 add_rsqrt_fusion
  12.1 0.1 copy.16.w_last
  12.7 9.3 %shard_map.138 = (f32[9,256,256]{2,1,0:T(8,128)S(1)}, f32[2048,256]{1,0:T(8,128)S(1)}, f32[2048,128]{1,0:T(8,128)S(1)}, f32[2048,128]{1,0:T(8,128)S(1)}, bf16[12...) custom-call(f32[1,128]{1,0:T(1,128)S(1)} %get-tuple-element.33.rate,, ...), custom_call_target="tpu_custom_call" | custom-call | flops 4294967296 | bytes 1048576 | tf_op jit(solution)/shard_map/pallas_call | solution.py:382
  22.0 1.4 %copy-done.6 = f32[9,256,256]{2,1,0:T(8,128)} copy-done((f32[9,256,256]{2,1,0:T(8,128)}, f32[9,256,256]{2,1,0:T(8,128)S(1)}, u32[]{:S(2)}) %copy-start.6) | copy-done | bytes 2359320
  23.4 1.3 %copy-done.8 = f32[2048,256]{1,0:T(8,128)} copy-done((f32[2048,256]{1,0:T(8,128)}, f32[2048,256]{1,0:T(8,128)S(1)}, u32[]{:S(2)}) %copy-start.8) | copy-done | bytes 2097176
  24.7 1.0 %copy-done.10 = f32[2048,128]{1,0:T(8,128)} copy-done((f32[2048,128]{1,0:T(8,128)}, f32[2048,128]{1,0:T(8,128)S(1)}, u32[]{:S(2)}) %copy-start.10) | copy-done | bytes 1048600
  25.7 0.8 %copy-done.12 = bf16[128,2048]{1,0:T(8,128)(2,1)} copy-done((bf16[128,2048]{1,0:T(8,128)(2,1)}, bf16[128,2048]{1,0:T(8,128)(2,1)S(1)}, u32[]{:S(2)}) %copy-start.12) | copy-done | bytes 524312
  26.5 0.8 copy-done.14
  27.3 0.8 copy-done.16
  28.1 1.7 %copy-done.7 = f32[9,256,256]{2,1,0:T(8,128)S(1)} copy-done((f32[9,256,256]{2,1,0:T(8,128)S(1)}, f32[9,256,256]{2,1,0:T(8,128)}, u32[]{:S(2)}) %copy-start.7) | copy-done | bytes 2359320
  29.8 1.6 %copy-done.9 = f32[2048,256]{1,0:T(8,128)S(1)} copy-done((f32[2048,256]{1,0:T(8,128)S(1)}, f32[2048,256]{1,0:T(8,128)}, u32[]{:S(2)}) %copy-start.9) | copy-done | bytes 2097176
  31.4 1.2 %copy-done.11 = f32[2048,128]{1,0:T(8,128)S(1)} copy-done((f32[2048,128]{1,0:T(8,128)S(1)}, f32[2048,128]{1,0:T(8,128)}, u32[]{:S(2)}) %copy-start.11) | copy-done | bytes 1048600
  32.6 1.0 %copy-done.13 = bf16[128,2048]{1,0:T(8,128)(2,1)S(1)} copy-done((bf16[128,2048]{1,0:T(8,128)(2,1)S(1)}, bf16[128,2048]{1,0:T(8,128)(2,1)}, u32[]{:S(2)}) %copy-start.13) | copy-done | bytes 524312
  33.7 1.0 %copy-done.15 = bf16[128,2048]{1,0:T(8,128)(2,1)S(1)} copy-done((bf16[128,2048]{1,0:T(8,128)(2,1)S(1)}, bf16[128,2048]{1,0:T(8,128)(2,1)}, u32[]{:S(2)}) %copy-start.15) | copy-done | bytes 524312
  34.7 1.0 %copy-done.17 = bf16[128,2048]{1,0:T(8,128)(2,1)S(1)} copy-done((bf16[128,2048]{1,0:T(8,128)(2,1)S(1)}, bf16[128,2048]{1,0:T(8,128)(2,1)}, u32[]{:S(2)}) %copy-start.17) | copy-done | bytes 524312
  35.7 18.9 %shard_map.139 = bf16[16,176,128]{2,1,0:T(8,128)(2,1)S(1)} custom-call(bf16[2048,128]{1,0:T(8,128)(2,1)S(1)} %bitcast.13, f32[9,256,256]{2,1,0:T(8,128)S(1)} %copy-done.7, f32[2048,256]{1,0:T(8,128)S(1)} %copy-done.9, f32[2048,128]{1,0:T(8,128)S(1)} %get-tuple-element.20.slope_one, f32[2048,128]{1,0:T(8,128)S(1)} %copy-done.11, ...), custom_call_target="tpu_custom_call" | custom-call | flops 8589934592 | bytes 1048576 | tf_op jit(solution)/shard_map/pallas_call | solution.py:409
  54.7 24.9 %all_to_all.10.received = bf16[16,176,128]{2,1,0:T(8,128)(2,1)S(1)} all-to-all(bf16[16,176,128]{2,1,0:T(8,128)(2,1)S(1)} %shard_map.139), channel_id=1, replica_groups=mesh['groups'=2,'ctx'=16] {'ctx'}, dimensions={0} | all-to-all | bytes 1441792 | tf_op jit(solution)/shard_map/all_to_all | solution.py:424
  79.6 1.1 %shard_map.140 = (bf16[128,1024]{1,0:T(8,128)(2,1)}, f32[1,64]{1,0:T(1,128)}, f32[1,64]{1,0:T(1,128)}, f32[64,64]{1,0:T(8,128)}, f32[64,1024]{1,0:T(8,128)}) custom-call(bf16[16,176,128]{2,1,0:T(8,128)(2,1)S(1)} %all_to_all.10.received), custom_call_target="tpu_custom_call" | custom-call | bytes 1048576 | tf_op jit(solution)/shard_map/pallas_call | solution.py:425
  (39 shorter events, 0.6 us)
Async XLA Ops:
  0.6 10.4 %copy-start = (f32[64,1024]{1,0:T(8,128)S(1)}, f32[64,1024]{1,0:T(8,128)}, u32[]{:S(2)}) copy-start(f32[64,1024]{1,0:T(8,128)} %param.16) | copy-start | bytes 786436
  0.6 1.0 %copy-start.1 = (bf16[128,1024]{1,0:T(8,128)(2,1)S(1)}, bf16[128,1024]{1,0:T(8,128)(2,1)}, u32[]{:S(2)}) copy-start(bf16[128,1024]{1,0:T(8,128)(2,1)} %tokens.1) | copy-start | bytes 786436
  1.6 0.9 %copy-start.2 = (bf16[128,1024]{1,0:T(8,128)(2,1)S(1)}, bf16[128,1024]{1,0:T(8,128)(2,1)}, u32[]{:S(2)}) copy-start(bf16[128,1024]{1,0:T(8,128)(2,1)} %cotan.1) | copy-start | bytes 786436
  2.6 9.5 %copy-start.18 = (f32[64,64]{1,0:T(8,128)S(1)}, f32[64,64]{1,0:T(8,128)}, u32[]{:S(2)}) copy-start(f32[64,64]{1,0:T(8,128)} %param.15) | copy-start | bytes 49156
  2.6 9.7 %copy-start.19 = (f32[64]{0:T(128)S(1)}, f32[64]{0:T(128)}, u32[]{:S(2)}) copy-start(f32[64]{0:T(128)} %param.13) | copy-start | bytes 772
  2.6 9.7 %copy-start.20 = (f32[64]{0:T(128)S(1)}, f32[64]{0:T(128)}, u32[]{:S(2)}) copy-start(f32[64]{0:T(128)} %param.14) | copy-start | bytes 772
  2.6 10.0 %copy-start.3 = (bf16[512,256]{1,0:T(8,128)(2,1)S(1)}, bf16[512,256]{1,0:T(8,128)(2,1)}, u32[]{:S(2)}) copy-start(bf16[512,256]{1,0:T(8,128)(2,1)} %constant.25.clone.matrix_low) | copy-start | bytes 786436
  2.6 10.0 %copy-start.4 = (bf16[512,256]{1,0:T(8,128)(2,1)S(1)}, bf16[512,256]{1,0:T(8,128)(2,1)}, u32[]{:S(2)}) copy-start(bf16[512,256]{1,0:T(8,128)(2,1)} %constant.24.clone.matrix_high) | copy-start | bytes 786436
  2.6 10.0 %copy-start.5 = (f32[256,128]{1,0:T(8,128)S(1)}, f32[256,128]{1,0:T(8,128)}, u32[]{:S(2)}) copy-start(f32[256,128]{1,0:T(8,128)} %constant.26.clone.twiddle) | copy-start | bytes 393220
  3.6 24.5 %all-to-all-start = ((bf16[16,128,128]{2,1,0:T(8,128)(2,1)}), bf16[16,128,128]{2,1,0:T(8,128)(2,1)S(1)}, u32[]{:S(2)}, u32[]{:S(2)}) async-start(bf16[16,128,128]{2,1,0:T(8,128)(2,1)} %shard_map.137), calls=%async_computation | async-start | bytes 1048576 | tf_op jit(solution)/shard_map/all_to_all | solution.py:372
  22.0 1.4 %copy-start.6 = (f32[9,256,256]{2,1,0:T(8,128)}, f32[9,256,256]{2,1,0:T(8,128)S(1)}, u32[]{:S(2)}) copy-start(f32[9,256,256]{2,1,0:T(8,128)S(1)} %get-tuple-element.18.spectrum) | copy-start | bytes 7077892
  23.4 1.3 %copy-start.8 = (f32[2048,256]{1,0:T(8,128)}, f32[2048,256]{1,0:T(8,128)S(1)}, u32[]{:S(2)}) copy-start(f32[2048,256]{1,0:T(8,128)S(1)} %get-tuple-element.19.env) | copy-start | bytes 6291460
  24.7 1.0 %copy-start.10 = (f32[2048,128]{1,0:T(8,128)}, f32[2048,128]{1,0:T(8,128)S(1)}, u32[]{:S(2)}) copy-start(f32[2048,128]{1,0:T(8,128)S(1)} %get-tuple-element.21.slope_two) | copy-start | bytes 3145732
  25.7 0.8 %copy-start.12 = (bf16[128,2048]{1,0:T(8,128)(2,1)}, bf16[128,2048]{1,0:T(8,128)(2,1)S(1)}, u32[]{:S(2)}) copy-start(bf16[128,2048]{1,0:T(8,128)(2,1)S(1)} %get-tuple-element.23.one_low) | copy-start | bytes 1572868
  26.5 0.8 copy-start.14
  27.3 0.8 copy-start.16
  28.1 1.7 %copy-start.7 = (f32[9,256,256]{2,1,0:T(8,128)S(1)}, f32[9,256,256]{2,1,0:T(8,128)}, u32[]{:S(2)}) copy-start(f32[9,256,256]{2,1,0:T(8,128)} %copy-done.6) | copy-start | bytes 7077892
  29.8 1.6 %copy-start.9 = (f32[2048,256]{1,0:T(8,128)S(1)}, f32[2048,256]{1,0:T(8,128)}, u32[]{:S(2)}) copy-start(f32[2048,256]{1,0:T(8,128)} %copy-done.8) | copy-start | bytes 6291460
  31.4 1.2 %copy-start.11 = (f32[2048,128]{1,0:T(8,128)S(1)}, f32[2048,128]{1,0:T(8,128)}, u32[]{:S(2)}) copy-start(f32[2048,128]{1,0:T(8,128)} %copy-done.10) | copy-start | bytes 3145732
  32.6 1.0 %copy-start.13 = (bf16[128,2048]{1,0:T(8,128)(2,1)S(1)}, bf16[128,2048]{1,0:T(8,128)(2,1)}, u32[]{:S(2)}) copy-start(bf16[128,2048]{1,0:T(8,128)(2,1)} %copy-done.12) | copy-start | bytes 1572868
  33.7 1.0 %copy-start.15 = (bf16[128,2048]{1,0:T(8,128)(2,1)S(1)}, bf16[128,2048]{1,0:T(8,128)(2,1)}, u32[]{:S(2)}) copy-start(bf16[128,2048]{1,0:T(8,128)(2,1)} %copy-done.14) | copy-start | bytes 1572868
  34.7 1.0 %copy-start.17 = (bf16[128,2048]{1,0:T(8,128)(2,1)S(1)}, bf16[128,2048]{1,0:T(8,128)(2,1)}, u32[]{:S(2)}) copy-start(bf16[128,2048]{1,0:T(8,128)(2,1)} %copy-done.16) | copy-start | bytes 1572868

commit v2 on v1

--- a/solution.py
+++ b/solution.py
@@ -12,6 +12,9 @@
 RADIX = 16
 HALF = RADIX // 2
 CHUNK = 32
+UNROLL_CHUNK = 1
+UNROLL_BIN = 1
+UNROLL_ROWS = 1
 F32 = jnp.float32
 BF16 = jnp.bfloat16
 
@@ -25,10 +28,14 @@
     return jnp.dot(left, right, preferred_element_type=F32)
 
 
-def dot_three(left, right):
-    left_high, left_low = left
-    right_high, right_low = right
-    return dot(left_high, right_high) + (dot(left_low, right_high) + dot(left_high, right_low))
+def wide_three(value):
+    high, low = split_pair(value)
+    return jnp.concatenate([high, low, high], axis=1)
+
+
+def tall_three(value):
+    high, low = split_pair(value)
+    return jnp.concatenate([high, high, low], axis=0)
 
 
 def dft_tables(padded):
@@ -38,11 +45,12 @@
     matrix = np.concatenate([np.cos(angles), np.sin(angles)], axis=0)
     high = matrix.astype(jnp.bfloat16)
     low = (matrix - high.astype(np.float64)).astype(jnp.bfloat16)
+    matrix = np.concatenate([high, low, high], axis=1)
     turn = 2.0 * np.pi * np.outer(np.arange(inner), np.arange(RADIX)) / padded
     twiddle = np.zeros((inner, 128), np.float32)
     twiddle[:, :RADIX] = np.cos(turn)
     twiddle[:, RADIX : 2 * RADIX] = np.sin(turn)
-    return jnp.asarray(high), jnp.asarray(low), jnp.asarray(twiddle)
+    return jnp.asarray(matrix), jnp.asarray(twiddle)
 
 
 def cos_of(index):
@@ -110,11 +118,10 @@
     return even, odd
 
 
-def residues_to_scratch(load, twiddle, high_ref, low_ref, inner):
+def residues_to_scratch(load, twiddle, stage, inner):
     def chunk(step, carry):
         start = pl.multiple_of(step * CHUNK, CHUNK)
-        rows = pl.ds(start, CHUNK)
-        turn = twiddle[rows, :]
+        turn = twiddle[pl.ds(start, CHUNK), :]
         for j, (real, imag) in enumerate(spread([load(q * inner + start) for q in range(HALF)])):
             if j > 0:
                 cosine, sine = turn[:, j : j + 1], turn[:, RADIX + j : RADIX + j + 1]
@@ -126,16 +133,17 @@
                 imag = jnp.zeros_like(real)
             for part, value in enumerate((real, imag)):
                 high, low = split_pair(value)
-                high_ref[j, rows, 128 * part : 128 * part + 128] = high
-                low_ref[j, rows, 128 * part : 128 * part + 128] = low
+                lanes = slice(128 * part, 128 * part + 128)
+                stage[j, pl.ds(start, CHUNK), lanes] = high
+                stage[j, pl.ds(inner + start, CHUNK), lanes] = high
+                stage[j, pl.ds(2 * inner + start, CHUNK), lanes] = low
         return carry
 
-    lax.fori_loop(0, inner // CHUNK, chunk, 0)
-
-
-def inner_dft(pair, matrix_high, matrix_low, inner, direction):
-    high, low = pair
-    product = dot_three((matrix_high[...], matrix_low[...]), (high, low))
+    lax.fori_loop(0, inner // CHUNK, chunk, 0, unroll=UNROLL_CHUNK)
+
+
+def inner_dft(stacked, matrix, inner, direction):
+    product = dot(matrix[...], stacked)
     cos_real, cos_imag = product[:inner, :128], product[:inner, 128:]
     sin_real, sin_imag = product[inner:, :128], product[inner:, 128:]
     if direction > 0:
@@ -151,22 +159,67 @@
     return pltpu.roll(value, 64, 1)
 
 
-def pack_kernel(tokens, cotan, out):
+def fetch(sources, buffers, semaphores):
+    copies = [
+        pltpu.make_async_copy(source, buffer, semaphores.at[index])
+        for index, (source, buffer) in enumerate(zip(sources, buffers))
+    ]
+    for copy in copies:
+        copy.start()
+    return copies
+
+
+def pack_kernel(tokens_hbm, cotan_hbm, out, tokens, cotan, semaphores):
+    for copy in fetch((tokens_hbm, cotan_hbm), (tokens, cotan), semaphores):
+        copy.wait()
     for block in range(out.shape[0]):
         lanes = slice(64 * block, 64 * block + 64)
         out[block] = jnp.concatenate([tokens[:, lanes], cotan[:, lanes]], axis=1)
 
 
+def diagonal(matrix):
+    empty = jnp.zeros_like(matrix)
+    return jnp.concatenate(
+        [jnp.concatenate([matrix, empty], axis=1), jnp.concatenate([empty, matrix], axis=1)], axis=0
+    )
+
+
+def twice(row):
+    return jnp.concatenate([row, row], axis=1)
+
+
+def exp_minus_one(value):
+    series = jnp.ones_like(value)
+    for order in range(9, 1, -1):
+        series = 1.0 + series * value * (1.0 / order)
+    return jnp.where(jnp.abs(value) < 0.35, value * series, jnp.exp(value) - 1.0)
+
+
 def kernel_spectrum_kernel(
-    length, rate, scale, w_first, w_bias, w_mid, w_last, matrix_high, matrix_low, twiddle,
+    length, rates, w_first, w_bias, w_mid, w_last, matrix, twiddle,
+    spectrum_hbm, env_hbm, slope_one_hbm, slope_two_hbm, one_high_hbm, one_low_hbm, two_high_hbm,
+    two_low_hbm, mid_back, last_back,
     spectrum, env_out, slope_one, slope_two, one_high, one_low, two_high, two_low,
-    taps, high_ref, low_ref,
+    taps, stage, semaphores,
 ):
-    padded = 2 * length
-    inner = padded // RADIX
+    inner = 2 * length // RADIX
     low_half = low_lanes(inner)
-    mid_pair = split_pair(w_mid[...])
-    last_pair = split_pair(w_last[...])
+    own = lax.axis_index("ctx")
+    lanes = pl.ds(pl.multiple_of(own // 2 * 128, 128), 128)
+    odd = own % 2 == 1
+    last = w_last[:, lanes]
+    last = diagonal(jnp.where(odd, swap(last), last)[:, 0:64])
+    rate = rates[:, lanes]
+    rate = twice(jnp.where(odd, swap(rate), rate)[:, 0:64])
+    double = 2.0 * rate
+    ratio = exp_minus_one(-double * (length - 1)) / exp_minus_one(-double)
+    geometric = 1.0 + 2.0 * jnp.exp(-double) * ratio
+    scale = lax.rsqrt(geometric)
+    mid = diagonal(w_mid[...])
+    mid_back[...] = tall_three(mid.T)
+    last_back[...] = tall_three(last.T)
+    mid, last = tall_three(mid), tall_three(last)
+    first, bias = twice(w_first[...]), twice(w_bias[...])
 
     def block(step, carry):
         start = pl.multiple_of(step * inner, inner)
@@ -174,53 +227,67 @@
         place = start + lax.broadcasted_iota(jnp.int32, (inner, 128), 0)
         lag = jnp.where(low_half, place, place - length)
         scaled = lag.astype(F32) / length
-        pre_one = scaled * w_first[...] + w_bias[...]
+        pre_one = scaled * first + bias
         gate_one = 1.0 / (1.0 + jnp.exp(-pre_one))
         hidden_one = pre_one * gate_one
         slope_one[rows, :] = gate_one * (1.0 + pre_one * (1.0 - gate_one))
-        pre_two = dot_three(split_pair(hidden_one), mid_pair)
+        pre_two = dot(wide_three(hidden_one), mid)
         gate_two = 1.0 / (1.0 + jnp.exp(-pre_two))
         hidden_two = pre_two * gate_two
         slope_two[rows, :] = gate_two * (1.0 + pre_two * (1.0 - gate_two))
-        position = dot_three(split_pair(hidden_two), last_pair)
+        position = dot(wide_three(hidden_two), last)
         live = jnp.where(lag == -length, 0.0, 1.0)
-        env = live * scale[...] * jnp.exp(-jnp.abs(lag).astype(F32) * rate[...])
+        env = live * scale * jnp.exp(-jnp.abs(lag).astype(F32) * rate)
         taps[rows, :] = (position * env).astype(BF16).astype(F32)
-        env_out[rows, 0:128] = jnp.where(low_half, 0.0, swap(env))
-        env_out[rows, 128:256] = jnp.where(low_half, 0.0, env)
+        env_out[rows, :] = env
         one_high[:, rows], one_low[:, rows] = split_pair(hidden_one.T)
         two_high[:, rows], two_low[:, rows] = split_pair(hidden_two.T)
         return carry
 
-    lax.fori_loop(0, HALF, block, 0)
-    residues_to_scratch(
-        lambda start: taps[pl.ds(start, CHUNK), :], twiddle, high_ref, low_ref, inner
-    )
+    lax.fori_loop(0, HALF, block, 0, unroll=UNROLL_ROWS)
+    copies = fetch(
+        (env_out, slope_one, slope_two, one_high, one_low, two_high, two_low),
+        (env_hbm, slope_one_hbm, slope_two_hbm, one_high_hbm, one_low_hbm, two_high_hbm, two_low_hbm),
+        semaphores,
+    )
+    residues_to_scratch(lambda start: taps[pl.ds(start, CHUNK), :], twiddle, stage, inner)
 
     def transform(j, carry):
-        real, imag = inner_dft((high_ref[j], low_ref[j]), matrix_high, matrix_low, inner, 1)
-        sign = (1 - 2 * (j % 2)).astype(F32)
+        real, imag = inner_dft(stage[j], matrix, inner, 1)
+        sign = 1.0 - 2.0 * lax.rem(jnp.asarray(j, jnp.int32), 2).astype(F32)
         spectrum[j, :, 0:128] = real + sign * swap(real)
         spectrum[j, :, 128:256] = imag + sign * swap(imag)
         return carry
 
-    lax.fori_loop(0, HALF + 1, transform, 0)
+    lax.fori_loop(0, HALF + 1, transform, 0, unroll=UNROLL_BIN)
+    last_copy = pltpu.make_async_copy(spectrum, spectrum_hbm, semaphores.at[len(copies)])
+    last_copy.start()
+    for copy in copies + [last_copy]:
+        copy.wait()
 
 
 def gradient_kernel(
-    length, signal, spectrum, env, slope_one, slope_two, one_high, one_low, two_high, two_low,
-    mid_back, last_back, matrix_high, matrix_low, twiddle, out, high_ref, low_ref, back_ref,
-    last_sum, mid_sum, first_sum,
+    length, signal, spectrum_hbm, env_hbm, slope_one_hbm, slope_two_hbm, one_high_hbm, one_low_hbm,
+    two_high_hbm, two_low_hbm, mid_back, last_back, matrix, twiddle, out,
+    spectrum, env, slope_one, slope_two, one_high, one_low, two_high, two_low, semaphores,
+    stage, back_ref, slope_high, slope_low, pre_high, pre_low,
 ):
     padded = 2 * length
     inner = padded // RADIX
     low_half = low_lanes(inner)
+    copies = fetch(
+        (spectrum_hbm, env_hbm, slope_one_hbm, slope_two_hbm, one_high_hbm, one_low_hbm,
+         two_high_hbm, two_low_hbm),
+        (spectrum, env, slope_one, slope_two, one_high, one_low, two_high, two_low),
+        semaphores,
+    )
     residues_to_scratch(
-        lambda start: signal[pl.ds(start, CHUNK), :].astype(F32), twiddle, high_ref, low_ref, inner
-    )
+        lambda start: signal[pl.ds(start, CHUNK), :].astype(F32), twiddle, stage, inner
+    )
+    copies[0].wait()
 
     def transform(j, carry):
-        real, imag = inner_dft((high_ref[j], low_ref[j]), matrix_high, matrix_low, inner, 1)
+        real, imag = inner_dft(stage[j], matrix, inner, 1)
         real_swap, imag_swap = swap(real), swap(imag)
         cotan_real = jnp.where(low_half, real_swap, real)
         cotan_imag = jnp.where(low_half, imag_swap, imag)
@@ -233,12 +300,13 @@
             ],
             axis=1,
         )
-        real, imag = inner_dft(split_pair(product), matrix_high, matrix_low, inner, -1)
+        real, imag = inner_dft(tall_three(product), matrix, inner, -1)
         back_ref[j, :, 0:128] = real
         back_ref[j, :, 128:256] = imag
         return carry
 
-    lax.fori_loop(0, HALF + 1, transform, 0)
+    lax.fori_loop(0, HALF + 1, transform, 0, unroll=UNROLL_BIN)
+    copies[1].wait()
 
     def unspread(step, carry):
         start = pl.multiple_of(step * CHUNK, CHUNK)
@@ -258,20 +326,21 @@
             imag_list.append(real * sine + imag * cosine)
         even, odd = gather_back(real_list, imag_list)
         for q in range(HALF):
-            back_ref[q, rows, 0:128] = even[q] + odd[q]
-            back_ref[q, rows, 128:256] = even[q] - odd[q]
+            joined, apart = even[q] + odd[q], even[q] - odd[q]
+            back_ref[q, rows, 0:128] = joined
+            at = pl.ds(q * inner + start, CHUNK)
+            lag_grad = jnp.where(low_lanes(CHUNK), swap(joined), apart)
+            slope_high[at, :], slope_low[at, :] = split_pair(lag_grad * env[at, :])
         return carry
 
-    lax.fori_loop(0, inner // CHUNK, unspread, 0)
-    last_sum[...] = jnp.zeros_like(last_sum)
-    mid_sum[...] = jnp.zeros_like(mid_sum)
-    first_sum[...] = jnp.zeros_like(first_sum)
-    mid_pair = split_pair(mid_back[...])
-    last_pair = split_pair(last_back[...])
+    lax.fori_loop(0, inner // CHUNK, unspread, 0, unroll=UNROLL_CHUNK)
+    for copy in copies[2:]:
+        copy.wait()
     local_rows = 128
     half_rows = local_rows // 2
 
     def block(q, carry):
+        first_sum, bias_sum = carry
         start = pl.multiple_of(q * inner, inner)
         rows = pl.ds(start, inner)
         for part in range(inner // local_rows):
@@ -281,27 +350,35 @@
             out[q * (inner // local_rows) + part, 0:half_rows, :] = jnp.where(
                 low_half[:half_rows], upper, swap(lower)
             ).astype(BF16)
-        slope = split_pair(back_ref[q] * env[rows, :])
-        last_sum[...] += dot_three((two_high[:, rows], two_low[:, rows]), slope)
-        pre_two = split_pair(dot_three(slope, last_pair) * slope_two[rows, :])
-        mid_sum[...] += dot_three((one_high[:, rows], one_low[:, rows]), pre_two)
-        pre_one = dot_three(pre_two, mid_pair) * slope_one[rows, :]
+        high, low = slope_high[rows, :], slope_low[rows, :]
+        slope = jnp.concatenate([high, low, high], axis=1)
+        high, low = split_pair(dot(slope, last_back[...]) * slope_two[rows, :])
+        pre_high[rows, :], pre_low[rows, :] = high, low
+        pre_two = jnp.concatenate([high, low, high], axis=1)
+        pre_one = dot(pre_two, mid_back[...]) * slope_one[rows, :]
         place = start + lax.broadcasted_iota(jnp.int32, (inner, 128), 0)
         scaled = jnp.where(low_half, place, place - length).astype(F32) / length
-        first_sum[0:8] += jnp.sum((pre_one * scaled).reshape(inner // 8, 8, 128), axis=0)
-        first_sum[8:16] += jnp.sum(pre_one.reshape(inner // 8, 8, 128), axis=0)
-        return carry
-
-    lax.fori_loop(0, HALF, block, 0)
+        first_sum = first_sum + jnp.sum((pre_one * scaled).reshape(inner // 8, 8, 128), axis=0)
+        bias_sum = bias_sum + jnp.sum(pre_one.reshape(inner // 8, 8, 128), axis=0)
+        return first_sum, bias_sum
+
+    none = jnp.zeros((8, 128), F32)
+    first_sum, bias_sum = lax.fori_loop(0, HALF, block, (none, none), unroll=UNROLL_ROWS)
+    last_sum = dot(two_high[...], slope_high[...]) + (
+        dot(two_low[...], slope_high[...]) + dot(two_high[...], slope_low[...])
+    )
+    mid_sum = dot(one_high[...], pre_high[...]) + (
+        dot(one_low[...], pre_high[...]) + dot(one_high[...], pre_low[...])
+    )
     low_64 = low_lanes(64)
     low_32 = low_lanes(32)
-    grad_last = swap(last_sum[0:64, 0:128]) + swap(last_sum[64:128, 128:256])
+    grad_last = last_sum[0:64] + swap(last_sum[64:128])
     pair = jnp.where(low_32, grad_last[0:32], swap(grad_last[32:64]))
     mid_total = mid_sum[0:64] + swap(mid_sum[64:128])
     mid_high = mid_total.astype(BF16).astype(F32)
     mid_rows = jnp.where(low_64, mid_high, swap(mid_total - mid_high))
-    first = jnp.sum(first_sum[0:8], axis=0, keepdims=True)
-    bias = jnp.sum(first_sum[8:16], axis=0, keepdims=True)
+    first = jnp.sum(first_sum, axis=0, keepdims=True)
+    bias = jnp.sum(bias_sum, axis=0, keepdims=True)
     first = first + swap(first)
     bias = bias + swap(bias)
     joined = jnp.where(low_lanes(1), first, bias)
@@ -310,36 +387,58 @@
     joined_rows = jnp.where(
         row_index == 0, joined_high, jnp.where(row_index == 1, joined - joined_high, 0.0)
     )
-    tail = jnp.concatenate([pair, mid_rows, joined_rows], axis=0).astype(BF16)
     for device in range(out.shape[0]):
-        out[device, half_rows:, :] = tail
-
-
-def unpack_kernel(loss_scale, received, grad_tokens, grad_first, grad_bias, grad_mid, grad_last):
-    devices = received.shape[0]
+        odd = device % 2
+        tail = [pair[16 * odd : 16 * odd + 16], mid_rows[32 * odd : 32 * odd + 32], joined_rows]
+        out[device, half_rows:, :] = jnp.concatenate(tail, axis=0).astype(BF16)
+
+
+def sums_kernel(received, half, joined_out):
+    half_rows = received.shape[1] - 64
+    mid = jnp.zeros((32, 128), F32)
+    joined = jnp.zeros((16, 128), F32)
+    for source in range(received.shape[0]):
+        lanes = slice(64 * source, 64 * source + 64)
+        last = received[source, half_rows : half_rows + 16, :]
+        half[0:16, lanes] = last[:, 0:64]
+        half[16:32, lanes] = last[:, 64:128]
+        mid = mid + received[source, half_rows + 16 : half_rows + 48, :].astype(F32)
+        joined = joined + received[source, half_rows + 48 : half_rows + 64, :].astype(F32)
+    mid = mid + swap(mid)
+    high = mid.astype(BF16).astype(F32)
+    columns = 64 * received.shape[0]
+    half[:, columns : columns + 128] = jnp.where(low_lanes(32), high, mid - high).astype(BF16)
+    joined_out[...] = joined
+
+
+def tokens_kernel(received, grad_tokens):
     half_rows = grad_tokens.shape[0] // 2
-    mid = jnp.zeros((64, 128), F32)
-    joined = jnp.zeros((16, 128), F32)
-    for source in range(devices):
+    for source in range(received.shape[0]):
         lanes = slice(64 * source, 64 * source + 64)
         tile = received[source, 0:half_rows, :]
         grad_tokens[0:half_rows, lanes] = tile[:, 0:64]
         grad_tokens[half_rows:, lanes] = tile[:, 64:128]
-        last = received[source, half_rows : half_rows + 32, :].astype(F32) * loss_scale
-        grad_last[0:32, lanes] = last[:, 0:64]
-        grad_last[32:64, lanes] = last[:, 64:128]
-        mid = mid + received[source, half_rows + 32 : half_rows + 96, :].astype(F32)
-        joined = joined + received[source, half_rows + 96 : half_rows + 112, :].astype(F32)
-    grad_mid[...] = ((mid + swap(mid)) * loss_scale)[:, 0:64]
+
+
+def weights_kernel(loss_scale, joined, mine, other, grad_first, grad_bias, grad_mid, grad_last):
+    odd = lax.rem(lax.axis_index("ctx"), 2)
+    columns = grad_last.shape[1]
+    for source, parity in ((mine, odd), (other, 1 - odd)):
+        last = source[:, 0:columns].astype(F32) * loss_scale
+        grad_last[pl.ds(pl.multiple_of(16 * parity, 16), 16), :] = last[0:16]
+        grad_last[pl.ds(pl.multiple_of(32 + 16 * parity, 16), 16), :] = last[16:32]
+        mid = source[:, columns : columns + 128].astype(F32) * loss_scale
+        grad_mid[pl.ds(pl.multiple_of(32 * parity, 32), 32), :] = (mid + swap(mid))[:, 0:64]
     first = (joined[0:1] + joined[1:2]) * loss_scale
     grad_first[...] = first[:, 0:64]
     grad_bias[...] = first[:, 64:128]
 
 
-def call(kernel, out_shape, scratch=(), flops=0, limit=24):
+def call(kernel, out_shape, scratch=(), flops=0, limit=24, **specs):
     return pl.pallas_call(
         kernel,
         out_shape=out_shape,
+        **specs,
         scratch_shapes=list(scratch),
         compiler_params=pltpu.CompilerParams(vmem_limit_bytes=limit << 20),
         cost_estimate=pl.CostEstimate(flops=flops, bytes_accessed=1 << 20, transcendentals=0),
@@ -350,88 +449,92 @@
     return jax.ShapeDtypeStruct(dims, dtype)
 
 
-def twice(value):
-    return jnp.concatenate([value, value]).reshape(1, -1)
-
-
-def diagonal(matrix):
-    empty = jnp.zeros_like(matrix)
-    return jnp.block([[matrix, empty], [empty, matrix]])
+ON_HBM = pl.BlockSpec(memory_space=pltpu.HBM)
+ON_VMEM = pl.BlockSpec(memory_space=pltpu.VMEM)
+
+
+def passed_arrays(length):
+    inner = 2 * length // RADIX
+    return [
+        ((HALF + 1, inner, 256), F32),
+        ((length, 128), F32),
+        ((length, 128), F32),
+        ((length, 128), F32),
+    ] + [((128, length), BF16)] * 4
+
+
+def held_arrays(length):
+    passed = passed_arrays(length)
+    return [pltpu.VMEM(*one) for one in passed], pltpu.SemaphoreType.DMA((len(passed),))
+
+
+def spectrum_call(length, *operands):
+    inner = 2 * length // RADIX
+    passed = passed_arrays(length)
+    held, semaphores = held_arrays(length)
+    return call(
+        functools.partial(kernel_spectrum_kernel, length),
+        [shape(*one) for one in passed] + [shape((384, 128), BF16)] * 2,
+        scratch=held
+        + [
+            pltpu.VMEM((length, 128), F32),
+            pltpu.VMEM((HALF + 1, 3 * inner, 256), BF16),
+            semaphores,
+        ],
+        flops=4 << 30,
+        limit=58,
+        out_specs=[ON_HBM] * len(passed) + [ON_VMEM] * 2,
+    )(*operands)
+
+
+def gradient_call(length, signal, *operands):
+    inner = 2 * length // RADIX
+    held, semaphores = held_arrays(length)
+    local_rows = 128
+    return call(
+        functools.partial(gradient_kernel, length),
+        shape((length // local_rows, local_rows // 2 + 64, 128), BF16),
+        scratch=held
+        + [
+            semaphores,
+            pltpu.VMEM((HALF + 1, 3 * inner, 256), BF16),
+            pltpu.VMEM((HALF + 1, inner, 256), F32),
+        ]
+        + [pltpu.VMEM((length, 128), BF16)] * 4,
+        flops=8 << 30,
+        limit=58,
+        in_specs=[ON_VMEM] + [ON_HBM] * len(held) + [ON_VMEM] * 4,
+    )(signal, *operands)
 
 
 def by_channels(tokens_in, grad_out, decay_rate, w_in, b_in, w_mid, w_out):
     devices = lax.axis_size("ctx")
-    own_index = lax.axis_index("ctx")
     local_rows = tokens_in.shape[0]
     length = local_rows * devices
-    padded = 2 * length
-    inner = padded // RADIX
-    bins = HALF + 1
-    matrix_high, matrix_low, twiddle = dft_tables(padded)
-    packed = call(pack_kernel, shape((devices, local_rows, 128), BF16))(tokens_in, grad_out)
+    matrix, twiddle = dft_tables(2 * length)
+    packed = call(
+        pack_kernel,
+        shape((devices, local_rows, 128), BF16),
+        scratch=[pltpu.VMEM(tokens_in.shape, BF16)] * 2 + [pltpu.SemaphoreType.DMA((2,))],
+        limit=58,
+        in_specs=[ON_HBM] * 2,
+    )(tokens_in, grad_out)
     signal = lax.all_to_all(packed, "ctx", split_axis=0, concat_axis=0, tiled=True)
-    signal = signal.reshape(length, 128)
-
-    own_last = lax.dynamic_slice_in_dim(w_out, own_index * 64, 64, axis=1)
-    own_rate = lax.dynamic_slice_in_dim(decay_rate, own_index * 64, 64, axis=0)
-    double = 2.0 * own_rate
-    geometric = 1.0 + 2.0 * jnp.exp(-double) * jnp.expm1(-double * (length - 1)) / jnp.expm1(
-        -double
-    )
-    stage = [pltpu.VMEM((bins, inner, 256), BF16)] * 2
-    (spectrum, env, slope_one, slope_two, one_high, one_low, two_high, two_low) = call(
-        functools.partial(kernel_spectrum_kernel, length),
-        [
-            shape((bins, inner, 256), F32),
-            shape((length, 256), F32),
-            shape((length, 128), F32),
-            shape((length, 128), F32),
-        ]
-        + [shape((128, length), BF16)] * 4,
-        scratch=[pltpu.VMEM((length, 128), F32)] + stage,
-        flops=4 << 30,
-    )(
-        twice(own_rate),
-        twice(lax.rsqrt(geometric)),
-        twice(w_in),
-        twice(b_in),
-        diagonal(w_mid),
-        diagonal(own_last),
-        matrix_high,
-        matrix_low,
-        twiddle,
-    )
-    empty = jnp.zeros((64, 64), F32)
-    last_back = jnp.block(
-        [[empty, empty], [own_last.T, empty], [empty, empty], [empty, own_last.T]]
-    )
-    sent_rows = local_rows // 2 + 32 + 64 + 16
-    sent = call(
-        functools.partial(gradient_kernel, length),
-        shape((devices, sent_rows, 128), BF16),
-        scratch=stage
-        + [
-            pltpu.VMEM((bins, inner, 256), F32),
-            pltpu.VMEM((128, 256), F32),
-            pltpu.VMEM((128, 128), F32),
-            pltpu.VMEM((16, 128), F32),
-        ],
-        flops=8 << 30,
-    )(
-        signal, spectrum, env, slope_one, slope_two, one_high, one_low, two_high, two_low,
-        diagonal(w_mid.T), last_back, matrix_high, matrix_low, twiddle,
-    )
+    forward = spectrum_call(
+        length, decay_rate.reshape(1, -1), w_in.reshape(1, -1), b_in.reshape(1, -1), w_mid, w_out,
+        matrix, twiddle,
+    )
+    sent = gradient_call(length, signal.reshape(length, 128), *forward, matrix, twiddle)
     received = lax.all_to_all(sent, "ctx", split_axis=0, concat_axis=0, tiled=True)
-    input_grad, grad_first, grad_bias, grad_mid, grad_last = call(
-        functools.partial(unpack_kernel, 1.0 / math.sqrt(length)),
-        [
-            shape(tokens_in.shape, BF16),
-            shape((1, 64), F32),
-            shape((1, 64), F32),
-            shape((64, 64), F32),
-            shape(w_out.shape, F32),
-        ],
+    half, joined = call(
+        sums_kernel, [shape((32, 64 * devices + 128), BF16), shape((16, 128), F32)]
     )(received)
+    other = lax.ppermute(half, "ctx", [(index, index ^ 1) for index in range(devices)])
+    input_grad = call(tokens_kernel, shape(tokens_in.shape, BF16), flops=1 << 26)(received)
+    grad_first, grad_bias, grad_mid, grad_last = call(
+        functools.partial(weights_kernel, 1.0 / math.sqrt(length)),
+        [shape((1, 64), F32), shape((1, 64), F32), shape((64, 64), F32), shape(w_out.shape, F32)],
+    )(joined, half, other)
     return input_grad, grad_first.reshape(64), grad_bias.reshape(64), grad_mid, grad_last
 
 
@@ -609,6 +712,7 @@
     devices = lax.axis_size("ctx")
     fits = (
         tokens_in.shape == (128, 64 * devices)
+        and devices % 2 == 0
         and devices * 128 % (128 * HALF) == 0
         and w_mid.shape == (64, 64)
     )

time: 81.5 us -> 66.9 us (0.82)
  local copies, waits for them, and re-layouts: 16.1 us -> 0.79 us
  blocking collectives: 24.9 us -> 18.6 us
  Pallas kernels: 30.3 us -> 36.4 us
  waiting for transfers between devices: 0.01 us -> 2.65 us
  other arithmetic: 1.26 us -> 0 us
    unnamed x44 -> x2, local copies, waits for them, and re-layouts: 15.9 us -> 0.79 us
    all_to_all x1, blocking collectives: 24.9 us -> 18.6 us  [by_channels(): lax.all_to_all(sent, 'ctx', split_axis=0, concat_axis=0, tiled=True)]
    pallas_call x4 -> x6, Pallas kernels: 30.3 us -> 36.4 us  [the longest x1 20.4 us: gradient_call(): call(functools.partial(gradient_kernel, length), shape((length // local_r...]
    all_to_all x1, waiting for transfers between devices: 0.01 us -> 2.31 us  [by_channels(): lax.all_to_all(packed, 'ctx', split_axis=0, concat_axis=0, tiled=True)]
  transfers between devices with their start and end apart: 1 -> 2, of which waited for: 0 -> 2; matrix products, arithmetic and copies ran while one was open for 2% -> 0% of each run, Pallas kernels for 12% -> 20%
where the time goes in v2:
time: 66.9 us; the launch traced here: 66.5 us
  Pallas kernels  36.4 us (54%)
  blocking collectives  18.6 us (28%)
  starting transfers between devices  7.45 us (11%)
  waiting for transfers between devices  2.65 us (4%)
  local copies, waits for them, and re-layouts  0.79 us (1%)
  between operations  0.67 us (1%)
    pallas_call x1, Pallas kernels, gradient_call(): call(functools.partial(gradient_kernel, length), shape((length // local_r...  20.4 us
    all_to_all x1, blocking collectives, by_channels(): lax.all_to_all(sent, 'ctx', split_axis=0, concat_axis=0, tiled=True)  18.6 us
    pallas_call x1, Pallas kernels, spectrum_call(): call(functools.partial(kernel_spectrum_kernel, length), [shape(*one) for...  12.2 us
    all_to_all x1, starting transfers between devices, by_channels(): lax.all_to_all(packed, 'ctx', split_axis=0, concat_axis=0, tiled=True)  7.37 us
    all_to_all x1, waiting for transfers between devices, by_channels(): lax.all_to_all(packed, 'ctx', split_axis=0, concat_axis=0, tiled=True)  2.31 us
    pallas_call x1, Pallas kernels, by_channels(): call(pack_kernel, shape((devices, local_rows, 128), BF16), scratch=[pltpu...  2.04 us
  transfers between devices with their start and end apart: 2, of which 2 were waited for; matrix products, arithmetic and copies ran while one was open for 0% of the time, Pallas kernels for 20%

profile of v2, /device:TPU:0, one launch (start us, length us, event | category | flops | bytes accessed | tf_op | source)
XLA Modules:
  0.0 66.5 jit_solution(3422445473543101944)
XLA Ops:
  0.6 2.0 %shard_map.128 = bf16[16,128,128]{2,1,0:T(8,128)(2,1)} custom-call(bf16[128,1024]{1,0:T(8,128)(2,1)} %tokens_hbm.1, bf16[128,1024]{1,0:T(8,128)(2,1)} %cotan_hbm.1), custom_call_target="tpu_custom_call" | custom-call | bytes 1048576 | tf_op jit(solution)/shard_map/pallas_call | solution.py:515
  2.7 7.4 %all-to-all-start = ((bf16[16,128,128]{2,1,0:T(8,128)(2,1)}), bf16[16,128,128]{2,1,0:T(8,128)(2,1)S(1)}, u32[]{:S(2)}, u32[]{:S(2)}) async-start(bf16[16,128,128]{2,1,0:T(8,128)(2,1)} %shard_map.128), calls=%async_computation | async-start | bytes 1048576 | tf_op jit(solution)/shard_map/all_to_all | solution.py:522
  10.1 12.2 %shard_map.129 = (f32[9,256,256]{2,1,0:T(8,128)}, f32[2048,128]{1,0:T(8,128)}, f32[2048,128]{1,0:T(8,128)}, f32[2048,128]{1,0:T(8,128)}, bf16[128,2048]{1,0:T(8,...) custom-call(f32[1,1024]{1,0:T(1,128)} %bitcast.7, ...), custom_call_target="tpu_custom_call" | custom-call | flops 4294967296 | bytes 1048576 | tf_op jit(solution)/shard_map/pallas_call | solution.py:475
  22.2 2.3 %all-to-all-done = bf16[16,128,128]{2,1,0:T(8,128)(2,1)S(1)} async-done(((bf16[16,128,128]{2,1,0:T(8,128)(2,1)}), bf16[16,128,128]{2,1,0:T(8,128)(2,1)S(1)}, u32[]{:S(2)}, u32[]{:S(2)}) %all-to-all-start) | async-done | bytes 524320 | tf_op jit(solution)/shard_map/all_to_all | solution.py:522
  24.5 0.0 copy-start
  24.5 0.8 %copy-done = bf16[16,128,128]{2,1,0:T(8,128)(2,1)} copy-done((bf16[16,128,128]{2,1,0:T(8,128)(2,1)}, bf16[16,128,128]{2,1,0:T(8,128)(2,1)S(1)}, u32[]{:S(2)}) %copy-start) | copy-done | bytes 524312
  25.3 20.4 %shard_map.130 = bf16[16,128,128]{2,1,0:T(8,128)(2,1)} custom-call(bf16[2048,128]{1,0:T(8,128)(2,1)} %bitcast.6, f32[9,256,256]{2,1,0:T(8,128)} %get-tuple-element.21.spectrum_hbm, f32[2048,128]{1,0:T(8,128)} %get-tuple-element.22.env_hbm, f32[2048,128]{1,0:T(8,128)} %get-tuple-element.23.slope_one_hbm, f32[2048,128]{1,0:T(8,128)} %get-tuple-element.24.slope_two_hbm, ...), custom_call_target="tpu_custom_call" | custom-call | flops 8589934592 | bytes 1048576 | tf_op jit(solution)/shard_map/pallas_call | solution.py:494
  45.8 18.6 %all_to_all.10.received = bf16[16,128,128]{2,1,0:T(8,128)(2,1)S(1)} all-to-all(bf16[16,128,128]{2,1,0:T(8,128)(2,1)} %shard_map.130), channel_id=1, replica_groups=mesh['groups'=2,'ctx'=16] {'ctx'}, dimensions={0} | all-to-all | bytes 1048576 | tf_op jit(solution)/shard_map/all_to_all | solution.py:528
  64.3 0.1 shard_map.132
  64.5 0.1 collective-permute-start
  64.5 0.9 %shard_map.131 = bf16[128,1024]{1,0:T(8,128)(2,1)} custom-call(bf16[16,128,128]{2,1,0:T(8,128)(2,1)S(1)} %all_to_all.10.received), custom_call_target="tpu_custom_call" | custom-call | flops 67108864 | bytes 1048576 | tf_op jit(solution)/shard_map/pallas_call | solution.py:533
  65.4 0.3 collective-permute-done.other
  65.8 0.7 %shard_map.133 = (f32[1,64]{1,0:T(1,128)}, f32[1,64]{1,0:T(1,128)}, f32[64,64]{1,0:T(8,128)}, f32[64,1024]{1,0:T(8,128)}) custom-call(f32[16,128]{1,0:T(8,128)S(1)} %get-tuple-element.31.joined, bf16[32,1152]{1,0:T(8,128)(2,1)S(1)} %get-tuple-element.32.mine, bf16[32,1152]{1,0:T(8,128)(2,1)S(1)} %collective-permute-done.other), custom_call_target="tpu_custom_call" | custom-call | bytes 1048576 | tf_op jit(solution)/shard_map/pallas_call | solution.py:534
Async XLA Ops:
  2.7 21.8 %all-to-all-start = ((bf16[16,128,128]{2,1,0:T(8,128)(2,1)}), bf16[16,128,128]{2,1,0:T(8,128)(2,1)S(1)}, u32[]{:S(2)}, u32[]{:S(2)}) async-start(bf16[16,128,128]{2,1,0:T(8,128)(2,1)} %shard_map.128), calls=%async_computation | async-start | bytes 1048576 | tf_op jit(solution)/shard_map/all_to_all | solution.py:522
  24.5 0.8 %copy-start = (bf16[16,128,128]{2,1,0:T(8,128)(2,1)}, bf16[16,128,128]{2,1,0:T(8,128)(2,1)S(1)}, u32[]{:S(2)}) copy-start(bf16[16,128,128]{2,1,0:T(8,128)(2,1)S(1)} %all-to-all-done) | copy-start | bytes 1572868
  64.5 1.3 %collective-permute-start = (bf16[32,1152]{1,0:T(8,128)(2,1)S(1)}, bf16[32,1152]{1,0:T(8,128)(2,1)S(1)}, u32[]{:S(2)}, u32[]{:S(2)}) collective-permute-start(bf16[32,1152]{1,0:T(8,128)(2,1)S(1)} %get-tuple-element.32.mine), channel_id=1, source_target_pairs={{0,1},{1,0},{2,3},{3,2},{4,5},{5,4},{6,7},{7,6},{8,9},{9,8},{10,11... | collective-permute-start | bytes 221192 | tf_op jit(solution)/shard_map/ppermute | solution.py:532

commit v3 on v2

--- a/solution.py
+++ b/solution.py
@@ -12,9 +12,11 @@
 RADIX = 16
 HALF = RADIX // 2
 CHUNK = 32
-UNROLL_CHUNK = 1
-UNROLL_BIN = 1
-UNROLL_ROWS = 1
+UNROLL_CHUNK = 8
+UNROLL_BIN = 9
+UNROLL_ROWS = 8
+FIRST_LIMIT = 56
+SECOND_LIMIT = 50
 F32 = jnp.float32
 BF16 = jnp.bfloat16
 
@@ -196,11 +198,9 @@
 
 
 def kernel_spectrum_kernel(
-    length, rates, w_first, w_bias, w_mid, w_last, matrix, twiddle,
-    spectrum_hbm, env_hbm, slope_one_hbm, slope_two_hbm, one_high_hbm, one_low_hbm, two_high_hbm,
-    two_low_hbm, mid_back, last_back,
-    spectrum, env_out, slope_one, slope_two, one_high, one_low, two_high, two_low,
-    taps, stage, semaphores,
+    length, rates, w_first, w_bias, w_mid, w_last, matrix, twiddle, wide_hbm, narrow_hbm,
+    spectrum, env_out, slope_one, slope_two, one_high, one_low, two_high, two_low, mid_back,
+    last_back, semaphores, taps, stage,
 ):
     inner = 2 * length // RADIX
     low_half = low_lanes(inner)
@@ -245,42 +245,35 @@
         return carry
 
     lax.fori_loop(0, HALF, block, 0, unroll=UNROLL_ROWS)
-    copies = fetch(
-        (env_out, slope_one, slope_two, one_high, one_low, two_high, two_low),
-        (env_hbm, slope_one_hbm, slope_two_hbm, one_high_hbm, one_low_hbm, two_high_hbm, two_low_hbm),
-        semaphores,
-    )
+    places = passed_places(length, wide_hbm, narrow_hbm)
+    held = (env_out, slope_one, slope_two, one_high, one_low, two_high, two_low, mid_back, last_back)
+    copies = fetch(held, places[1:], semaphores)
     residues_to_scratch(lambda start: taps[pl.ds(start, CHUNK), :], twiddle, stage, inner)
 
     def transform(j, carry):
         real, imag = inner_dft(stage[j], matrix, inner, 1)
         sign = 1.0 - 2.0 * lax.rem(jnp.asarray(j, jnp.int32), 2).astype(F32)
-        spectrum[j, :, 0:128] = real + sign * swap(real)
-        spectrum[j, :, 128:256] = imag + sign * swap(imag)
+        spectrum[pl.ds((2 * j + 0) * inner, inner), :] = real + sign * swap(real)
+        spectrum[pl.ds((2 * j + 1) * inner, inner), :] = imag + sign * swap(imag)
         return carry
 
     lax.fori_loop(0, HALF + 1, transform, 0, unroll=UNROLL_BIN)
-    last_copy = pltpu.make_async_copy(spectrum, spectrum_hbm, semaphores.at[len(copies)])
+    last_copy = pltpu.make_async_copy(spectrum, places[0], semaphores.at[len(copies)])
     last_copy.start()
     for copy in copies + [last_copy]:
         copy.wait()
 
 
 def gradient_kernel(
-    length, signal, spectrum_hbm, env_hbm, slope_one_hbm, slope_two_hbm, one_high_hbm, one_low_hbm,
-    two_high_hbm, two_low_hbm, mid_back, last_back, matrix, twiddle, out,
-    spectrum, env, slope_one, slope_two, one_high, one_low, two_high, two_low, semaphores,
-    stage, back_ref, slope_high, slope_low, pre_high, pre_low,
+    length, signal, wide_hbm, narrow_hbm, matrix, twiddle, out,
+    spectrum, env, slope_one, slope_two, one_high, one_low, two_high, two_low, mid_back, last_back,
+    semaphores, stage, back_ref, slope_high, slope_low, pre_high, pre_low,
 ):
     padded = 2 * length
     inner = padded // RADIX
     low_half = low_lanes(inner)
-    copies = fetch(
-        (spectrum_hbm, env_hbm, slope_one_hbm, slope_two_hbm, one_high_hbm, one_low_hbm,
-         two_high_hbm, two_low_hbm),
-        (spectrum, env, slope_one, slope_two, one_high, one_low, two_high, two_low),
-        semaphores,
-    )
+    held = (spectrum, env, slope_one, slope_two, one_high, one_low, two_high, two_low, mid_back, last_back)
+    copies = fetch(passed_places(length, wide_hbm, narrow_hbm), held, semaphores)
     residues_to_scratch(
         lambda start: signal[pl.ds(start, CHUNK), :].astype(F32), twiddle, stage, inner
     )
@@ -291,8 +284,8 @@
         real_swap, imag_swap = swap(real), swap(imag)
         cotan_real = jnp.where(low_half, real_swap, real)
         cotan_imag = jnp.where(low_half, imag_swap, imag)
-        other_real = jnp.where(low_half, spectrum[j, :, 0:128], real_swap)
-        other_imag = jnp.where(low_half, spectrum[j, :, 128:256], imag_swap)
+        other_real = jnp.where(low_half, spectrum[pl.ds((2 * j + 0) * inner, inner), :], real_swap)
+        other_imag = jnp.where(low_half, spectrum[pl.ds((2 * j + 1) * inner, inner), :], imag_swap)
         product = jnp.concatenate(
             [
                 cotan_real * other_real + cotan_imag * other_imag,
@@ -453,58 +446,55 @@
 ON_VMEM = pl.BlockSpec(memory_space=pltpu.VMEM)
 
 
-def passed_arrays(length):
-    inner = 2 * length // RADIX
-    return [
-        ((HALF + 1, inner, 256), F32),
-        ((length, 128), F32),
-        ((length, 128), F32),
-        ((length, 128), F32),
-    ] + [((128, length), BF16)] * 4
+def passed_places(length, wide, narrow):
+    bins = 2 * (HALF + 1) * (2 * length // RADIX)
+    parts = [wide.at[pl.ds(0, bins), :]]
+    parts += [wide.at[pl.ds(bins + index * length, length), :] for index in range(3)]
+    parts += [narrow.at[pl.ds(128 * index, 128), :] for index in range(4)]
+    return parts + [narrow.at[pl.ds(512, 384), pl.ds(128 * index, 128)] for index in range(2)]
+
+
+def passed_shapes(length):
+    bins = 2 * (HALF + 1) * (2 * length // RADIX)
+    return [shape((bins + 3 * length, 128), F32), shape((512 + 384, length), BF16)]
 
 
 def held_arrays(length):
-    passed = passed_arrays(length)
-    return [pltpu.VMEM(*one) for one in passed], pltpu.SemaphoreType.DMA((len(passed),))
+    bins = 2 * (HALF + 1) * (2 * length // RADIX)
+    held = [pltpu.VMEM((bins, 128), F32)] + [pltpu.VMEM((length, 128), F32)] * 3
+    held += [pltpu.VMEM((128, length), BF16)] * 4 + [pltpu.VMEM((384, 128), BF16)] * 2
+    return held + [pltpu.SemaphoreType.DMA((len(held),))]
 
 
 def spectrum_call(length, *operands):
     inner = 2 * length // RADIX
-    passed = passed_arrays(length)
-    held, semaphores = held_arrays(length)
     return call(
         functools.partial(kernel_spectrum_kernel, length),
-        [shape(*one) for one in passed] + [shape((384, 128), BF16)] * 2,
-        scratch=held
-        + [
-            pltpu.VMEM((length, 128), F32),
-            pltpu.VMEM((HALF + 1, 3 * inner, 256), BF16),
-            semaphores,
-        ],
+        passed_shapes(length),
+        scratch=held_arrays(length)
+        + [pltpu.VMEM((length, 128), F32), pltpu.VMEM((HALF + 1, 3 * inner, 256), BF16)],
         flops=4 << 30,
-        limit=58,
-        out_specs=[ON_HBM] * len(passed) + [ON_VMEM] * 2,
+        limit=FIRST_LIMIT,
+        out_specs=[ON_HBM] * 2,
     )(*operands)
 
 
-def gradient_call(length, signal, *operands):
+def gradient_call(length, *operands):
     inner = 2 * length // RADIX
-    held, semaphores = held_arrays(length)
     local_rows = 128
     return call(
         functools.partial(gradient_kernel, length),
         shape((length // local_rows, local_rows // 2 + 64, 128), BF16),
-        scratch=held
+        scratch=held_arrays(length)
         + [
-            semaphores,
             pltpu.VMEM((HALF + 1, 3 * inner, 256), BF16),
             pltpu.VMEM((HALF + 1, inner, 256), F32),
         ]
         + [pltpu.VMEM((length, 128), BF16)] * 4,
         flops=8 << 30,
-        limit=58,
-        in_specs=[ON_VMEM] + [ON_HBM] * len(held) + [ON_VMEM] * 4,
-    )(signal, *operands)
+        limit=SECOND_LIMIT,
+        in_specs=[ON_VMEM] + [ON_HBM] * 2 + [ON_VMEM] * 2,
+    )(*operands)
 
 
 def by_channels(tokens_in, grad_out, decay_rate, w_in, b_in, w_mid, w_out):

time: 66.9 us -> 57 us (0.85)
  Pallas kernels: 36.4 us -> 23.5 us
  waiting for transfers between devices: 2.65 us -> 6.66 us
  local copies, waits for them, and re-layouts: 0.79 us -> 0.01 us
    pallas_call x1, Pallas kernels: 20.4 us -> 11.6 us  [gradient_call(): call(functools.partial(gradient_kernel, length), shape((length // local_r...]
    pallas_call x1, Pallas kernels: 12.2 us -> 8.11 us  [spectrum_call(): call(functools.partial(kernel_spectrum_kernel, length), passed_shapes(len...]
    all_to_all x1, waiting for transfers between devices: 2.31 us -> 6.32 us  [by_channels(): lax.all_to_all(packed, 'ctx', split_axis=0, concat_axis=0, tiled=True)]
    unnamed x2 -> x4, local copies, waits for them, and re-layouts: 0.79 us -> 0.01 us
  transfers between devices with their start and end apart: 2 -> 2, of which waited for: 2 -> 2; matrix products, arithmetic and copies ran while one was open for 0% -> 0% of each run, Pallas kernels for 20% -> 16%
where the time goes in v3:
time: 57 us; the launch traced here: 56.7 us
  Pallas kernels  23.5 us (41%)
  blocking collectives  18.4 us (32%)
  starting transfers between devices  7.45 us (13%)
  waiting for transfers between devices  6.66 us (12%)
  between operations  0.68 us (1%)
    all_to_all x1, blocking collectives, by_channels(): lax.all_to_all(sent, 'ctx', split_axis=0, concat_axis=0, tiled=True)  18.4 us
    pallas_call x1, Pallas kernels, gradient_call(): call(functools.partial(gradient_kernel, length), shape((length // local_r...  11.6 us
    pallas_call x1, Pallas kernels, spectrum_call(): call(functools.partial(kernel_spectrum_kernel, length), passed_shapes(len...  8.11 us
    all_to_all x1, starting transfers between devices, by_channels(): lax.all_to_all(packed, 'ctx', split_axis=0, concat_axis=0, tiled=True)  7.37 us
    all_to_all x1, waiting for transfers between devices, by_channels(): lax.all_to_all(packed, 'ctx', split_axis=0, concat_axis=0, tiled=True)  6.32 us
    pallas_call x1, Pallas kernels, by_channels(): call(pack_kernel, shape((devices, local_rows, 128), BF16), scratch=[pltpu...  2.05 us
  transfers between devices with their start and end apart: 2, of which 2 were waited for; matrix products, arithmetic and copies ran while one was open for 0% of the time, Pallas kernels for 16%

profile of v3, /device:TPU:0, one launch (start us, length us, event | category | flops | bytes accessed | tf_op | source)
XLA Modules:
  0.0 56.7 jit_solution(12584661737292456544)
XLA Ops:
  0.6 2.0 %shard_map.128 = bf16[16,128,128]{2,1,0:T(8,128)(2,1)} custom-call(bf16[128,1024]{1,0:T(8,128)(2,1)} %tokens_hbm.1, bf16[128,1024]{1,0:T(8,128)(2,1)} %cotan_hbm.1), custom_call_target="tpu_custom_call" | custom-call | bytes 1048576 | tf_op jit(solution)/shard_map/pallas_call | solution.py:505
  2.7 7.4 %all-to-all-start = ((bf16[16,128,128]{2,1,0:T(8,128)(2,1)}), bf16[16,128,128]{2,1,0:T(8,128)(2,1)S(1)}, u32[]{:S(2)}, u32[]{:S(2)}) async-start(bf16[16,128,128]{2,1,0:T(8,128)(2,1)} %shard_map.128), calls=%async_computation | async-start | bytes 1048576 | tf_op jit(solution)/shard_map/all_to_all | solution.py:512
  10.1 0.0 copy-start
  10.1 0.0 copy-start.1
  10.1 8.1 %shard_map.129 = (f32[10752,128]{1,0:T(8,128)}, bf16[896,2048]{1,0:T(8,128)(2,1)}) custom-call(f32[1,1024]{1,0:T(1,128)} %bitcast.7, f32[1,64]{1,0:T(1,128)} %bitcast.8, f32[1,64]{1,0:T(1,128)} %bitcast.9, f32[64,64]{1,0:T(8,128)} %w_mid.1, f32[64,1024]{1,0:T(8,128)} %w_last.1, bf16[512,768]{1,0:T(8,128)(2,1)} %constant.4.clone.matrix, ...), custom_call_target="tpu_custom_call" | custom-call | flops 4294967296 | bytes 1048576 | tf_op jit(solution)/shard_map/pallas_call | solution.py:471
  18.2 6.3 %all-to-all-done = bf16[16,128,128]{2,1,0:T(8,128)(2,1)S(1)} async-done(((bf16[16,128,128]{2,1,0:T(8,128)(2,1)}), bf16[16,128,128]{2,1,0:T(8,128)(2,1)S(1)}, u32[]{:S(2)}, u32[]{:S(2)}) %all-to-all-start) | async-done | bytes 524320 | tf_op jit(solution)/shard_map/all_to_all | solution.py:512
  24.5 0.0 copy-done
  24.5 0.0 copy-done.1
  24.5 11.6 %shard_map.130 = bf16[16,128,128]{2,1,0:T(8,128)(2,1)S(1)} custom-call(bf16[2048,128]{1,0:T(8,128)(2,1)S(1)} %bitcast.6, f32[10752,128]{1,0:T(8,128)} %get-tuple-element.13.wide_hbm, bf16[896,2048]{1,0:T(8,128)(2,1)} %get-tuple-element.14.narrow_hbm, bf16[512,768]{1,0:T(8,128)(2,1)S(1)} %copy-done, f32[256,128]{1,0:T(8,128)S(1)} %copy-done.1), custom_call_target="tpu_custom_call" | custom-call | flops 8589934592 | bytes 1048576 | tf_op jit(solution)/shard_map/pallas_call | solution.py:485
  36.1 18.4 %all_to_all.10.received = bf16[16,128,128]{2,1,0:T(8,128)(2,1)S(1)} all-to-all(bf16[16,128,128]{2,1,0:T(8,128)(2,1)S(1)} %shard_map.130), channel_id=1, replica_groups=mesh['groups'=2,'ctx'=16] {'ctx'}, dimensions={0} | all-to-all | bytes 1048576 | tf_op jit(solution)/shard_map/all_to_all | solution.py:518
  54.5 0.1 shard_map.132
  54.6 0.1 collective-permute-start
  54.7 0.9 %shard_map.131 = bf16[128,1024]{1,0:T(8,128)(2,1)} custom-call(bf16[16,128,128]{2,1,0:T(8,128)(2,1)S(1)} %all_to_all.10.received), custom_call_target="tpu_custom_call" | custom-call | flops 67108864 | bytes 1048576 | tf_op jit(solution)/shard_map/pallas_call | solution.py:523
  55.6 0.3 collective-permute-done.other
  55.9 0.7 %shard_map.133 = (f32[1,64]{1,0:T(1,128)}, f32[1,64]{1,0:T(1,128)}, f32[64,64]{1,0:T(8,128)}, f32[64,1024]{1,0:T(8,128)}) custom-call(f32[16,128]{1,0:T(8,128)S(1)} %get-tuple-element.15.joined, bf16[32,1152]{1,0:T(8,128)(2,1)S(1)} %get-tuple-element.16.mine, bf16[32,1152]{1,0:T(8,128)(2,1)S(1)} %collective-permute-done.other), custom_call_target="tpu_custom_call" | custom-call | bytes 1048576 | tf_op jit(solution)/shard_map/pallas_call | solution.py:524
Async XLA Ops:
  2.7 21.8 %all-to-all-start = ((bf16[16,128,128]{2,1,0:T(8,128)(2,1)}), bf16[16,128,128]{2,1,0:T(8,128)(2,1)S(1)}, u32[]{:S(2)}, u32[]{:S(2)}) async-start(bf16[16,128,128]{2,1,0:T(8,128)(2,1)} %shard_map.128), calls=%async_computation | async-start | bytes 1048576 | tf_op jit(solution)/shard_map/all_to_all | solution.py:512
  10.1 14.5 %copy-start = (bf16[512,768]{1,0:T(8,128)(2,1)S(1)}, bf16[512,768]{1,0:T(8,128)(2,1)}, u32[]{:S(2)}) copy-start(bf16[512,768]{1,0:T(8,128)(2,1)} %constant.4.clone.matrix) | copy-start | bytes 2359300
  10.1 14.5 %copy-start.1 = (f32[256,128]{1,0:T(8,128)S(1)}, f32[256,128]{1,0:T(8,128)}, u32[]{:S(2)}) copy-start(f32[256,128]{1,0:T(8,128)} %constant.5.clone.twiddle) | copy-start | bytes 393220
  54.6 1.3 %collective-permute-start = (bf16[32,1152]{1,0:T(8,128)(2,1)S(1)}, bf16[32,1152]{1,0:T(8,128)(2,1)S(1)}, u32[]{:S(2)}, u32[]{:S(2)}) collective-permute-start(bf16[32,1152]{1,0:T(8,128)(2,1)S(1)} %get-tuple-element.16.mine), channel_id=1, source_target_pairs={{0,1},{1,0},{2,3},{3,2},{4,5},{5,4},{6,7},{7,6},{8,9},{9,8},{10,11... | collective-permute-start | bytes 221192 | tf_op jit(solution)/shard_map/ppermute | solution.py:522

commit v4 on v3

--- a/solution.py
+++ b/solution.py
@@ -15,6 +15,7 @@
 UNROLL_CHUNK = 8
 UNROLL_BIN = 9
 UNROLL_ROWS = 8
+PACK_PARTS = 4
 FIRST_LIMIT = 56
 SECOND_LIMIT = 50
 F32 = jnp.float32
@@ -171,12 +172,32 @@
     return copies
 
 
-def pack_kernel(tokens_hbm, cotan_hbm, out, tokens, cotan, semaphores):
-    for copy in fetch((tokens_hbm, cotan_hbm), (tokens, cotan), semaphores):
-        copy.wait()
-    for block in range(out.shape[0]):
-        lanes = slice(64 * block, 64 * block + 64)
-        out[block] = jnp.concatenate([tokens[:, lanes], cotan[:, lanes]], axis=1)
+def pack_kernel(tokens_hbm, cotan_hbm, out_hbm, tokens, cotan, out, load_semaphores, store_semaphores):
+    loads, stores = [], []
+    rows_each = tokens.shape[0] // PACK_PARTS
+    for part in range(PACK_PARTS):
+        rows = pl.ds(part * rows_each, rows_each)
+        loads.append(
+            fetch(
+                (tokens_hbm.at[rows, :], cotan_hbm.at[rows, :]),
+                (tokens.at[rows, :], cotan.at[rows, :]),
+                load_semaphores.at[part],
+            )
+        )
+    for part in range(PACK_PARTS):
+        rows = pl.ds(part * rows_each, rows_each)
+        for copy in loads[part]:
+            copy.wait()
+        for block in range(out.shape[0]):
+            lanes = slice(64 * block, 64 * block + 64)
+            out[block, rows, :] = jnp.concatenate([tokens[rows, lanes], cotan[rows, lanes]], axis=1)
+        store = pltpu.make_async_copy(
+            out.at[:, rows, :], out_hbm.at[:, rows, :], store_semaphores.at[part]
+        )
+        store.start()
+        stores.append(store)
+    for store in stores:
+        store.wait()
 
 
 def diagonal(matrix):
@@ -199,8 +220,7 @@
 
 def kernel_spectrum_kernel(
     length, rates, w_first, w_bias, w_mid, w_last, matrix, twiddle, wide_hbm, narrow_hbm,
-    spectrum, env_out, slope_one, slope_two, one_high, one_low, two_high, two_low, mid_back,
-    last_back, semaphores, taps, stage,
+    spectrum, slope_two, consts, two_high, two_low, mid_back, last_back, semaphores, taps, stage,
 ):
     inner = 2 * length // RADIX
     low_half = low_lanes(inner)
@@ -220,6 +240,7 @@
     last_back[...] = tall_three(last.T)
     mid, last = tall_three(mid), tall_three(last)
     first, bias = twice(w_first[...]), twice(w_bias[...])
+    consts[...] = jnp.concatenate([rate, scale, first, bias, jnp.zeros((4, 128), F32)], axis=0)
 
     def block(step, carry):
         start = pl.multiple_of(step * inner, inner)
@@ -230,7 +251,6 @@
         pre_one = scaled * first + bias
         gate_one = 1.0 / (1.0 + jnp.exp(-pre_one))
         hidden_one = pre_one * gate_one
-        slope_one[rows, :] = gate_one * (1.0 + pre_one * (1.0 - gate_one))
         pre_two = dot(wide_three(hidden_one), mid)
         gate_two = 1.0 / (1.0 + jnp.exp(-pre_two))
         hidden_two = pre_two * gate_two
@@ -239,14 +259,12 @@
         live = jnp.where(lag == -length, 0.0, 1.0)
         env = live * scale * jnp.exp(-jnp.abs(lag).astype(F32) * rate)
         taps[rows, :] = (position * env).astype(BF16).astype(F32)
-        env_out[rows, :] = env
-        one_high[:, rows], one_low[:, rows] = split_pair(hidden_one.T)
         two_high[:, rows], two_low[:, rows] = split_pair(hidden_two.T)
         return carry
 
     lax.fori_loop(0, HALF, block, 0, unroll=UNROLL_ROWS)
     places = passed_places(length, wide_hbm, narrow_hbm)
-    held = (env_out, slope_one, slope_two, one_high, one_low, two_high, two_low, mid_back, last_back)
+    held = (slope_two, consts, two_high, two_low, mid_back, last_back)
     copies = fetch(held, places[1:], semaphores)
     residues_to_scratch(lambda start: taps[pl.ds(start, CHUNK), :], twiddle, stage, inner)
 
@@ -266,13 +284,13 @@
 
 def gradient_kernel(
     length, signal, wide_hbm, narrow_hbm, matrix, twiddle, out,
-    spectrum, env, slope_one, slope_two, one_high, one_low, two_high, two_low, mid_back, last_back,
-    semaphores, stage, back_ref, slope_high, slope_low, pre_high, pre_low,
+    spectrum, slope_two, consts, two_high, two_low, mid_back, last_back, semaphores, stage, back_ref, slope_high, slope_low, pre_high, pre_low,
+    one_high, one_low, decay,
 ):
     padded = 2 * length
     inner = padded // RADIX
     low_half = low_lanes(inner)
-    held = (spectrum, env, slope_one, slope_two, one_high, one_low, two_high, two_low, mid_back, last_back)
+    held = (spectrum, slope_two, consts, two_high, two_low, mid_back, last_back)
     copies = fetch(passed_places(length, wide_hbm, narrow_hbm), held, semaphores)
     residues_to_scratch(
         lambda start: signal[pl.ds(start, CHUNK), :].astype(F32), twiddle, stage, inner
@@ -299,7 +317,13 @@
         return carry
 
     lax.fori_loop(0, HALF + 1, transform, 0, unroll=UNROLL_BIN)
-    copies[1].wait()
+    for copy in copies[1:]:
+        copy.wait()
+    rate, scale, first, bias = (consts[index : index + 1, :] for index in range(4))
+    place = lax.broadcasted_iota(jnp.int32, (inner, 128), 0)
+    near = jnp.where(low_half, place, inner - 1 - place).astype(F32)
+    decay[...] = jnp.exp(-near * rate)
+    low_row = low_lanes(1)
 
     def unspread(step, carry):
         start = pl.multiple_of(step * CHUNK, CHUNK)
@@ -323,13 +347,22 @@
             back_ref[q, rows, 0:128] = joined
             at = pl.ds(q * inner + start, CHUNK)
             lag_grad = jnp.where(low_lanes(CHUNK), swap(joined), apart)
-            slope_high[at, :], slope_low[at, :] = split_pair(lag_grad * env[at, :])
+            far = jnp.where(low_row, q * inner, length - q * inner - inner + 1).astype(F32)
+            weighted = lag_grad * (scale * jnp.exp(-far * rate)) * decay[rows, :]
+            if q == 0:
+                row = start + lax.broadcasted_iota(jnp.int32, (CHUNK, 128), 0)
+                weighted = jnp.where((row == 0) & ~low_lanes(CHUNK), 0.0, weighted)
+            slope_high[at, :], slope_low[at, :] = split_pair(weighted)
         return carry
 
     lax.fori_loop(0, inner // CHUNK, unspread, 0, unroll=UNROLL_CHUNK)
-    for copy in copies[2:]:
-        copy.wait()
     local_rows = 128
+    rise = jnp.exp(place.astype(F32) * (first * (-1.0 / length)))
+    first_column = jnp.broadcast_to(first, (8, 128)).T[:, 0:1]
+    bias_column = jnp.broadcast_to(bias, (8, 128)).T[:, 0:1]
+    along = lax.broadcasted_iota(jnp.int32, (128, inner), 1)
+    low_column = lax.broadcasted_iota(jnp.int32, (128, 1), 0) < 64
+    rise_across = jnp.exp(along.astype(F32) * (first_column * (-1.0 / length)))
     half_rows = local_rows // 2
 
     def block(q, carry):
@@ -348,9 +381,17 @@
         high, low = split_pair(dot(slope, last_back[...]) * slope_two[rows, :])
         pre_high[rows, :], pre_low[rows, :] = high, low
         pre_two = jnp.concatenate([high, low, high], axis=1)
-        pre_one = dot(pre_two, mid_back[...]) * slope_one[rows, :]
-        place = start + lax.broadcasted_iota(jnp.int32, (inner, 128), 0)
-        scaled = jnp.where(low_half, place, place - length).astype(F32) / length
+        base = jnp.where(low_row, start, start - length)
+        scaled = (place + base).astype(F32) * (1.0 / length)
+        before = scaled * first + bias
+        gate = 1.0 / (1.0 + rise * jnp.exp(-(base.astype(F32) * (1.0 / length) * first + bias)))
+        slope_one = gate * (1.0 + before * (1.0 - gate))
+        base = jnp.where(low_column, start, start - length)
+        across = (along + base).astype(F32) * (1.0 / length) * first_column + bias_column
+        offset = base.astype(F32) * (1.0 / length) * first_column + bias_column
+        across = across * (1.0 / (1.0 + rise_across * jnp.exp(-offset)))
+        one_high[:, rows], one_low[:, rows] = split_pair(across)
+        pre_one = dot(pre_two, mid_back[...]) * slope_one
         first_sum = first_sum + jnp.sum((pre_one * scaled).reshape(inner // 8, 8, 128), axis=0)
         bias_sum = bias_sum + jnp.sum(pre_one.reshape(inner // 8, 8, 128), axis=0)
         return first_sum, bias_sum
@@ -363,44 +404,43 @@
     mid_sum = dot(one_high[...], pre_high[...]) + (
         dot(one_low[...], pre_high[...]) + dot(one_high[...], pre_low[...])
     )
-    low_64 = low_lanes(64)
     low_32 = low_lanes(32)
     grad_last = last_sum[0:64] + swap(last_sum[64:128])
-    pair = jnp.where(low_32, grad_last[0:32], swap(grad_last[32:64]))
-    mid_total = mid_sum[0:64] + swap(mid_sum[64:128])
-    mid_high = mid_total.astype(BF16).astype(F32)
-    mid_rows = jnp.where(low_64, mid_high, swap(mid_total - mid_high))
+    last_rows = jnp.where(low_32, grad_last[0:32], swap(grad_last[32:64]))
+    grad_mid = mid_sum[0:64] + swap(mid_sum[64:128])
+    mid_rows = jnp.where(low_32, grad_mid[0:32], swap(grad_mid[32:64]))
     first = jnp.sum(first_sum, axis=0, keepdims=True)
     bias = jnp.sum(bias_sum, axis=0, keepdims=True)
     first = first + swap(first)
     bias = bias + swap(bias)
     joined = jnp.where(low_lanes(1), first, bias)
     joined_high = joined.astype(BF16).astype(F32)
-    row_index = lax.broadcasted_iota(jnp.int32, (16, 128), 0)
+    row_index = lax.broadcasted_iota(jnp.int32, (8, 128), 0)
     joined_rows = jnp.where(
         row_index == 0, joined_high, jnp.where(row_index == 1, joined - joined_high, 0.0)
     )
     for device in range(out.shape[0]):
-        odd = device % 2
-        tail = [pair[16 * odd : 16 * odd + 16], mid_rows[32 * odd : 32 * odd + 32], joined_rows]
+        half = slice(16 * (device % 2), 16 * (device % 2) + 16)
+        tail = [last_rows[half], mid_rows[half], joined_rows]
         out[device, half_rows:, :] = jnp.concatenate(tail, axis=0).astype(BF16)
 
 
 def sums_kernel(received, half, joined_out):
-    half_rows = received.shape[1] - 64
-    mid = jnp.zeros((32, 128), F32)
-    joined = jnp.zeros((16, 128), F32)
+    half_rows = received.shape[1] - 40
+    mid = jnp.zeros((16, 128), F32)
+    joined = jnp.zeros((8, 128), F32)
     for source in range(received.shape[0]):
         lanes = slice(64 * source, 64 * source + 64)
         last = received[source, half_rows : half_rows + 16, :]
         half[0:16, lanes] = last[:, 0:64]
         half[16:32, lanes] = last[:, 64:128]
-        mid = mid + received[source, half_rows + 16 : half_rows + 48, :].astype(F32)
-        joined = joined + received[source, half_rows + 48 : half_rows + 64, :].astype(F32)
-    mid = mid + swap(mid)
+        mid = mid + received[source, half_rows + 16 : half_rows + 32, :].astype(F32)
+        joined = joined + received[source, half_rows + 32 : half_rows + 40, :].astype(F32)
+    mid = jnp.concatenate([mid, swap(mid)], axis=0)
     high = mid.astype(BF16).astype(F32)
     columns = 64 * received.shape[0]
-    half[:, columns : columns + 128] = jnp.where(low_lanes(32), high, mid - high).astype(BF16)
+    rest = swap(mid - high)
+    half[:, columns : columns + 128] = jnp.where(low_lanes(32), high, rest).astype(BF16)
     joined_out[...] = joined
 
 
@@ -421,7 +461,9 @@
         grad_last[pl.ds(pl.multiple_of(16 * parity, 16), 16), :] = last[0:16]
         grad_last[pl.ds(pl.multiple_of(32 + 16 * parity, 16), 16), :] = last[16:32]
         mid = source[:, columns : columns + 128].astype(F32) * loss_scale
-        grad_mid[pl.ds(pl.multiple_of(32 * parity, 32), 32), :] = (mid + swap(mid))[:, 0:64]
+        mid = (mid + swap(mid))[:, 0:64]
+        grad_mid[pl.ds(pl.multiple_of(16 * parity, 16), 16), :] = mid[0:16]
+        grad_mid[pl.ds(pl.multiple_of(32 + 16 * parity, 16), 16), :] = mid[16:32]
     first = (joined[0:1] + joined[1:2]) * loss_scale
     grad_first[...] = first[:, 0:64]
     grad_bias[...] = first[:, 64:128]
@@ -448,21 +490,21 @@
 
 def passed_places(length, wide, narrow):
     bins = 2 * (HALF + 1) * (2 * length // RADIX)
-    parts = [wide.at[pl.ds(0, bins), :]]
-    parts += [wide.at[pl.ds(bins + index * length, length), :] for index in range(3)]
-    parts += [narrow.at[pl.ds(128 * index, 128), :] for index in range(4)]
-    return parts + [narrow.at[pl.ds(512, 384), pl.ds(128 * index, 128)] for index in range(2)]
+    parts = [wide.at[pl.ds(0, bins), :], wide.at[pl.ds(bins, length), :]]
+    parts += [wide.at[pl.ds(bins + length, 8), :]]
+    parts += [narrow.at[pl.ds(128 * index, 128), :] for index in range(2)]
+    return parts + [narrow.at[pl.ds(256, 384), pl.ds(128 * index, 128)] for index in range(2)]
 
 
 def passed_shapes(length):
     bins = 2 * (HALF + 1) * (2 * length // RADIX)
-    return [shape((bins + 3 * length, 128), F32), shape((512 + 384, length), BF16)]
+    return [shape((bins + length + 8, 128), F32), shape((256 + 384, length), BF16)]
 
 
 def held_arrays(length):
     bins = 2 * (HALF + 1) * (2 * length // RADIX)
-    held = [pltpu.VMEM((bins, 128), F32)] + [pltpu.VMEM((length, 128), F32)] * 3
-    held += [pltpu.VMEM((128, length), BF16)] * 4 + [pltpu.VMEM((384, 128), BF16)] * 2
+    held = [pltpu.VMEM((rows, 128), F32) for rows in (bins, length, 8)]
+    held += [pltpu.VMEM((128, length), BF16)] * 2 + [pltpu.VMEM((384, 128), BF16)] * 2
     return held + [pltpu.SemaphoreType.DMA((len(held),))]
 
 
@@ -484,13 +526,15 @@
     local_rows = 128
     return call(
         functools.partial(gradient_kernel, length),
-        shape((length // local_rows, local_rows // 2 + 64, 128), BF16),
+        shape((length // local_rows, local_rows // 2 + 40, 128), BF16),
         scratch=held_arrays(length)
         + [
             pltpu.VMEM((HALF + 1, 3 * inner, 256), BF16),
             pltpu.VMEM((HALF + 1, inner, 256), F32),
         ]
-        + [pltpu.VMEM((length, 128), BF16)] * 4,
+        + [pltpu.VMEM((length, 128), BF16)] * 4
+        + [pltpu.VMEM((128, length), BF16)] * 2
+        + [pltpu.VMEM((inner, 128), F32)],
         flops=8 << 30,
         limit=SECOND_LIMIT,
         in_specs=[ON_VMEM] + [ON_HBM] * 2 + [ON_VMEM] * 2,
@@ -505,9 +549,15 @@
     packed = call(
         pack_kernel,
         shape((devices, local_rows, 128), BF16),
-        scratch=[pltpu.VMEM(tokens_in.shape, BF16)] * 2 + [pltpu.SemaphoreType.DMA((2,))],
+        scratch=[pltpu.VMEM(tokens_in.shape, BF16)] * 2
+        + [
+            pltpu.VMEM((devices, local_rows, 128), BF16),
+            pltpu.SemaphoreType.DMA((PACK_PARTS, 2)),
+            pltpu.SemaphoreType.DMA((PACK_PARTS,)),
+        ],
         limit=58,
         in_specs=[ON_HBM] * 2,
+        out_specs=ON_HBM,
     )(tokens_in, grad_out)
     signal = lax.all_to_all(packed, "ctx", split_axis=0, concat_axis=0, tiled=True)
     forward = spectrum_call(
@@ -517,7 +567,7 @@
     sent = gradient_call(length, signal.reshape(length, 128), *forward, matrix, twiddle)
     received = lax.all_to_all(sent, "ctx", split_axis=0, concat_axis=0, tiled=True)
     half, joined = call(
-        sums_kernel, [shape((32, 64 * devices + 128), BF16), shape((16, 128), F32)]
+        sums_kernel, [shape((32, 64 * devices + 128), BF16), shape((8, 128), F32)]
     )(received)
     other = lax.ppermute(half, "ctx", [(index, index ^ 1) for index in range(devices)])
     input_grad = call(tokens_kernel, shape(tokens_in.shape, BF16), flops=1 << 26)(received)

time: 57 us -> 54.9 us (0.963)
  blocking collectives: 18.4 us -> 16.6 us
    all_to_all x1, blocking collectives: 18.4 us -> 16.6 us  [by_channels(): lax.all_to_all(sent, 'ctx', split_axis=0, concat_axis=0, tiled=True)]
where the time goes in v4:
time: 54.9 us; the launch traced here: 54.5 us
  Pallas kernels  23 us (42%)
  blocking collectives  16.6 us (30%)
  starting transfers between devices  7.51 us (14%)
  waiting for transfers between devices  6.74 us (12%)
  between operations  0.68 us (1%)
    all_to_all x1, blocking collectives, by_channels(): lax.all_to_all(sent, 'ctx', split_axis=0, concat_axis=0, tiled=True)  16.6 us
    pallas_call x1, Pallas kernels, gradient_call(): call(functools.partial(gradient_kernel, length), shape((length // local_r...  11.2 us
    pallas_call x1, Pallas kernels, spectrum_call(): call(functools.partial(kernel_spectrum_kernel, length), passed_shapes(len...  7.94 us
    all_to_all x1, starting transfers between devices, by_channels(): lax.all_to_all(packed, 'ctx', split_axis=0, concat_axis=0, tiled=True)  7.37 us
    all_to_all x1, waiting for transfers between devices, by_channels(): lax.all_to_all(packed, 'ctx', split_axis=0, concat_axis=0, tiled=True)  6.5 us
    pallas_call x1, Pallas kernels, by_channels(): call(pack_kernel, shape((devices, local_rows, 128), BF16), scratch=[pltpu...  2.06 us
  transfers between devices with their start and end apart: 2, of which 2 were waited for; matrix products, arithmetic and copies ran while one was open for 0% of the time, Pallas kernels for 16%

profile of v4, /device:TPU:0, one launch (start us, length us, event | category | flops | bytes accessed | tf_op | source)
XLA Modules:
  0.0 54.5 jit_solution(5106058504966862826)
XLA Ops:
  0.6 2.1 %shard_map.128 = bf16[16,128,128]{2,1,0:T(8,128)(2,1)} custom-call(bf16[128,1024]{1,0:T(8,128)(2,1)} %tokens_hbm.1, bf16[128,1024]{1,0:T(8,128)(2,1)} %cotan_hbm.1), custom_call_target="tpu_custom_call" | custom-call | bytes 1048576 | tf_op jit(solution)/shard_map/pallas_call | solution.py:549
  2.7 7.4 %all-to-all-start = ((bf16[16,128,128]{2,1,0:T(8,128)(2,1)}), bf16[16,128,128]{2,1,0:T(8,128)(2,1)S(1)}, u32[]{:S(2)}, u32[]{:S(2)}) async-start(bf16[16,128,128]{2,1,0:T(8,128)(2,1)} %shard_map.128), calls=%async_computation | async-start | bytes 1048576 | tf_op jit(solution)/shard_map/all_to_all | solution.py:562
  10.1 0.0 copy-start
  10.1 0.0 copy-start.1
  10.1 7.9 %shard_map.129 = (f32[6664,128]{1,0:T(8,128)}, bf16[640,2048]{1,0:T(8,128)(2,1)}) custom-call(f32[1,1024]{1,0:T(1,128)} %bitcast.7, f32[1,64]{1,0:T(1,128)} %bitcast.8, f32[1,64]{1,0:T(1,128)} %bitcast.9, f32[64,64]{1,0:T(8,128)} %w_mid.1, f32[64,1024]{1,0:T(8,128)} %w_last.1, bf16[512,768]{1,0:T(8,128)(2,1)} %constant.4.clone.matrix, ...), custom_call_target="tpu_custom_call" | custom-call | flops 4294967296 | bytes 1048576 | tf_op jit(solution)/shard_map/pallas_call | solution.py:513
  18.0 6.5 %all-to-all-done = bf16[16,128,128]{2,1,0:T(8,128)(2,1)S(1)} async-done(((bf16[16,128,128]{2,1,0:T(8,128)(2,1)}), bf16[16,128,128]{2,1,0:T(8,128)(2,1)S(1)}, u32[]{:S(2)}, u32[]{:S(2)}) %all-to-all-start) | async-done | bytes 524320 | tf_op jit(solution)/shard_map/all_to_all | solution.py:562
  24.5 0.0 copy-done
  24.5 0.0 copy-done.1
  24.6 11.2 %shard_map.130 = bf16[16,104,128]{2,1,0:T(8,128)(2,1)S(1)} custom-call(bf16[2048,128]{1,0:T(8,128)(2,1)S(1)} %bitcast.6, f32[6664,128]{1,0:T(8,128)} %get-tuple-element.13.wide_hbm, bf16[640,2048]{1,0:T(8,128)(2,1)} %get-tuple-element.14.narrow_hbm, bf16[512,768]{1,0:T(8,128)(2,1)S(1)} %copy-done, f32[256,128]{1,0:T(8,128)S(1)} %copy-done.1), custom_call_target="tpu_custom_call" | custom-call | flops 8589934592 | bytes 1048576 | tf_op jit(solution)/shard_map/pallas_call | solution.py:527
  35.7 16.6 %all_to_all.10.received = bf16[16,104,128]{2,1,0:T(8,128)(2,1)S(1)} all-to-all(bf16[16,104,128]{2,1,0:T(8,128)(2,1)S(1)} %shard_map.130), channel_id=1, replica_groups=mesh['groups'=2,'ctx'=16] {'ctx'}, dimensions={0} | all-to-all | bytes 851968 | tf_op jit(solution)/shard_map/all_to_all | solution.py:568
  52.3 0.2 shard_map.132
  52.5 0.1 collective-permute-start
  52.7 0.9 %shard_map.131 = bf16[128,1024]{1,0:T(8,128)(2,1)} custom-call(bf16[16,104,128]{2,1,0:T(8,128)(2,1)S(1)} %all_to_all.10.received), custom_call_target="tpu_custom_call" | custom-call | flops 67108864 | bytes 1048576 | tf_op jit(solution)/shard_map/pallas_call | solution.py:573
  53.6 0.2 collective-permute-done.other
  53.8 0.7 %shard_map.133 = (f32[1,64]{1,0:T(1,128)}, f32[1,64]{1,0:T(1,128)}, f32[64,64]{1,0:T(8,128)}, f32[64,1024]{1,0:T(8,128)}) custom-call(f32[8,128]{1,0:T(8,128)S(1)} %get-tuple-element.15.joined, bf16[32,1152]{1,0:T(8,128)(2,1)S(1)} %get-tuple-element.16.mine, bf16[32,1152]{1,0:T(8,128)(2,1)S(1)} %collective-permute-done.other), custom_call_target="tpu_custom_call" | custom-call | bytes 1048576 | tf_op jit(solution)/shard_map/pallas_call | solution.py:574
Async XLA Ops:
  2.7 21.8 %all-to-all-start = ((bf16[16,128,128]{2,1,0:T(8,128)(2,1)}), bf16[16,128,128]{2,1,0:T(8,128)(2,1)S(1)}, u32[]{:S(2)}, u32[]{:S(2)}) async-start(bf16[16,128,128]{2,1,0:T(8,128)(2,1)} %shard_map.128), calls=%async_computation | async-start | bytes 1048576 | tf_op jit(solution)/shard_map/all_to_all | solution.py:562
  10.1 14.5 %copy-start = (bf16[512,768]{1,0:T(8,128)(2,1)S(1)}, bf16[512,768]{1,0:T(8,128)(2,1)}, u32[]{:S(2)}) copy-start(bf16[512,768]{1,0:T(8,128)(2,1)} %constant.4.clone.matrix) | copy-start | bytes 2359300
  10.1 14.5 %copy-start.1 = (f32[256,128]{1,0:T(8,128)S(1)}, f32[256,128]{1,0:T(8,128)}, u32[]{:S(2)}) copy-start(f32[256,128]{1,0:T(8,128)} %constant.5.clone.twiddle) | copy-start | bytes 393220
  52.5 1.3 %collective-permute-start = (bf16[32,1152]{1,0:T(8,128)(2,1)S(1)}, bf16[32,1152]{1,0:T(8,128)(2,1)S(1)}, u32[]{:S(2)}, u32[]{:S(2)}) collective-permute-start(bf16[32,1152]{1,0:T(8,128)(2,1)S(1)} %get-tuple-element.16.mine), channel_id=1, source_target_pairs={{0,1},{1,0},{2,3},{3,2},{4,5},{5,4},{6,7},{7,6},{8,9},{9,8},{10,11... | collective-permute-start | bytes 221192 | tf_op jit(solution)/shard_map/ppermute | solution.py:572

commit v5 on v4

--- a/solution.py
+++ b/solution.py
@@ -31,9 +31,24 @@
     return jnp.dot(left, right, preferred_element_type=F32)
 
 
-def wide_three(value):
-    high, low = split_pair(value)
-    return jnp.concatenate([high, low, high], axis=1)
+def pair_lanes(value):
+    return jnp.concatenate(split_pair(value), axis=1)
+
+
+def square(matrix):
+    high, low = split_pair(matrix)
+    return jnp.concatenate(
+        [
+            jnp.concatenate([high, low], axis=1),
+            jnp.concatenate([high, jnp.zeros_like(low)], axis=1),
+        ],
+        axis=0,
+    )
+
+
+def dot_pair(rows, squared):
+    product = dot(rows, squared)
+    return product[:, 0:128] + product[:, 128:256]
 
 
 def tall_three(value):
@@ -220,7 +235,7 @@
 
 def kernel_spectrum_kernel(
     length, rates, w_first, w_bias, w_mid, w_last, matrix, twiddle, wide_hbm, narrow_hbm,
-    spectrum, slope_two, consts, two_high, two_low, mid_back, last_back, semaphores, taps, stage,
+    spectrum, slope_two, consts, one, two, mid_back, last_back, semaphores, taps, stage,
 ):
     inner = 2 * length // RADIX
     low_half = low_lanes(inner)
@@ -236,9 +251,9 @@
     geometric = 1.0 + 2.0 * jnp.exp(-double) * ratio
     scale = lax.rsqrt(geometric)
     mid = diagonal(w_mid[...])
-    mid_back[...] = tall_three(mid.T)
-    last_back[...] = tall_three(last.T)
-    mid, last = tall_three(mid), tall_three(last)
+    mid_back[...] = square(mid.T)
+    last_back[...] = square(last.T)
+    mid, last = square(mid), square(last)
     first, bias = twice(w_first[...]), twice(w_bias[...])
     consts[...] = jnp.concatenate([rate, scale, first, bias, jnp.zeros((4, 128), F32)], axis=0)
 
@@ -251,20 +266,21 @@
         pre_one = scaled * first + bias
         gate_one = 1.0 / (1.0 + jnp.exp(-pre_one))
         hidden_one = pre_one * gate_one
-        pre_two = dot(wide_three(hidden_one), mid)
+        pre_two = dot_pair(pair_lanes(hidden_one), mid)
         gate_two = 1.0 / (1.0 + jnp.exp(-pre_two))
         hidden_two = pre_two * gate_two
         slope_two[rows, :] = gate_two * (1.0 + pre_two * (1.0 - gate_two))
-        position = dot(wide_three(hidden_two), last)
+        position = dot_pair(pair_lanes(hidden_two), last)
         live = jnp.where(lag == -length, 0.0, 1.0)
         env = live * scale * jnp.exp(-jnp.abs(lag).astype(F32) * rate)
         taps[rows, :] = (position * env).astype(BF16).astype(F32)
-        two_high[:, rows], two_low[:, rows] = split_pair(hidden_two.T)
+        one[0:128, rows], one[128:256, rows] = split_pair(hidden_one.T)
+        two[0:128, rows], two[128:256, rows] = split_pair(hidden_two.T)
         return carry
 
     lax.fori_loop(0, HALF, block, 0, unroll=UNROLL_ROWS)
     places = passed_places(length, wide_hbm, narrow_hbm)
-    held = (slope_two, consts, two_high, two_low, mid_back, last_back)
+    held = (slope_two, consts, one, two, mid_back, last_back)
     copies = fetch(held, places[1:], semaphores)
     residues_to_scratch(lambda start: taps[pl.ds(start, CHUNK), :], twiddle, stage, inner)
 
@@ -284,21 +300,29 @@
 
 def gradient_kernel(
     length, signal, wide_hbm, narrow_hbm, matrix, twiddle, out,
-    spectrum, slope_two, consts, two_high, two_low, mid_back, last_back, semaphores, stage, back_ref, slope_high, slope_low, pre_high, pre_low,
-    one_high, one_low, decay,
+    spectrum, slope_two, consts, one, two, mid_back, last_back, semaphores, stage, back_ref, slopes,
+    pre, decay,
 ):
     padded = 2 * length
     inner = padded // RADIX
     low_half = low_lanes(inner)
-    held = (spectrum, slope_two, consts, two_high, two_low, mid_back, last_back)
+    held = (spectrum, slope_two, consts, one, two, mid_back, last_back)
     copies = fetch(passed_places(length, wide_hbm, narrow_hbm), held, semaphores)
     residues_to_scratch(
         lambda start: signal[pl.ds(start, CHUNK), :].astype(F32), twiddle, stage, inner
     )
+
+    def analyse(j, carry):
+        real, imag = inner_dft(stage[j], matrix, inner, 1)
+        back_ref[j, :, 0:128] = real
+        back_ref[j, :, 128:256] = imag
+        return carry
+
+    lax.fori_loop(0, HALF + 1, analyse, 0, unroll=UNROLL_BIN)
     copies[0].wait()
 
     def transform(j, carry):
-        real, imag = inner_dft(stage[j], matrix, inner, 1)
+        real, imag = back_ref[j, :, 0:128], back_ref[j, :, 128:256]
         real_swap, imag_swap = swap(real), swap(imag)
         cotan_real = jnp.where(low_half, real_swap, real)
         cotan_imag = jnp.where(low_half, imag_swap, imag)
@@ -352,18 +376,13 @@
             if q == 0:
                 row = start + lax.broadcasted_iota(jnp.int32, (CHUNK, 128), 0)
                 weighted = jnp.where((row == 0) & ~low_lanes(CHUNK), 0.0, weighted)
-            slope_high[at, :], slope_low[at, :] = split_pair(weighted)
+            slopes[at, :] = pair_lanes(weighted)
         return carry
 
     lax.fori_loop(0, inner // CHUNK, unspread, 0, unroll=UNROLL_CHUNK)
     local_rows = 128
+    half_rows = local_rows // 2
     rise = jnp.exp(place.astype(F32) * (first * (-1.0 / length)))
-    first_column = jnp.broadcast_to(first, (8, 128)).T[:, 0:1]
-    bias_column = jnp.broadcast_to(bias, (8, 128)).T[:, 0:1]
-    along = lax.broadcasted_iota(jnp.int32, (128, inner), 1)
-    low_column = lax.broadcasted_iota(jnp.int32, (128, 1), 0) < 64
-    rise_across = jnp.exp(along.astype(F32) * (first_column * (-1.0 / length)))
-    half_rows = local_rows // 2
 
     def block(q, carry):
         first_sum, bias_sum = carry
@@ -376,33 +395,23 @@
             out[q * (inner // local_rows) + part, 0:half_rows, :] = jnp.where(
                 low_half[:half_rows], upper, swap(lower)
             ).astype(BF16)
-        high, low = slope_high[rows, :], slope_low[rows, :]
-        slope = jnp.concatenate([high, low, high], axis=1)
-        high, low = split_pair(dot(slope, last_back[...]) * slope_two[rows, :])
-        pre_high[rows, :], pre_low[rows, :] = high, low
-        pre_two = jnp.concatenate([high, low, high], axis=1)
+        pre_two = pair_lanes(dot_pair(slopes[rows, :], last_back[...]) * slope_two[rows, :])
+        pre[rows, :] = pre_two
         base = jnp.where(low_row, start, start - length)
         scaled = (place + base).astype(F32) * (1.0 / length)
         before = scaled * first + bias
         gate = 1.0 / (1.0 + rise * jnp.exp(-(base.astype(F32) * (1.0 / length) * first + bias)))
         slope_one = gate * (1.0 + before * (1.0 - gate))
-        base = jnp.where(low_column, start, start - length)
-        across = (along + base).astype(F32) * (1.0 / length) * first_column + bias_column
-        offset = base.astype(F32) * (1.0 / length) * first_column + bias_column
-        across = across * (1.0 / (1.0 + rise_across * jnp.exp(-offset)))
-        one_high[:, rows], one_low[:, rows] = split_pair(across)
-        pre_one = dot(pre_two, mid_back[...]) * slope_one
+        pre_one = dot_pair(pre_two, mid_back[...]) * slope_one
         first_sum = first_sum + jnp.sum((pre_one * scaled).reshape(inner // 8, 8, 128), axis=0)
         bias_sum = bias_sum + jnp.sum(pre_one.reshape(inner // 8, 8, 128), axis=0)
         return first_sum, bias_sum
 
     none = jnp.zeros((8, 128), F32)
     first_sum, bias_sum = lax.fori_loop(0, HALF, block, (none, none), unroll=UNROLL_ROWS)
-    last_sum = dot(two_high[...], slope_high[...]) + (
-        dot(two_low[...], slope_high[...]) + dot(two_high[...], slope_low[...])
-    )
-    mid_sum = dot(one_high[...], pre_high[...]) + (
-        dot(one_low[...], pre_high[...]) + dot(one_high[...], pre_low[...])
+    last_sum, mid_sum = (
+        product[0:128, 0:128] + (product[0:128, 128:256] + product[128:256, 0:128])
+        for product in (dot(two[...], slopes[...]), dot(one[...], pre[...]))
     )
     low_32 = low_lanes(32)
     grad_last = last_sum[0:64] + swap(last_sum[64:128])
@@ -492,19 +501,19 @@
     bins = 2 * (HALF + 1) * (2 * length // RADIX)
     parts = [wide.at[pl.ds(0, bins), :], wide.at[pl.ds(bins, length), :]]
     parts += [wide.at[pl.ds(bins + length, 8), :]]
-    parts += [narrow.at[pl.ds(128 * index, 128), :] for index in range(2)]
-    return parts + [narrow.at[pl.ds(256, 384), pl.ds(128 * index, 128)] for index in range(2)]
+    parts += [narrow.at[pl.ds(256 * index, 256), :] for index in range(2)]
+    return parts + [narrow.at[pl.ds(512, 256), pl.ds(256 * index, 256)] for index in range(2)]
 
 
 def passed_shapes(length):
     bins = 2 * (HALF + 1) * (2 * length // RADIX)
-    return [shape((bins + length + 8, 128), F32), shape((256 + 384, length), BF16)]
+    return [shape((bins + length + 8, 128), F32), shape((512 + 256, length), BF16)]
 
 
 def held_arrays(length):
     bins = 2 * (HALF + 1) * (2 * length // RADIX)
     held = [pltpu.VMEM((rows, 128), F32) for rows in (bins, length, 8)]
-    held += [pltpu.VMEM((128, length), BF16)] * 2 + [pltpu.VMEM((384, 128), BF16)] * 2
+    held += [pltpu.VMEM((256, length), BF16)] * 2 + [pltpu.VMEM((256, 256), BF16)] * 2
     return held + [pltpu.SemaphoreType.DMA((len(held),))]
 
 
@@ -532,8 +541,7 @@
             pltpu.VMEM((HALF + 1, 3 * inner, 256), BF16),
             pltpu.VMEM((HALF + 1, inner, 256), F32),
         ]
-        + [pltpu.VMEM((length, 128), BF16)] * 4
-        + [pltpu.VMEM((128, length), BF16)] * 2
+        + [pltpu.VMEM((length, 256), BF16)] * 2
         + [pltpu.VMEM((inner, 128), F32)],
         flops=8 << 30,
         limit=SECOND_LIMIT,

time: 54.9 us -> 51.6 us (0.940)
  Pallas kernels: 23 us -> 19.7 us
    pallas_call x1, Pallas kernels: 11.2 us -> 7.87 us  [gradient_call(): call(functools.partial(gradient_kernel, length), shape((length // local_r...]
  transfers between devices with their start and end apart: 2 -> 2, of which waited for: 2 -> 2; matrix products, arithmetic and copies ran while one was open for 0% -> 0% of each run, Pallas kernels for 16% -> 17%
where the time goes in v5:
time: 51.6 us; the launch traced here: 51.3 us
  Pallas kernels  19.7 us (38%)
  blocking collectives  16.6 us (32%)
  starting transfers between devices  7.51 us (15%)
  waiting for transfers between devices  6.71 us (13%)
  between operations  0.68 us (1%)
    all_to_all x1, blocking collectives, by_channels(): lax.all_to_all(sent, 'ctx', split_axis=0, concat_axis=0, tiled=True)  16.6 us
    pallas_call x1, Pallas kernels, spectrum_call(): call(functools.partial(kernel_spectrum_kernel, length), passed_shapes(len...  7.97 us
    pallas_call x1, Pallas kernels, gradient_call(): call(functools.partial(gradient_kernel, length), shape((length // local_r...  7.87 us
    all_to_all x1, starting transfers between devices, by_channels(): lax.all_to_all(packed, 'ctx', split_axis=0, concat_axis=0, tiled=True)  7.37 us
    all_to_all x1, waiting for transfers between devices, by_channels(): lax.all_to_all(packed, 'ctx', split_axis=0, concat_axis=0, tiled=True)  6.46 us
    pallas_call x1, Pallas kernels, by_channels(): call(pack_kernel, shape((devices, local_rows, 128), BF16), scratch=[pltpu...  2.08 us
  transfers between devices with their start and end apart: 2, of which 2 were waited for; matrix products, arithmetic and copies ran while one was open for 0% of the time, Pallas kernels for 17%

profile of v5, /device:TPU:0, one launch (start us, length us, event | category | flops | bytes accessed | tf_op | source)
XLA Modules:
  0.0 51.3 jit_solution(8272302879395719)
XLA Ops:
  0.6 2.1 %shard_map.128 = bf16[16,128,128]{2,1,0:T(8,128)(2,1)} custom-call(bf16[128,1024]{1,0:T(8,128)(2,1)} %tokens_hbm.1, bf16[128,1024]{1,0:T(8,128)(2,1)} %cotan_hbm.1), custom_call_target="tpu_custom_call" | custom-call | bytes 1048576 | tf_op jit(solution)/shard_map/pallas_call | solution.py:557
  2.7 7.4 %all-to-all-start = ((bf16[16,128,128]{2,1,0:T(8,128)(2,1)}), bf16[16,128,128]{2,1,0:T(8,128)(2,1)S(1)}, u32[]{:S(2)}, u32[]{:S(2)}) async-start(bf16[16,128,128]{2,1,0:T(8,128)(2,1)} %shard_map.128), calls=%async_computation | async-start | bytes 1048576 | tf_op jit(solution)/shard_map/all_to_all | solution.py:570
  10.1 0.0 copy-start
  10.1 0.0 copy-start.1
  10.1 8.0 %shard_map.129 = (f32[6664,128]{1,0:T(8,128)}, bf16[768,2048]{1,0:T(8,128)(2,1)}) custom-call(f32[1,1024]{1,0:T(1,128)} %bitcast.7, f32[1,64]{1,0:T(1,128)} %bitcast.8, f32[1,64]{1,0:T(1,128)} %bitcast.9, f32[64,64]{1,0:T(8,128)} %w_mid.1, f32[64,1024]{1,0:T(8,128)} %w_last.1, bf16[512,768]{1,0:T(8,128)(2,1)} %constant.4.clone.matrix, ...), custom_call_target="tpu_custom_call" | custom-call | flops 4294967296 | bytes 1048576 | tf_op jit(solution)/shard_map/pallas_call | solution.py:522
  18.1 6.5 %all-to-all-done = bf16[16,128,128]{2,1,0:T(8,128)(2,1)S(1)} async-done(((bf16[16,128,128]{2,1,0:T(8,128)(2,1)}), bf16[16,128,128]{2,1,0:T(8,128)(2,1)S(1)}, u32[]{:S(2)}, u32[]{:S(2)}) %all-to-all-start) | async-done | bytes 524320 | tf_op jit(solution)/shard_map/all_to_all | solution.py:570
  24.6 0.0 copy-done
  24.6 0.0 copy-done.1
  24.6 7.9 %shard_map.130 = bf16[16,104,128]{2,1,0:T(8,128)(2,1)S(1)} custom-call(bf16[2048,128]{1,0:T(8,128)(2,1)S(1)} %bitcast.6, f32[6664,128]{1,0:T(8,128)} %get-tuple-element.13.wide_hbm, bf16[768,2048]{1,0:T(8,128)(2,1)} %get-tuple-element.14.narrow_hbm, bf16[512,768]{1,0:T(8,128)(2,1)S(1)} %copy-done, f32[256,128]{1,0:T(8,128)S(1)} %copy-done.1), custom_call_target="tpu_custom_call" | custom-call | flops 8589934592 | bytes 1048576 | tf_op jit(solution)/shard_map/pallas_call | solution.py:536
  32.5 16.6 %all_to_all.10.received = bf16[16,104,128]{2,1,0:T(8,128)(2,1)S(1)} all-to-all(bf16[16,104,128]{2,1,0:T(8,128)(2,1)S(1)} %shard_map.130), channel_id=1, replica_groups=mesh['groups'=2,'ctx'=16] {'ctx'}, dimensions={0} | all-to-all | bytes 851968 | tf_op jit(solution)/shard_map/all_to_all | solution.py:576
  49.1 0.2 shard_map.132
  49.2 0.1 collective-permute-start
  49.4 0.9 %shard_map.131 = bf16[128,1024]{1,0:T(8,128)(2,1)} custom-call(bf16[16,104,128]{2,1,0:T(8,128)(2,1)S(1)} %all_to_all.10.received), custom_call_target="tpu_custom_call" | custom-call | flops 67108864 | bytes 1048576 | tf_op jit(solution)/shard_map/pallas_call | solution.py:581
  50.3 0.2 collective-permute-done.other
  50.5 0.7 %shard_map.133 = (f32[1,64]{1,0:T(1,128)}, f32[1,64]{1,0:T(1,128)}, f32[64,64]{1,0:T(8,128)}, f32[64,1024]{1,0:T(8,128)}) custom-call(f32[8,128]{1,0:T(8,128)S(1)} %get-tuple-element.15.joined, bf16[32,1152]{1,0:T(8,128)(2,1)S(1)} %get-tuple-element.16.mine, bf16[32,1152]{1,0:T(8,128)(2,1)S(1)} %collective-permute-done.other), custom_call_target="tpu_custom_call" | custom-call | bytes 1048576 | tf_op jit(solution)/shard_map/pallas_call | solution.py:582
Async XLA Ops:
  2.7 21.8 %all-to-all-start = ((bf16[16,128,128]{2,1,0:T(8,128)(2,1)}), bf16[16,128,128]{2,1,0:T(8,128)(2,1)S(1)}, u32[]{:S(2)}, u32[]{:S(2)}) async-start(bf16[16,128,128]{2,1,0:T(8,128)(2,1)} %shard_map.128), calls=%async_computation | async-start | bytes 1048576 | tf_op jit(solution)/shard_map/all_to_all | solution.py:570
  10.1 14.5 %copy-start = (bf16[512,768]{1,0:T(8,128)(2,1)S(1)}, bf16[512,768]{1,0:T(8,128)(2,1)}, u32[]{:S(2)}) copy-start(bf16[512,768]{1,0:T(8,128)(2,1)} %constant.4.clone.matrix) | copy-start | bytes 2359300
  10.1 14.5 %copy-start.1 = (f32[256,128]{1,0:T(8,128)S(1)}, f32[256,128]{1,0:T(8,128)}, u32[]{:S(2)}) copy-start(f32[256,128]{1,0:T(8,128)} %constant.5.clone.twiddle) | copy-start | bytes 393220
  49.2 1.3 %collective-permute-start = (bf16[32,1152]{1,0:T(8,128)(2,1)S(1)}, bf16[32,1152]{1,0:T(8,128)(2,1)S(1)}, u32[]{:S(2)}, u32[]{:S(2)}) collective-permute-start(bf16[32,1152]{1,0:T(8,128)(2,1)S(1)} %get-tuple-element.16.mine), channel_id=1, source_target_pairs={{0,1},{1,0},{2,3},{3,2},{4,5},{5,4},{6,7},{7,6},{8,9},{9,8},{10,11... | collective-permute-start | bytes 221192 | tf_op jit(solution)/shard_map/ppermute | solution.py:580

commit v6 on v5

--- a/solution.py
+++ b/solution.py
@@ -177,11 +177,15 @@
     return pltpu.roll(value, 64, 1)
 
 
-def fetch(sources, buffers, semaphores):
-    copies = [
+def copies_of(sources, buffers, semaphores):
+    return [
         pltpu.make_async_copy(source, buffer, semaphores.at[index])
         for index, (source, buffer) in enumerate(zip(sources, buffers))
     ]
+
+
+def fetch(sources, buffers, semaphores):
+    copies = copies_of(sources, buffers, semaphores)
     for copy in copies:
         copy.start()
     return copies
@@ -235,7 +239,7 @@
 
 def kernel_spectrum_kernel(
     length, rates, w_first, w_bias, w_mid, w_last, matrix, twiddle, wide_hbm, narrow_hbm,
-    spectrum, slope_two, consts, one, two, mid_back, last_back, semaphores, taps, stage,
+    spectrum, slope_two, slope_one, consts, one, two, mid_back, last_back, semaphores, taps, stage,
 ):
     inner = 2 * length // RADIX
     low_half = low_lanes(inner)
@@ -266,6 +270,7 @@
         pre_one = scaled * first + bias
         gate_one = 1.0 / (1.0 + jnp.exp(-pre_one))
         hidden_one = pre_one * gate_one
+        slope_one[rows, :] = gate_one * (1.0 + pre_one * (1.0 - gate_one))
         pre_two = dot_pair(pair_lanes(hidden_one), mid)
         gate_two = 1.0 / (1.0 + jnp.exp(-pre_two))
         hidden_two = pre_two * gate_two
@@ -280,7 +285,7 @@
 
     lax.fori_loop(0, HALF, block, 0, unroll=UNROLL_ROWS)
     places = passed_places(length, wide_hbm, narrow_hbm)
-    held = (slope_two, consts, one, two, mid_back, last_back)
+    held = (slope_two, slope_one, consts, one, two, mid_back, last_back)
     copies = fetch(held, places[1:], semaphores)
     residues_to_scratch(lambda start: taps[pl.ds(start, CHUNK), :], twiddle, stage, inner)
 
@@ -300,17 +305,22 @@
 
 def gradient_kernel(
     length, signal, wide_hbm, narrow_hbm, matrix, twiddle, out,
-    spectrum, slope_two, consts, one, two, mid_back, last_back, semaphores, stage, back_ref, slopes,
-    pre, decay,
+    spectrum, slope_two, slope_one, consts, one, two, mid_back, last_back, semaphores, stage, back_ref,
+    slopes, pre, decay,
 ):
     padded = 2 * length
     inner = padded // RADIX
     low_half = low_lanes(inner)
-    held = (spectrum, slope_two, consts, one, two, mid_back, last_back)
-    copies = fetch(passed_places(length, wide_hbm, narrow_hbm), held, semaphores)
+    held = (spectrum, slope_two, slope_one, consts, one, two, mid_back, last_back)
+    copies = copies_of(passed_places(length, wide_hbm, narrow_hbm), held, semaphores)
+    first_needed, needed_later = (copies[0], copies[3]), copies[1:3] + copies[4:]
+    for copy in first_needed:
+        copy.start()
     residues_to_scratch(
         lambda start: signal[pl.ds(start, CHUNK), :].astype(F32), twiddle, stage, inner
     )
+    for copy in needed_later:
+        copy.start()
 
     def analyse(j, carry):
         real, imag = inner_dft(stage[j], matrix, inner, 1)
@@ -319,7 +329,8 @@
         return carry
 
     lax.fori_loop(0, HALF + 1, analyse, 0, unroll=UNROLL_BIN)
-    copies[0].wait()
+    for copy in first_needed:
+        copy.wait()
 
     def transform(j, carry):
         real, imag = back_ref[j, :, 0:128], back_ref[j, :, 128:256]
@@ -341,8 +352,6 @@
         return carry
 
     lax.fori_loop(0, HALF + 1, transform, 0, unroll=UNROLL_BIN)
-    for copy in copies[1:]:
-        copy.wait()
     rate, scale, first, bias = (consts[index : index + 1, :] for index in range(4))
     place = lax.broadcasted_iota(jnp.int32, (inner, 128), 0)
     near = jnp.where(low_half, place, inner - 1 - place).astype(F32)
@@ -380,9 +389,10 @@
         return carry
 
     lax.fori_loop(0, inner // CHUNK, unspread, 0, unroll=UNROLL_CHUNK)
+    for copy in needed_later:
+        copy.wait()
     local_rows = 128
     half_rows = local_rows // 2
-    rise = jnp.exp(place.astype(F32) * (first * (-1.0 / length)))
 
     def block(q, carry):
         first_sum, bias_sum = carry
@@ -399,10 +409,7 @@
         pre[rows, :] = pre_two
         base = jnp.where(low_row, start, start - length)
         scaled = (place + base).astype(F32) * (1.0 / length)
-        before = scaled * first + bias
-        gate = 1.0 / (1.0 + rise * jnp.exp(-(base.astype(F32) * (1.0 / length) * first + bias)))
-        slope_one = gate * (1.0 + before * (1.0 - gate))
-        pre_one = dot_pair(pre_two, mid_back[...]) * slope_one
+        pre_one = dot_pair(pre_two, mid_back[...]) * slope_one[rows, :]
         first_sum = first_sum + jnp.sum((pre_one * scaled).reshape(inner // 8, 8, 128), axis=0)
         bias_sum = bias_sum + jnp.sum(pre_one.reshape(inner // 8, 8, 128), axis=0)
         return first_sum, bias_sum
@@ -499,20 +506,21 @@
 
 def passed_places(length, wide, narrow):
     bins = 2 * (HALF + 1) * (2 * length // RADIX)
-    parts = [wide.at[pl.ds(0, bins), :], wide.at[pl.ds(bins, length), :]]
-    parts += [wide.at[pl.ds(bins + length, 8), :]]
+    parts = [wide.at[pl.ds(0, bins), :]]
+    parts += [wide.at[pl.ds(bins + index * length, length), :] for index in range(2)]
+    parts += [wide.at[pl.ds(bins + 2 * length, 8), :]]
     parts += [narrow.at[pl.ds(256 * index, 256), :] for index in range(2)]
     return parts + [narrow.at[pl.ds(512, 256), pl.ds(256 * index, 256)] for index in range(2)]
 
 
 def passed_shapes(length):
     bins = 2 * (HALF + 1) * (2 * length // RADIX)
-    return [shape((bins + length + 8, 128), F32), shape((512 + 256, length), BF16)]
+    return [shape((bins + 2 * length + 8, 128), F32), shape((512 + 256, length), BF16)]
 
 
 def held_arrays(length):
     bins = 2 * (HALF + 1) * (2 * length // RADIX)
-    held = [pltpu.VMEM((rows, 128), F32) for rows in (bins, length, 8)]
+    held = [pltpu.VMEM((rows, 128), F32) for rows in (bins, length, length, 8)]
     held += [pltpu.VMEM((256, length), BF16)] * 2 + [pltpu.VMEM((256, 256), BF16)] * 2
     return held + [pltpu.SemaphoreType.DMA((len(held),))]
 

time: 51.6 us -> 50.8 us (0.984)
    pallas_call x1, Pallas kernels: 7.87 us -> 7.02 us  [gradient_call(): call(functools.partial(gradient_kernel, length), shape((length // local_r...]
  transfers between devices with their start and end apart: 2 -> 2, of which waited for: 2 -> 2; matrix products, arithmetic and copies ran while one was open for 0% -> 0% of each run, Pallas kernels for 17% -> 18%
where the time goes in v6:
time: 50.8 us; the launch traced here: 50.4 us
  Pallas kernels  19.3 us (38%)
  blocking collectives  16.6 us (33%)
  starting transfers between devices  7.51 us (15%)
  waiting for transfers between devices  6.28 us (12%)
  between operations  0.68 us (1%)
    all_to_all x1, blocking collectives, by_channels(): lax.all_to_all(sent, 'ctx', split_axis=0, concat_axis=0, tiled=True)  16.6 us
    pallas_call x1, Pallas kernels, spectrum_call(): call(functools.partial(kernel_spectrum_kernel, length), passed_shapes(len...  8.4 us
    all_to_all x1, starting transfers between devices, by_channels(): lax.all_to_all(packed, 'ctx', split_axis=0, concat_axis=0, tiled=True)  7.37 us
    pallas_call x1, Pallas kernels, gradient_call(): call(functools.partial(gradient_kernel, length), shape((length // local_r...  7.02 us
    all_to_all x1, waiting for transfers between devices, by_channels(): lax.all_to_all(packed, 'ctx', split_axis=0, concat_axis=0, tiled=True)  6.03 us
    pallas_call x1, Pallas kernels, by_channels(): call(pack_kernel, shape((devices, local_rows, 128), BF16), scratch=[pltpu...  2.1 us
  transfers between devices with their start and end apart: 2, of which 2 were waited for; matrix products, arithmetic and copies ran while one was open for 0% of the time, Pallas kernels for 18%

profile of v6, /device:TPU:0, one launch (start us, length us, event | category | flops | bytes accessed | tf_op | source)
XLA Modules:
  0.0 50.4 jit_solution(15086567739990351227)
XLA Ops:
  0.6 2.1 %shard_map.128 = bf16[16,128,128]{2,1,0:T(8,128)(2,1)} custom-call(bf16[128,1024]{1,0:T(8,128)(2,1)} %tokens_hbm.1, bf16[128,1024]{1,0:T(8,128)(2,1)} %cotan_hbm.1), custom_call_target="tpu_custom_call" | custom-call | bytes 1048576 | tf_op jit(solution)/shard_map/pallas_call | solution.py:565
  2.7 7.4 %all-to-all-start = ((bf16[16,128,128]{2,1,0:T(8,128)(2,1)}), bf16[16,128,128]{2,1,0:T(8,128)(2,1)S(1)}, u32[]{:S(2)}, u32[]{:S(2)}) async-start(bf16[16,128,128]{2,1,0:T(8,128)(2,1)} %shard_map.128), calls=%async_computation | async-start | bytes 1048576 | tf_op jit(solution)/shard_map/all_to_all | solution.py:578
  10.1 0.0 copy-start
  10.1 0.0 copy-start.1
  10.1 8.4 %shard_map.129 = (f32[8712,128]{1,0:T(8,128)}, bf16[768,2048]{1,0:T(8,128)(2,1)}) custom-call(f32[1,1024]{1,0:T(1,128)} %bitcast.7, f32[1,64]{1,0:T(1,128)} %bitcast.8, f32[1,64]{1,0:T(1,128)} %bitcast.9, f32[64,64]{1,0:T(8,128)} %w_mid.1, f32[64,1024]{1,0:T(8,128)} %w_last.1, bf16[512,768]{1,0:T(8,128)(2,1)} %constant.4.clone.matrix, ...), custom_call_target="tpu_custom_call" | custom-call | flops 4294967296 | bytes 1048576 | tf_op jit(solution)/shard_map/pallas_call | solution.py:530
  18.6 6.0 %all-to-all-done = bf16[16,128,128]{2,1,0:T(8,128)(2,1)S(1)} async-done(((bf16[16,128,128]{2,1,0:T(8,128)(2,1)}), bf16[16,128,128]{2,1,0:T(8,128)(2,1)S(1)}, u32[]{:S(2)}, u32[]{:S(2)}) %all-to-all-start) | async-done | bytes 524320 | tf_op jit(solution)/shard_map/all_to_all | solution.py:578
  24.6 0.0 copy-done
  24.6 0.0 copy-done.1
  24.6 7.0 %shard_map.130 = bf16[16,104,128]{2,1,0:T(8,128)(2,1)S(1)} custom-call(bf16[2048,128]{1,0:T(8,128)(2,1)S(1)} %bitcast.6, f32[8712,128]{1,0:T(8,128)} %get-tuple-element.13.wide_hbm, bf16[768,2048]{1,0:T(8,128)(2,1)} %get-tuple-element.14.narrow_hbm, bf16[512,768]{1,0:T(8,128)(2,1)S(1)} %copy-done, f32[256,128]{1,0:T(8,128)S(1)} %copy-done.1), custom_call_target="tpu_custom_call" | custom-call | flops 8589934592 | bytes 1048576 | tf_op jit(solution)/shard_map/pallas_call | solution.py:544
  31.6 16.6 %all_to_all.10.received = bf16[16,104,128]{2,1,0:T(8,128)(2,1)S(1)} all-to-all(bf16[16,104,128]{2,1,0:T(8,128)(2,1)S(1)} %shard_map.130), channel_id=1, replica_groups=mesh['groups'=2,'ctx'=16] {'ctx'}, dimensions={0} | all-to-all | bytes 851968 | tf_op jit(solution)/shard_map/all_to_all | solution.py:584
  48.2 0.2 shard_map.132
  48.4 0.1 collective-permute-start
  48.6 0.9 %shard_map.131 = bf16[128,1024]{1,0:T(8,128)(2,1)} custom-call(bf16[16,104,128]{2,1,0:T(8,128)(2,1)S(1)} %all_to_all.10.received), custom_call_target="tpu_custom_call" | custom-call | flops 67108864 | bytes 1048576 | tf_op jit(solution)/shard_map/pallas_call | solution.py:589
  49.5 0.2 collective-permute-done.other
  49.7 0.7 %shard_map.133 = (f32[1,64]{1,0:T(1,128)}, f32[1,64]{1,0:T(1,128)}, f32[64,64]{1,0:T(8,128)}, f32[64,1024]{1,0:T(8,128)}) custom-call(f32[8,128]{1,0:T(8,128)S(1)} %get-tuple-element.15.joined, bf16[32,1152]{1,0:T(8,128)(2,1)S(1)} %get-tuple-element.16.mine, bf16[32,1152]{1,0:T(8,128)(2,1)S(1)} %collective-permute-done.other), custom_call_target="tpu_custom_call" | custom-call | bytes 1048576 | tf_op jit(solution)/shard_map/pallas_call | solution.py:590
Async XLA Ops:
  2.7 21.8 %all-to-all-start = ((bf16[16,128,128]{2,1,0:T(8,128)(2,1)}), bf16[16,128,128]{2,1,0:T(8,128)(2,1)S(1)}, u32[]{:S(2)}, u32[]{:S(2)}) async-start(bf16[16,128,128]{2,1,0:T(8,128)(2,1)} %shard_map.128), calls=%async_computation | async-start | bytes 1048576 | tf_op jit(solution)/shard_map/all_to_all | solution.py:578
  10.1 14.5 %copy-start = (bf16[512,768]{1,0:T(8,128)(2,1)S(1)}, bf16[512,768]{1,0:T(8,128)(2,1)}, u32[]{:S(2)}) copy-start(bf16[512,768]{1,0:T(8,128)(2,1)} %constant.4.clone.matrix) | copy-start | bytes 2359300
  10.1 14.5 %copy-start.1 = (f32[256,128]{1,0:T(8,128)S(1)}, f32[256,128]{1,0:T(8,128)}, u32[]{:S(2)}) copy-start(f32[256,128]{1,0:T(8,128)} %constant.5.clone.twiddle) | copy-start | bytes 393220
  48.4 1.3 %collective-permute-start = (bf16[32,1152]{1,0:T(8,128)(2,1)S(1)}, bf16[32,1152]{1,0:T(8,128)(2,1)S(1)}, u32[]{:S(2)}, u32[]{:S(2)}) collective-permute-start(bf16[32,1152]{1,0:T(8,128)(2,1)S(1)} %get-tuple-element.16.mine), channel_id=1, source_target_pairs={{0,1},{1,0},{2,3},{3,2},{4,5},{5,4},{6,7},{7,6},{8,9},{9,8},{10,11... | collective-permute-start | bytes 221192 | tf_op jit(solution)/shard_map/ppermute | solution.py:588

commit v7 on v6

--- a/solution.py
+++ b/solution.py
@@ -161,12 +161,15 @@
 
 
 def inner_dft(stacked, matrix, inner, direction):
-    product = dot(matrix[...], stacked)
-    cos_real, cos_imag = product[:inner, :128], product[:inner, 128:]
-    sin_real, sin_imag = product[inner:, :128], product[inner:, 128:]
-    if direction > 0:
-        return cos_real + sin_imag, cos_imag - sin_real
-    return cos_real - sin_imag, cos_imag + sin_real
+    reals, imags = [], []
+    for row in range(0, inner, 128):
+        cosines = dot(matrix[row : row + 128, :], stacked)
+        sines = dot(matrix[inner + row : inner + row + 128, :], stacked)
+        cos_real, cos_imag = cosines[:, :128], cosines[:, 128:]
+        sin_real, sin_imag = sines[:, :128], sines[:, 128:]
+        reals.append(cos_real + sin_imag if direction > 0 else cos_real - sin_imag)
+        imags.append(cos_imag - sin_real if direction > 0 else cos_imag + sin_real)
+    return jnp.concatenate(reals, axis=0), jnp.concatenate(imags, axis=0)
 
 
 def low_lanes(rows):
@@ -395,7 +398,6 @@
     half_rows = local_rows // 2
 
     def block(q, carry):
-        first_sum, bias_sum = carry
         start = pl.multiple_of(q * inner, inner)
         rows = pl.ds(start, inner)
         for part in range(inner // local_rows):
@@ -405,20 +407,28 @@
             out[q * (inner // local_rows) + part, 0:half_rows, :] = jnp.where(
                 low_half[:half_rows], upper, swap(lower)
             ).astype(BF16)
-        pre_two = pair_lanes(dot_pair(slopes[rows, :], last_back[...]) * slope_two[rows, :])
-        pre[rows, :] = pre_two
+        return carry
+
+    pre[...] = pair_lanes(dot_pair(slopes[...], last_back[...]) * slope_two[...])
+    lax.fori_loop(0, HALF, block, 0, unroll=UNROLL_ROWS)
+    last_product = dot(two[...], slopes[...])
+
+    def first_layer(q, carry):
+        first_sum, bias_sum = carry
+        start = pl.multiple_of(q * inner, inner)
+        rows = pl.ds(start, inner)
         base = jnp.where(low_row, start, start - length)
         scaled = (place + base).astype(F32) * (1.0 / length)
-        pre_one = dot_pair(pre_two, mid_back[...]) * slope_one[rows, :]
+        pre_one = dot_pair(pre[rows, :], mid_back[...]) * slope_one[rows, :]
         first_sum = first_sum + jnp.sum((pre_one * scaled).reshape(inner // 8, 8, 128), axis=0)
         bias_sum = bias_sum + jnp.sum(pre_one.reshape(inner // 8, 8, 128), axis=0)
         return first_sum, bias_sum
 
     none = jnp.zeros((8, 128), F32)
-    first_sum, bias_sum = lax.fori_loop(0, HALF, block, (none, none), unroll=UNROLL_ROWS)
+    first_sum, bias_sum = lax.fori_loop(0, HALF, first_layer, (none, none), unroll=UNROLL_ROWS)
     last_sum, mid_sum = (
         product[0:128, 0:128] + (product[0:128, 128:256] + product[128:256, 0:128])
-        for product in (dot(two[...], slopes[...]), dot(one[...], pre[...]))
+        for product in (last_product, dot(one[...], pre[...]))
     )
     low_32 = low_lanes(32)
     grad_last = last_sum[0:64] + swap(last_sum[64:128])

time: 50.8 us -> 50.3 us (level)
  Pallas kernels: 19.3 us -> 18.5 us
where the time goes in v7:
time: 50.3 us; the launch traced here: 50 us
  Pallas kernels  18.5 us (37%)
  blocking collectives  16.6 us (33%)
  starting transfers between devices  7.51 us (15%)
  waiting for transfers between devices  6.64 us (13%)
  between operations  0.68 us (1%)
    all_to_all x1, blocking collectives, by_channels(): lax.all_to_all(sent, 'ctx', split_axis=0, concat_axis=0, tiled=True)  16.6 us
    pallas_call x1, Pallas kernels, spectrum_call(): call(functools.partial(kernel_spectrum_kernel, length), passed_shapes(len...  8.04 us
    all_to_all x1, starting transfers between devices, by_channels(): lax.all_to_all(packed, 'ctx', split_axis=0, concat_axis=0, tiled=True)  7.37 us
    pallas_call x1, Pallas kernels, gradient_call(): call(functools.partial(gradient_kernel, length), shape((length // local_r...  6.56 us
    all_to_all x1, waiting for transfers between devices, by_channels(): lax.all_to_all(packed, 'ctx', split_axis=0, concat_axis=0, tiled=True)  6.39 us
    pallas_call x1, Pallas kernels, by_channels(): call(pack_kernel, shape((devices, local_rows, 128), BF16), scratch=[pltpu...  2.1 us
  transfers between devices with their start and end apart: 2, of which 2 were waited for; matrix products, arithmetic and copies ran while one was open for 0% of the time, Pallas kernels for 18%

profile of v7, /device:TPU:0, one launch (start us, length us, event | category | flops | bytes accessed | tf_op | source)
XLA Modules:
  0.0 50.0 jit_solution(17888260118609473447)
XLA Ops:
  0.6 2.1 %shard_map.128 = bf16[16,128,128]{2,1,0:T(8,128)(2,1)} custom-call(bf16[128,1024]{1,0:T(8,128)(2,1)} %tokens_hbm.1, bf16[128,1024]{1,0:T(8,128)(2,1)} %cotan_hbm.1), custom_call_target="tpu_custom_call" | custom-call | bytes 1048576 | tf_op jit(solution)/shard_map/pallas_call | solution.py:575
  2.7 7.4 %all-to-all-start = ((bf16[16,128,128]{2,1,0:T(8,128)(2,1)}), bf16[16,128,128]{2,1,0:T(8,128)(2,1)S(1)}, u32[]{:S(2)}, u32[]{:S(2)}) async-start(bf16[16,128,128]{2,1,0:T(8,128)(2,1)} %shard_map.128), calls=%async_computation | async-start | bytes 1048576 | tf_op jit(solution)/shard_map/all_to_all | solution.py:588
  10.1 0.0 copy-start
  10.1 0.0 copy-start.1
  10.1 8.0 %shard_map.129 = (f32[8712,128]{1,0:T(8,128)}, bf16[768,2048]{1,0:T(8,128)(2,1)}) custom-call(f32[1,1024]{1,0:T(1,128)} %bitcast.7, f32[1,64]{1,0:T(1,128)} %bitcast.8, f32[1,64]{1,0:T(1,128)} %bitcast.9, f32[64,64]{1,0:T(8,128)} %w_mid.1, f32[64,1024]{1,0:T(8,128)} %w_last.1, bf16[512,768]{1,0:T(8,128)(2,1)} %constant.4.clone.matrix, ...), custom_call_target="tpu_custom_call" | custom-call | flops 4294967296 | bytes 1048576 | tf_op jit(solution)/shard_map/pallas_call | solution.py:540
  18.2 6.4 %all-to-all-done = bf16[16,128,128]{2,1,0:T(8,128)(2,1)S(1)} async-done(((bf16[16,128,128]{2,1,0:T(8,128)(2,1)}), bf16[16,128,128]{2,1,0:T(8,128)(2,1)S(1)}, u32[]{:S(2)}, u32[]{:S(2)}) %all-to-all-start) | async-done | bytes 524320 | tf_op jit(solution)/shard_map/all_to_all | solution.py:588
  24.6 0.0 copy-done
  24.6 0.0 copy-done.1
  24.6 6.6 %shard_map.130 = bf16[16,104,128]{2,1,0:T(8,128)(2,1)S(1)} custom-call(bf16[2048,128]{1,0:T(8,128)(2,1)S(1)} %bitcast.6, f32[8712,128]{1,0:T(8,128)} %get-tuple-element.13.wide_hbm, bf16[768,2048]{1,0:T(8,128)(2,1)} %get-tuple-element.14.narrow_hbm, bf16[512,768]{1,0:T(8,128)(2,1)S(1)} %copy-done, f32[256,128]{1,0:T(8,128)S(1)} %copy-done.1), custom_call_target="tpu_custom_call" | custom-call | flops 8589934592 | bytes 1048576 | tf_op jit(solution)/shard_map/pallas_call | solution.py:554
  31.2 16.6 %all_to_all.10.received = bf16[16,104,128]{2,1,0:T(8,128)(2,1)S(1)} all-to-all(bf16[16,104,128]{2,1,0:T(8,128)(2,1)S(1)} %shard_map.130), channel_id=1, replica_groups=mesh['groups'=2,'ctx'=16] {'ctx'}, dimensions={0} | all-to-all | bytes 851968 | tf_op jit(solution)/shard_map/all_to_all | solution.py:594
  47.8 0.2 shard_map.132
  47.9 0.1 collective-permute-start
  48.1 0.9 %shard_map.131 = bf16[128,1024]{1,0:T(8,128)(2,1)} custom-call(bf16[16,104,128]{2,1,0:T(8,128)(2,1)S(1)} %all_to_all.10.received), custom_call_target="tpu_custom_call" | custom-call | flops 67108864 | bytes 1048576 | tf_op jit(solution)/shard_map/pallas_call | solution.py:599
  49.0 0.2 collective-permute-done.other
  49.2 0.7 %shard_map.133 = (f32[1,64]{1,0:T(1,128)}, f32[1,64]{1,0:T(1,128)}, f32[64,64]{1,0:T(8,128)}, f32[64,1024]{1,0:T(8,128)}) custom-call(f32[8,128]{1,0:T(8,128)S(1)} %get-tuple-element.15.joined, bf16[32,1152]{1,0:T(8,128)(2,1)S(1)} %get-tuple-element.16.mine, bf16[32,1152]{1,0:T(8,128)(2,1)S(1)} %collective-permute-done.other), custom_call_target="tpu_custom_call" | custom-call | bytes 1048576 | tf_op jit(solution)/shard_map/pallas_call | solution.py:600
Async XLA Ops:
  2.7 21.8 %all-to-all-start = ((bf16[16,128,128]{2,1,0:T(8,128)(2,1)}), bf16[16,128,128]{2,1,0:T(8,128)(2,1)S(1)}, u32[]{:S(2)}, u32[]{:S(2)}) async-start(bf16[16,128,128]{2,1,0:T(8,128)(2,1)} %shard_map.128), calls=%async_computation | async-start | bytes 1048576 | tf_op jit(solution)/shard_map/all_to_all | solution.py:588
  10.1 14.5 %copy-start = (bf16[512,768]{1,0:T(8,128)(2,1)S(1)}, bf16[512,768]{1,0:T(8,128)(2,1)}, u32[]{:S(2)}) copy-start(bf16[512,768]{1,0:T(8,128)(2,1)} %constant.4.clone.matrix) | copy-start | bytes 2359300
  10.1 14.5 %copy-start.1 = (f32[256,128]{1,0:T(8,128)S(1)}, f32[256,128]{1,0:T(8,128)}, u32[]{:S(2)}) copy-start(f32[256,128]{1,0:T(8,128)} %constant.5.clone.twiddle) | copy-start | bytes 393220
  47.9 1.3 %collective-permute-start = (bf16[32,1152]{1,0:T(8,128)(2,1)S(1)}, bf16[32,1152]{1,0:T(8,128)(2,1)S(1)}, u32[]{:S(2)}, u32[]{:S(2)}) collective-permute-start(bf16[32,1152]{1,0:T(8,128)(2,1)S(1)} %get-tuple-element.16.mine), channel_id=1, source_target_pairs={{0,1},{1,0},{2,3},{3,2},{4,5},{5,4},{6,7},{7,6},{8,9},{9,8},{10,11... | collective-permute-start | bytes 221192 | tf_op jit(solution)/shard_map/ppermute | solution.py:598

commit v8 on v7

--- a/solution.py
+++ b/solution.py
@@ -11,8 +11,8 @@
 
 RADIX = 16
 HALF = RADIX // 2
-CHUNK = 32
-UNROLL_CHUNK = 8
+CHUNK = 64
+UNROLL_CHUNK = 4
 UNROLL_BIN = 9
 UNROLL_ROWS = 8
 PACK_PARTS = 4

time: 50.3 us -> 50.3 us (level)
  no operation moved by 1% of the time
where the time goes in v8:
time: 50.3 us; the launch traced here: 50 us
  Pallas kernels  18.5 us (37%)
  blocking collectives  16.6 us (33%)
  starting transfers between devices  7.51 us (15%)
  waiting for transfers between devices  6.62 us (13%)
  between operations  0.68 us (1%)
    all_to_all x1, blocking collectives, by_channels(): lax.all_to_all(sent, 'ctx', split_axis=0, concat_axis=0, tiled=True)  16.6 us
    pallas_call x1, Pallas kernels, spectrum_call(): call(functools.partial(kernel_spectrum_kernel, length), passed_shapes(len...  8.06 us
    all_to_all x1, starting transfers between devices, by_channels(): lax.all_to_all(packed, 'ctx', split_axis=0, concat_axis=0, tiled=True)  7.37 us
    pallas_call x1, Pallas kernels, gradient_call(): call(functools.partial(gradient_kernel, length), shape((length // local_r...  6.55 us
    all_to_all x1, waiting for transfers between devices, by_channels(): lax.all_to_all(packed, 'ctx', split_axis=0, concat_axis=0, tiled=True)  6.38 us
    pallas_call x1, Pallas kernels, by_channels(): call(pack_kernel, shape((devices, local_rows, 128), BF16), scratch=[pltpu...  2.1 us
  transfers between devices with their start and end apart: 2, of which 2 were waited for; matrix products, arithmetic and copies ran while one was open for 0% of the time, Pallas kernels for 18%

profile of v8, /device:TPU:0, one launch (start us, length us, event | category | flops | bytes accessed | tf_op | source)
XLA Modules:
  0.0 50.0 jit_solution(6841840804904391988)
XLA Ops:
  0.6 2.1 %shard_map.128 = bf16[16,128,128]{2,1,0:T(8,128)(2,1)} custom-call(bf16[128,1024]{1,0:T(8,128)(2,1)} %tokens_hbm.1, bf16[128,1024]{1,0:T(8,128)(2,1)} %cotan_hbm.1), custom_call_target="tpu_custom_call" | custom-call | bytes 1048576 | tf_op jit(solution)/shard_map/pallas_call | solution.py:575
  2.7 7.4 %all-to-all-start = ((bf16[16,128,128]{2,1,0:T(8,128)(2,1)}), bf16[16,128,128]{2,1,0:T(8,128)(2,1)S(1)}, u32[]{:S(2)}, u32[]{:S(2)}) async-start(bf16[16,128,128]{2,1,0:T(8,128)(2,1)} %shard_map.128), calls=%async_computation | async-start | bytes 1048576 | tf_op jit(solution)/shard_map/all_to_all | solution.py:588
  10.1 0.0 copy-start
  10.1 0.0 copy-start.1
  10.1 8.1 %shard_map.129 = (f32[8712,128]{1,0:T(8,128)}, bf16[768,2048]{1,0:T(8,128)(2,1)}) custom-call(f32[1,1024]{1,0:T(1,128)} %bitcast.7, f32[1,64]{1,0:T(1,128)} %bitcast.8, f32[1,64]{1,0:T(1,128)} %bitcast.9, f32[64,64]{1,0:T(8,128)} %w_mid.1, f32[64,1024]{1,0:T(8,128)} %w_last.1, bf16[512,768]{1,0:T(8,128)(2,1)} %constant.4.clone.matrix, ...), custom_call_target="tpu_custom_call" | custom-call | flops 4294967296 | bytes 1048576 | tf_op jit(solution)/shard_map/pallas_call | solution.py:540
  18.2 6.4 %all-to-all-done = bf16[16,128,128]{2,1,0:T(8,128)(2,1)S(1)} async-done(((bf16[16,128,128]{2,1,0:T(8,128)(2,1)}), bf16[16,128,128]{2,1,0:T(8,128)(2,1)S(1)}, u32[]{:S(2)}, u32[]{:S(2)}) %all-to-all-start) | async-done | bytes 524320 | tf_op jit(solution)/shard_map/all_to_all | solution.py:588
  24.6 0.0 copy-done
  24.6 0.0 copy-done.1
  24.6 6.5 %shard_map.130 = bf16[16,104,128]{2,1,0:T(8,128)(2,1)S(1)} custom-call(bf16[2048,128]{1,0:T(8,128)(2,1)S(1)} %bitcast.6, f32[8712,128]{1,0:T(8,128)} %get-tuple-element.13.wide_hbm, bf16[768,2048]{1,0:T(8,128)(2,1)} %get-tuple-element.14.narrow_hbm, bf16[512,768]{1,0:T(8,128)(2,1)S(1)} %copy-done, f32[256,128]{1,0:T(8,128)S(1)} %copy-done.1), custom_call_target="tpu_custom_call" | custom-call | flops 8589934592 | bytes 1048576 | tf_op jit(solution)/shard_map/pallas_call | solution.py:554
  31.1 16.6 %all_to_all.10.received = bf16[16,104,128]{2,1,0:T(8,128)(2,1)S(1)} all-to-all(bf16[16,104,128]{2,1,0:T(8,128)(2,1)S(1)} %shard_map.130), channel_id=1, replica_groups=mesh['groups'=2,'ctx'=16] {'ctx'}, dimensions={0} | all-to-all | bytes 851968 | tf_op jit(solution)/shard_map/all_to_all | solution.py:594
  47.8 0.2 shard_map.132
  47.9 0.1 collective-permute-start
  48.1 0.9 %shard_map.131 = bf16[128,1024]{1,0:T(8,128)(2,1)} custom-call(bf16[16,104,128]{2,1,0:T(8,128)(2,1)S(1)} %all_to_all.10.received), custom_call_target="tpu_custom_call" | custom-call | flops 67108864 | bytes 1048576 | tf_op jit(solution)/shard_map/pallas_call | solution.py:599
  49.0 0.2 collective-permute-done.other
  49.2 0.7 %shard_map.133 = (f32[1,64]{1,0:T(1,128)}, f32[1,64]{1,0:T(1,128)}, f32[64,64]{1,0:T(8,128)}, f32[64,1024]{1,0:T(8,128)}) custom-call(f32[8,128]{1,0:T(8,128)S(1)} %get-tuple-element.15.joined, bf16[32,1152]{1,0:T(8,128)(2,1)S(1)} %get-tuple-element.16.mine, bf16[32,1152]{1,0:T(8,128)(2,1)S(1)} %collective-permute-done.other), custom_call_target="tpu_custom_call" | custom-call | bytes 1048576 | tf_op jit(solution)/shard_map/pallas_call | solution.py:600
Async XLA Ops:
  2.7 21.8 %all-to-all-start = ((bf16[16,128,128]{2,1,0:T(8,128)(2,1)}), bf16[16,128,128]{2,1,0:T(8,128)(2,1)S(1)}, u32[]{:S(2)}, u32[]{:S(2)}) async-start(bf16[16,128,128]{2,1,0:T(8,128)(2,1)} %shard_map.128), calls=%async_computation | async-start | bytes 1048576 | tf_op jit(solution)/shard_map/all_to_all | solution.py:588
  10.1 14.5 %copy-start = (bf16[512,768]{1,0:T(8,128)(2,1)S(1)}, bf16[512,768]{1,0:T(8,128)(2,1)}, u32[]{:S(2)}) copy-start(bf16[512,768]{1,0:T(8,128)(2,1)} %constant.4.clone.matrix) | copy-start | bytes 2359300
  10.1 14.5 %copy-start.1 = (f32[256,128]{1,0:T(8,128)S(1)}, f32[256,128]{1,0:T(8,128)}, u32[]{:S(2)}) copy-start(f32[256,128]{1,0:T(8,128)} %constant.5.clone.twiddle) | copy-start | bytes 393220
  47.9 1.3 %collective-permute-start = (bf16[32,1152]{1,0:T(8,128)(2,1)S(1)}, bf16[32,1152]{1,0:T(8,128)(2,1)S(1)}, u32[]{:S(2)}, u32[]{:S(2)}) collective-permute-start(bf16[32,1152]{1,0:T(8,128)(2,1)S(1)} %get-tuple-element.16.mine), channel_id=1, source_target_pairs={{0,1},{1,0},{2,3},{3,2},{4,5},{5,4},{6,7},{7,6},{8,9},{9,8},{10,11... | collective-permute-start | bytes 221192 | tf_op jit(solution)/shard_map/ppermute | solution.py:598

commit v9 on v8

--- a/solution.py
+++ b/solution.py
@@ -15,7 +15,7 @@
 UNROLL_CHUNK = 4
 UNROLL_BIN = 9
 UNROLL_ROWS = 8
-PACK_PARTS = 4
+PACK_PARTS = 2
 FIRST_LIMIT = 56
 SECOND_LIMIT = 50
 F32 = jnp.float32

time: 50.3 us -> 50.2 us (level)
  no operation moved by 1% of the time
where the time goes in v9:
time: 50.2 us; the launch traced here: 49.9 us
  Pallas kernels  18.5 us (37%)
  blocking collectives  16.6 us (33%)
  starting transfers between devices  7.51 us (15%)
  waiting for transfers between devices  6.62 us (13%)
  between operations  0.68 us (1%)
    all_to_all x1, blocking collectives, by_channels(): lax.all_to_all(sent, 'ctx', split_axis=0, concat_axis=0, tiled=True)  16.6 us
    pallas_call x1, Pallas kernels, spectrum_call(): call(functools.partial(kernel_spectrum_kernel, length), passed_shapes(len...  8.06 us
    all_to_all x1, starting transfers between devices, by_channels(): lax.all_to_all(packed, 'ctx', split_axis=0, concat_axis=0, tiled=True)  7.37 us
    pallas_call x1, Pallas kernels, gradient_call(): call(functools.partial(gradient_kernel, length), shape((length // local_r...  6.55 us
    all_to_all x1, waiting for transfers between devices, by_channels(): lax.all_to_all(packed, 'ctx', split_axis=0, concat_axis=0, tiled=True)  6.38 us
    pallas_call x1, Pallas kernels, by_channels(): call(pack_kernel, shape((devices, local_rows, 128), BF16), scratch=[pltpu...  2.06 us
  transfers between devices with their start and end apart: 2, of which 2 were waited for; matrix products, arithmetic and copies ran while one was open for 0% of the time, Pallas kernels for 18%

profile of v9, /device:TPU:0, one launch (start us, length us, event | category | flops | bytes accessed | tf_op | source)
XLA Modules:
  0.0 49.9 jit_solution(7876280860180247391)
XLA Ops:
  0.6 2.1 %shard_map.128 = bf16[16,128,128]{2,1,0:T(8,128)(2,1)} custom-call(bf16[128,1024]{1,0:T(8,128)(2,1)} %tokens_hbm.1, bf16[128,1024]{1,0:T(8,128)(2,1)} %cotan_hbm.1), custom_call_target="tpu_custom_call" | custom-call | bytes 1048576 | tf_op jit(solution)/shard_map/pallas_call | solution.py:575
  2.7 7.4 %all-to-all-start = ((bf16[16,128,128]{2,1,0:T(8,128)(2,1)}), bf16[16,128,128]{2,1,0:T(8,128)(2,1)S(1)}, u32[]{:S(2)}, u32[]{:S(2)}) async-start(bf16[16,128,128]{2,1,0:T(8,128)(2,1)} %shard_map.128), calls=%async_computation | async-start | bytes 1048576 | tf_op jit(solution)/shard_map/all_to_all | solution.py:588
  10.1 0.0 copy-start
  10.1 0.0 copy-start.1
  10.1 8.1 %shard_map.129 = (f32[8712,128]{1,0:T(8,128)}, bf16[768,2048]{1,0:T(8,128)(2,1)}) custom-call(f32[1,1024]{1,0:T(1,128)} %bitcast.7, f32[1,64]{1,0:T(1,128)} %bitcast.8, f32[1,64]{1,0:T(1,128)} %bitcast.9, f32[64,64]{1,0:T(8,128)} %w_mid.1, f32[64,1024]{1,0:T(8,128)} %w_last.1, bf16[512,768]{1,0:T(8,128)(2,1)} %constant.4.clone.matrix, ...), custom_call_target="tpu_custom_call" | custom-call | flops 4294967296 | bytes 1048576 | tf_op jit(solution)/shard_map/pallas_call | solution.py:540
  18.2 6.4 %all-to-all-done = bf16[16,128,128]{2,1,0:T(8,128)(2,1)S(1)} async-done(((bf16[16,128,128]{2,1,0:T(8,128)(2,1)}), bf16[16,128,128]{2,1,0:T(8,128)(2,1)S(1)}, u32[]{:S(2)}, u32[]{:S(2)}) %all-to-all-start) | async-done | bytes 524320 | tf_op jit(solution)/shard_map/all_to_all | solution.py:588
  24.5 0.0 copy-done
  24.5 0.0 copy-done.1
  24.6 6.5 %shard_map.130 = bf16[16,104,128]{2,1,0:T(8,128)(2,1)S(1)} custom-call(bf16[2048,128]{1,0:T(8,128)(2,1)S(1)} %bitcast.6, f32[8712,128]{1,0:T(8,128)} %get-tuple-element.13.wide_hbm, bf16[768,2048]{1,0:T(8,128)(2,1)} %get-tuple-element.14.narrow_hbm, bf16[512,768]{1,0:T(8,128)(2,1)S(1)} %copy-done, f32[256,128]{1,0:T(8,128)S(1)} %copy-done.1), custom_call_target="tpu_custom_call" | custom-call | flops 8589934592 | bytes 1048576 | tf_op jit(solution)/shard_map/pallas_call | solution.py:554
  31.1 16.6 %all_to_all.10.received = bf16[16,104,128]{2,1,0:T(8,128)(2,1)S(1)} all-to-all(bf16[16,104,128]{2,1,0:T(8,128)(2,1)S(1)} %shard_map.130), channel_id=1, replica_groups=mesh['groups'=2,'ctx'=16] {'ctx'}, dimensions={0} | all-to-all | bytes 851968 | tf_op jit(solution)/shard_map/all_to_all | solution.py:594
  47.7 0.2 shard_map.132
  47.9 0.1 collective-permute-start
  48.0 0.9 %shard_map.131 = bf16[128,1024]{1,0:T(8,128)(2,1)} custom-call(bf16[16,104,128]{2,1,0:T(8,128)(2,1)S(1)} %all_to_all.10.received), custom_call_target="tpu_custom_call" | custom-call | flops 67108864 | bytes 1048576 | tf_op jit(solution)/shard_map/pallas_call | solution.py:599
  48.9 0.2 collective-permute-done.other
  49.2 0.7 %shard_map.133 = (f32[1,64]{1,0:T(1,128)}, f32[1,64]{1,0:T(1,128)}, f32[64,64]{1,0:T(8,128)}, f32[64,1024]{1,0:T(8,128)}) custom-call(f32[8,128]{1,0:T(8,128)S(1)} %get-tuple-element.15.joined, bf16[32,1152]{1,0:T(8,128)(2,1)S(1)} %get-tuple-element.16.mine, bf16[32,1152]{1,0:T(8,128)(2,1)S(1)} %collective-permute-done.other), custom_call_target="tpu_custom_call" | custom-call | bytes 1048576 | tf_op jit(solution)/shard_map/pallas_call | solution.py:600
Async XLA Ops:
  2.7 21.8 %all-to-all-start = ((bf16[16,128,128]{2,1,0:T(8,128)(2,1)}), bf16[16,128,128]{2,1,0:T(8,128)(2,1)S(1)}, u32[]{:S(2)}, u32[]{:S(2)}) async-start(bf16[16,128,128]{2,1,0:T(8,128)(2,1)} %shard_map.128), calls=%async_computation | async-start | bytes 1048576 | tf_op jit(solution)/shard_map/all_to_all | solution.py:588
  10.1 14.5 %copy-start = (bf16[512,768]{1,0:T(8,128)(2,1)S(1)}, bf16[512,768]{1,0:T(8,128)(2,1)}, u32[]{:S(2)}) copy-start(bf16[512,768]{1,0:T(8,128)(2,1)} %constant.4.clone.matrix) | copy-start | bytes 2359300
  10.1 14.5 %copy-start.1 = (f32[256,128]{1,0:T(8,128)S(1)}, f32[256,128]{1,0:T(8,128)}, u32[]{:S(2)}) copy-start(f32[256,128]{1,0:T(8,128)} %constant.5.clone.twiddle) | copy-start | bytes 393220
  47.9 1.3 %collective-permute-start = (bf16[32,1152]{1,0:T(8,128)(2,1)S(1)}, bf16[32,1152]{1,0:T(8,128)(2,1)S(1)}, u32[]{:S(2)}, u32[]{:S(2)}) collective-permute-start(bf16[32,1152]{1,0:T(8,128)(2,1)S(1)} %get-tuple-element.16.mine), channel_id=1, source_target_pairs={{0,1},{1,0},{2,3},{3,2},{4,5},{5,4},{6,7},{7,6},{8,9},{9,8},{10,11... | collective-permute-start | bytes 221192 | tf_op jit(solution)/shard_map/ppermute | solution.py:598
